TPU v7x, 512 devices: a whole 4x8x8 slice. The times are simulated.
512 devices in a mesh: beam: 128 (over z, y, x_hi), grp: 4 (over x_lo, core).
Axes of the slice: x: 4 (x_hi: 2, x_lo: 2; x = x_hi * 2 + x_lo), y: 8, z: 8, core: 2. Of those that a mesh axis runs over, the one named last changes fastest.
Arguments:
- potential: bfloat16 [2, 262144], P(None, 'beam'), may hold values from -6 to 6
- wave_vectors: int32 [512, 2], replicated, may hold values from -64 to 63
- probe_sites: int32 [64, 2], replicated, may hold values from 0 to 511
Outputs:
- probe_waves: float32 [2, 64, 65536], P(None, 'grp', 'beam')
All inputs are finite; a program needn't handle non-finite values.
Results may differ from a plain program's by a relative error of at most 0.012.
Values may be sent and summed in bfloat16 or wider, within the bound.
No kernel may reach another device: no remote copies, remote signals or barrier semaphores. Data moves between devices by JAX's collectives and lax.ppermute only.
A program may use at most 64 MiB of HBM per device.

v0:
```python
import math

import jax
import jax.numpy as jnp
from jax import lax
from jax.sharding import Mesh
from jax.sharding import PartitionSpec as P

G = 512
BAND = 256
SLICES = 2
BEAM = ("beam_0", "beam_1", "beam_2")


PHASE_SCALE = 2.5
CHIRP_RATE = 20


def copy_for_each(shard, axis):
    size = lax.axis_size(axis)
    return lax.all_to_all(
        jnp.broadcast_to(shard[None], (size, *shard.shape)), axis, 0, 0, tiled=True
    )


def laid_out(tiles, dim):
    tiles = jnp.moveaxis(tiles, 0, dim)
    dims = tiles.shape
    return tiles.reshape(*dims[:dim], dims[dim] * dims[dim + 1], *dims[dim + 2 :])


def gathered_by_axis(shard, axes, dim):
    far, near = axes
    tiles = copy_for_each(copy_for_each(shard, far), near)
    return laid_out(tiles.swapaxes(0, 1).reshape(-1, *shard.shape), dim)


def of_everyone(shard, axis):
    return copy_for_each(shard, axis).sum(axis=0)


def dft_table(freqs, places, length, sign):
    phases = jnp.mod(freqs[:, None] * places[None, :], length)
    angle = 2.0 * math.pi / length * phases.astype(jnp.float32)
    factor = 1.0 / math.sqrt(length)
    return (
        (jnp.cos(angle) * factor).astype(jnp.bfloat16),
        (sign * jnp.sin(angle) * factor).astype(jnp.bfloat16),
    )


def propagator(freqs):
    squared = freqs[:, None] * freqs[:, None] + freqs[None, :] * freqs[None, :]
    inside = (9 * squared < G * G).astype(jnp.float32)
    chirp = jnp.mod(CHIRP_RATE * squared, G * G)
    angle = -2.0 * math.pi / (G * G) * chirp.astype(jnp.float32)
    return (inside * jnp.cos(angle), inside * jnp.sin(angle))


def rounded(pair):
    return (pair[0].astype(jnp.bfloat16), pair[1].astype(jnp.bfloat16))


def times(pair, other):
    return (pair[0] * other[0] - pair[1] * other[1], pair[0] * other[1] + pair[1] * other[0])


def combine_blocks(blocks, height, width):
    return (
        blocks[:height, :width] - blocks[height:, width:],
        blocks[:height, width:] + blocks[height:, :width],
    )


def left_product(table, data):
    blocks = jnp.dot(
        jnp.concatenate(table, 0), jnp.concatenate(data, 1), preferred_element_type=jnp.float32
    )
    return combine_blocks(blocks, table[0].shape[0], data[0].shape[1])


def right_product(data, table):
    blocks = jnp.dot(
        jnp.concatenate(data, 0), jnp.concatenate(table, 1), preferred_element_type=jnp.float32
    )
    return combine_blocks(blocks, data[0].shape[0], table[0].shape[1])


def transform(data, first, second):
    return right_product(rounded(left_product(first, data)), second)


def exit_wave(wave_x, wave_y, slabs):
    places = jnp.arange(G, dtype=jnp.int32)
    full_freqs = jnp.where(places < G // 2, places, places - G)
    band_freqs = jnp.arange(BAND, dtype=jnp.int32) - BAND // 2
    forward = dft_table(places, places, G, -1.0)
    inverse = dft_table(places, places, G, 1.0)
    crop_rows = dft_table(band_freqs, places, G, -1.0)
    crop_cols = (crop_rows[0].T, crop_rows[1].T)
    full_prop = propagator(full_freqs)
    band_prop = propagator(band_freqs)
    phases = jnp.mod(wave_x * places[:, None] + wave_y * places[None, :], G)
    angle = 2.0 * math.pi / G * phases.astype(jnp.float32)
    wave = (jnp.cos(angle), jnp.sin(angle))
    result = None
    for layer in range(SLICES):
        shift = PHASE_SCALE * slabs[layer].astype(jnp.float32)
        passed = rounded(times(wave, (jnp.cos(shift), jnp.sin(shift))))
        if layer + 1 < SLICES:
            spectrum = rounded(times(transform(passed, forward, forward), full_prop))
            wave = transform(spectrum, inverse, inverse)
        else:
            result = rounded(times(transform(passed, crop_rows, crop_cols), band_prop))
    return result


def coefficients(vectors, sites, count):
    wave_x = vectors[:, 0]
    wave_y = vectors[:, 1]
    phases = jnp.mod(sites[:, 0:1] * wave_x[None, :] + sites[:, 1:2] * wave_y[None, :], G)
    angle = -2.0 * math.pi / G * phases.astype(jnp.float32)
    weight = jnp.exp(
        -(wave_x * wave_x + wave_y * wave_y).astype(jnp.float32) * (8.0 / (BAND * BAND))
    )
    weight = weight[None, :] * (1.0 / math.sqrt(count))
    return (
        (weight * jnp.cos(angle)).astype(jnp.bfloat16),
        (weight * jnp.sin(angle)).astype(jnp.bfloat16),
    )


def local(potential, wave_vectors, probe_sites):
    groups = lax.axis_size("grp")
    beams_here = lax.axis_size(BEAM)
    group_index = lax.axis_index("grp")
    beam_index = lax.axis_index(BEAM)
    whole = gathered_by_axis(potential, (("beam_0", "beam_1"), "beam_2"), 1)
    slabs = whole.reshape(SLICES, G, G)
    own_beam = beam_index * groups + group_index
    vector = lax.dynamic_slice_in_dim(wave_vectors, own_beam, 1, 0)
    exit_real, exit_imag = exit_wave(vector[0, 0], vector[0, 1], slabs)
    outgoing = jnp.stack([exit_real, exit_imag], 0).reshape(1, 2, beams_here, -1)
    members = lax.dynamic_slice_in_dim(
        wave_vectors.reshape(beams_here, groups, 2), group_index, 1, 1
    )[:, 0, :]
    coef_real, coef_imag = coefficients(members, probe_sites, beams_here * groups)
    stacked = jnp.concatenate([coef_real, coef_imag], 0)
    probes = coef_real.shape[0]
    received = lax.all_to_all(outgoing, BEAM, split_axis=2, concat_axis=0, tiled=True)
    s_real = received[:, 0, 0, :]
    s_imag = received[:, 1, 0, :]
    blocks = jnp.dot(
        stacked, jnp.concatenate([s_real, s_imag], 1), preferred_element_type=jnp.float32
    )
    real, imag = combine_blocks(blocks, probes, s_real.shape[1])
    partial_sum = jnp.stack([real, imag], 0)
    total = of_everyone(partial_sum, "grp")
    rows = probes // groups
    return lax.dynamic_slice_in_dim(total, group_index * rows, rows, 1)


def solution(mesh):
    finer = Mesh(
        mesh.devices.reshape(8, 8, 2, mesh.shape["grp"]), ("beam_0", "beam_1", "beam_2", "grp")
    )
    in_specs = (P(None, BEAM), P(), P())
    out_specs = P(None, "grp", BEAM)
    return jax.shard_map(local, mesh=finer, in_specs=in_specs, out_specs=out_specs, check_vma=False)
```

profile of v0, /device:TPU:1, one launch (start us, length us, event | category | flops | bytes accessed | tf_op | source)
XLA Modules:
  0.0 205.7 jit_solution(242035378116865096)
XLA Ops:
  0.0 1.8 broadcast_in_dim.6
  1.8 17.1 %all-to-all-start = ((bf16[64,2,2048]{2,1,0:T(2,128)(2,1)}), bf16[64,2,2048]{2,1,0:T(2,128)(2,1)S(1)}, u32[]{:S(2)}, u32[]{:S(2)}) async-start(bf16[64,2,2048]{2,1,0:T(2,128)(2,1)} %broadcast_in_dim.6), calls=%async_computation | async-start | bytes 1048576 | tf_op jit(solution)/shard_map/all_to_all | solution.py:21
  18.9 0.8 reshape.91
  21.2 1.2 iota_multiply_fusion
  22.4 4.6 %multiply_convert_fusion.1 = bf16[512,512]{0,1:T(8,128)(2,1)} fusion(), kind=kLoop, calls=%fused_computation.81 | loop fusion | flops 4194304 | bytes 524288 | tf_op jit(solution)/shard_map/convert_element_type | solution.py:48
  27.1 5.4 %multiply_convert_fusion = (bf16[512,512]{0,1:T(8,128)(2,1)}, bf16[512,512]{0,1:T(8,128)(2,1)}) fusion(), kind=kLoop, calls=%fused_computation.80 | loop fusion | flops 4718592 | bytes 1048576 | tf_op jit(solution)/shard_map/convert_element_type | solution.py:48
  32.4 3.9 %all-to-all-done = bf16[64,2,2048]{2,1,0:T(2,128)(2,1)S(1)} async-done(((bf16[64,2,2048]{2,1,0:T(2,128)(2,1)}), bf16[64,2,2048]{2,1,0:T(2,128)(2,1)S(1)}, u32[]{:S(2)}, u32[]{:S(2)}) %all-to-all-start) | async-done | bytes 524320 | tf_op jit(solution)/shard_map/all_to_all | solution.py:21
  36.3 1.5 broadcast_in_dim.7
  37.8 4.0 %all-to-all-start.1 = ((bf16[2,64,2,2048]{3,2,1,0:T(2,128)(2,1)}), bf16[2,64,2,2048]{3,2,1,0:T(2,128)(2,1)S(1)}, u32[]{:S(2)}, u32[]{:S(2)}) async-start(bf16[2,64,2,2048]{3,2,1,0:T(2,128)(2,1)} %broadcast_in_dim.7), calls=%async_computation.1 | async-start | bytes 2097152 | tf_op jit(solution)/shard_map/all_to_all | solution.py:21
  41.8 3.2 %multiply_convert_fusion.6 = (bf16[256,512]{1,0:T(8,128)(2,1)}, bf16[256,512]{1,0:T(8,128)(2,1)}) fusion(s32[256]{0:T(256)S(1)} %iota_add_fusion), kind=kLoop, calls=%fused_computation.120 | loop fusion | flops 2359296 | bytes 525312 | tf_op jit(solution)/shard_map/convert_element_type | solution.py:47
  45.0 2.9 %multiply_convert_fusion.4 = (bf16[512,256]{1,0:T(8,128)(2,1)S(1)}, bf16[512,256]{1,0:T(8,128)(2,1)}) fusion(s32[256]{0:T(256)S(1)} %iota_add_fusion), kind=kLoop, calls=%fused_computation.113 | loop fusion | flops 2359296 | bytes 525312 | tf_op jit(solution)/shard_map/convert_element_type | solution.py:47
  47.9 5.6 %all-to-all-done.1 = bf16[2,64,2,2048]{3,2,1,0:T(2,128)(2,1)S(1)} async-done(((bf16[2,64,2,2048]{3,2,1,0:T(2,128)(2,1)}), bf16[2,64,2,2048]{3,2,1,0:T(2,128)(2,1)S(1)}, u32[]{:S(2)}, u32[]{:S(2)}) %all-to-all-start.1) | async-done | bytes 1048608 | tf_op jit(solution)/shard_map/all_to_all | solution.py:21
  53.5 1.2 copy.38
  54.7 72.8 %sine_reduce_fusion.1 = (f32[128,2048]{1,0:T(8,128)}, f32[128,2048]{1,0:T(8,128)}, f32[128,2048]{1,0:T(8,128)}, f32[128,2048]{1,0:T(8,128)S(1)}) fusion(bf16[2,128,2048]{2,0,1:T(2,128)(2,1)S(1)} %bitcast.35), kind=kLoop, calls=%fused_computation.78 | loop fusion | flops 1048576 | bytes 5242880 | tf_op jit(solution)/shard_map/sin | solution.py:109
  128.2 1.5 sin.49
  130.1 5.1 %subtract_convert_fusion.2 = (bf16[512,512]{0,1:T(8,128)(2,1)S(1)}, bf16[512,512]{0,1:T(8,128)(2,1)S(1)}) fusion(f32[512,512]{0,1:T(8,128)S(1)} %copy.40, f32[512,512]{0,1:T(8,128)S(1)} %copy.39, s32[512]{0:T(512)S(1)} %get-tuple-element.39, s32[512]{0:T(512)S(1)} %get-tuple-element.40), kind=kLoop, calls=%fused_computation.77 | loop fusion | flops 5767168 | bytes 3149824 | tf_op jit(solution)/shard_map/convert_element_type | solution.py:61
  135.2 1.3 fusion.4
  136.9 1.3 fusion.1
  138.2 5.5 %subtract_convert_fusion.1 = (bf16[512,512]{0,1:T(8,128)(2,1)S(1)}, bf16[512,512]{0,1:T(8,128)(2,1)S(1)}) fusion(s32[512]{0:T(512)S(1)} %fusion.88, f32[1024,1024]{0,1:T(8,128)S(1)} %fusion.1), kind=kLoop, calls=%fused_computation.73 | loop fusion | flops 7602176 | bytes 5246976 | tf_op jit(solution)/shard_map/convert_element_type | solution.py:61
  143.7 1.3 fusion.3
  145.1 1.3 fusion.17
  147.0 1.5 sin.52
  148.9 2.8 %fusion.2 = f32[1024,1024]{0,1:T(8,128)S(1)} fusion(bf16[512,512]{0,1:T(8,128)(2,1)} %get-tuple-element.42, bf16[512,512]{1,0:T(8,128)(2,1)} %get-tuple-element.14, bf16[512,512]{1,0:T(8,128)(2,1)} %get-tuple-element.13, bf16[512,512]{0,1:T(8,128)(2,1)} %multiply_convert_fusion.1), kind=kOutput, calls=%fused_computation.19 | convolution fusion | flops 1077936128 | bytes 6291456 | tf_op jit(solution)/shard_map/dot_general | solution.py:83
  151.7 0.9 subtract_convert_fusion
  153.7 0.8 copy-done.4
  154.9 1.4 subtract_convert_fusion.3
  156.4 1.3 pad_maximum_fusion.8
  157.7 11.5 %all-to-all-start.2 = ((bf16[1,2,128,512]{3,1,0,2:T(2,128)(2,1)}), bf16[1,2,128,512]{3,1,0,2:T(2,128)(2,1)S(1)}, u32[]{:S(2)}, u32[]{:S(2)}) async-start(bf16[1,2,128,512]{3,1,0,2:T(2,128)(2,1)} %pad_maximum_fusion.8), calls=%async_computation.2 | async-start | bytes 524288 | tf_op jit(solution)/shard_map/all_to_all | solution.py:150
  169.5 13.3 %all-to-all-done.2 = bf16[1,2,128,512]{3,1,0,2:T(2,128)(2,1)S(1)} async-done(((bf16[1,2,128,512]{3,1,0,2:T(2,128)(2,1)}), bf16[1,2,128,512]{3,1,0,2:T(2,128)(2,1)S(1)}, u32[]{:S(2)}, u32[]{:S(2)}) %all-to-all-start.2) | async-done | bytes 262176 | tf_op jit(solution)/shard_map/all_to_all | solution.py:150
  183.1 1.1 broadcast_in_dim.8
  184.2 7.4 %all-to-all-start.3 = ((f32[4,2,64,512]{3,2,1,0:T(8,128)}), f32[4,2,64,512]{3,2,1,0:T(8,128)S(1)}, u32[]{:S(2)}, u32[]{:S(2)}) async-start(f32[4,2,64,512]{3,2,1,0:T(8,128)} %broadcast_in_dim.8), calls=%async_computation.3 | async-start | bytes 2097152 | tf_op jit(solution)/shard_map/all_to_all | solution.py:21
  191.5 13.5 %all-to-all-done.3 = f32[4,2,64,512]{3,2,1,0:T(8,128)S(1)} async-done(((f32[4,2,64,512]{3,2,1,0:T(8,128)}), f32[4,2,64,512]{3,2,1,0:T(8,128)S(1)}, u32[]{:S(2)}, u32[]{:S(2)}) %all-to-all-start.3) | async-done | bytes 1048608 | tf_op jit(solution)/shard_map/all_to_all | solution.py:21
  (44 shorter events, 6.6 us)
Async XLA Ops:
  1.8 34.6 %all-to-all-start = ((bf16[64,2,2048]{2,1,0:T(2,128)(2,1)}), bf16[64,2,2048]{2,1,0:T(2,128)(2,1)S(1)}, u32[]{:S(2)}, u32[]{:S(2)}) async-start(bf16[64,2,2048]{2,1,0:T(2,128)(2,1)} %broadcast_in_dim.6), calls=%async_computation | async-start | bytes 1048576 | tf_op jit(solution)/shard_map/all_to_all | solution.py:21
  37.8 15.7 %all-to-all-start.1 = ((bf16[2,64,2,2048]{3,2,1,0:T(2,128)(2,1)}), bf16[2,64,2,2048]{3,2,1,0:T(2,128)(2,1)S(1)}, u32[]{:S(2)}, u32[]{:S(2)}) async-start(bf16[2,64,2,2048]{3,2,1,0:T(2,128)(2,1)} %broadcast_in_dim.7), calls=%async_computation.1 | async-start | bytes 2097152 | tf_op jit(solution)/shard_map/all_to_all | solution.py:21
  130.1 5.1 %copy-start.2 = (bf16[512,512]{0,1:T(8,128)(2,1)S(1)}, bf16[512,512]{0,1:T(8,128)(2,1)}, u32[]{:S(2)}) copy-start(bf16[512,512]{0,1:T(8,128)(2,1)} %get-tuple-element.42) | copy-start | bytes 1572868
  130.1 5.1 %copy-start.3 = (bf16[512,512]{0,1:T(8,128)(2,1)S(1)}, bf16[512,512]{0,1:T(8,128)(2,1)}, u32[]{:S(2)}) copy-start(bf16[512,512]{0,1:T(8,128)(2,1)} %get-tuple-element.41) | copy-start | bytes 1572868
  138.2 5.6 %copy-start.1 = (bf16[512,512]{0,1:T(8,128)(2,1)S(1)}, bf16[512,512]{0,1:T(8,128)(2,1)}, u32[]{:S(2)}) copy-start(bf16[512,512]{0,1:T(8,128)(2,1)} %multiply_convert_fusion.1) | copy-start | bytes 1572868
  145.0 1.3 copy-start
  151.7 1.0 copy-start.5
  151.7 1.0 copy-start.6
  153.5 1.0 copy-start.4
  154.9 14.3 %copy-start.7 = (s32[64,2]{0,1:T(2,128)S(1)}, s32[64,2]{0,1:T(2,128)}, u32[]{:S(2)}) copy-start(s32[64,2]{0,1:T(2,128)} %param.5) | copy-start | bytes 1540
  157.7 25.0 %all-to-all-start.2 = ((bf16[1,2,128,512]{3,1,0,2:T(2,128)(2,1)}), bf16[1,2,128,512]{3,1,0,2:T(2,128)(2,1)S(1)}, u32[]{:S(2)}, u32[]{:S(2)}) async-start(bf16[1,2,128,512]{3,1,0,2:T(2,128)(2,1)} %pad_maximum_fusion.8), calls=%async_computation.2 | async-start | bytes 524288 | tf_op jit(solution)/shard_map/all_to_all | solution.py:150
  184.2 20.8 %all-to-all-start.3 = ((f32[4,2,64,512]{3,2,1,0:T(8,128)}), f32[4,2,64,512]{3,2,1,0:T(8,128)S(1)}, u32[]{:S(2)}, u32[]{:S(2)}) async-start(f32[4,2,64,512]{3,2,1,0:T(8,128)} %broadcast_in_dim.8), calls=%async_computation.3 | async-start | bytes 2097152 | tf_op jit(solution)/shard_map/all_to_all | solution.py:21
where the time goes:
time: 206 us
  other arithmetic  107 us (52%)
  starting transfers between devices  40 us (19%)
  waiting for transfers between devices  36.2 us (18%)
  local copies, waits for them, and re-layouts  14.6 us (7%)
  matrix products  8.07 us (4%)
    sin x1, other arithmetic, exit_wave(): passed = rounded(times(wave, (jnp.cos(shift), jnp.sin(shift))))  72.8 us
    all_to_all x3, starting transfers between devices, copy_for_each(): lax.all_to_all(jnp.broadcast_to(shard[None], (size, *shard.shape)), axis,...  28.5 us
    all_to_all x3, waiting for transfers between devices, copy_for_each(): lax.all_to_all(jnp.broadcast_to(shard[None], (size, *shard.shape)), axis,...  22.9 us
    convert_element_type x7, other arithmetic, rounded(): return (pair[0].astype(jnp.bfloat16), pair[1].astype(jnp.bfloat16))  14.7 us
    all_to_all x1, waiting for transfers between devices, local(): lax.all_to_all(outgoing, BEAM, split_axis=2, concat_axis=0, tiled=True)  13.3 us
    all_to_all x1, starting transfers between devices, local(): lax.all_to_all(outgoing, BEAM, split_axis=2, concat_axis=0, tiled=True)  11.5 us
    convert_element_type x2, other arithmetic, dft_table(): (sign * jnp.sin(angle) * factor).astype(jnp.bfloat16)  10 us
    convert_element_type x2, other arithmetic, dft_table(): (jnp.cos(angle) * factor).astype(jnp.bfloat16)  6.09 us
  transfers between devices with their start and end apart: 4, of which 4 were waited for; matrix products, arithmetic and copies ran while one was open for 10% of the time, Pallas kernels for 0%

commit v1 on v0

v1 whole, which is shorter than its diff:
```python
import math

import jax
import jax.numpy as jnp
import numpy as np
from jax import lax
from jax.experimental import pallas as pl
from jax.experimental.pallas import tpu as pltpu
from jax.sharding import PartitionSpec as P

G = 512
BAND = 256
NQ = 384
PHASE_SCALE = 2.5
CHIRP_RATE = 20
BLOCK = 64
ROWS = 18

F32 = jnp.float32
BF16 = jnp.bfloat16


def frequencies():
    reach = math.isqrt((G * G - 1) // 9)
    band = np.arange(-BAND // 2, BAND // 2)
    high = np.arange(BAND // 2, reach + 1)
    low = np.arange(-reach, -BAND // 2)
    return np.concatenate([band, high, low])


def forward_table(places):
    freqs = frequencies()
    phases = np.mod(freqs[None, :] * places[:, None], G)
    angle = 2.0 * np.pi / G * phases
    table = np.zeros((2, places.shape[0], NQ), np.float64)
    table[0, :, : freqs.size] = np.cos(angle) / np.sqrt(G)
    table[1, :, : freqs.size] = -np.sin(angle) / np.sqrt(G)
    return table


def constant_tables():
    places = np.arange(G)
    permuted = (4 * np.arange(G // 4)[None, :] + np.arange(4)[:, None]).reshape(-1)
    natural = forward_table(places)
    shuffled = forward_table(permuted)
    right = np.concatenate([natural[0], natural[1]], 1)
    left = np.concatenate([shuffled[0].T, shuffled[1].T], 0)
    back = np.concatenate([shuffled[0], -shuffled[1]], 1)
    freqs = frequencies()
    squared = np.full((NQ,), 1.0e9)
    squared[: freqs.size] = freqs * freqs
    angle = np.zeros((NQ,))
    angle[: freqs.size] = -2.0 * np.pi / (G * G) * np.mod(CHIRP_RATE * freqs * freqs, G * G)
    chirp = np.stack([np.cos(angle), np.sin(angle), squared], 0)
    lanes = np.zeros((8, NQ))
    lanes[:3] = chirp
    return (
        right.astype(BF16),
        left.astype(BF16),
        back.astype(BF16),
        lanes.astype(np.float32),
    )


def half_turn_fits():
    nodes = 0.5 * np.cos(np.pi * (np.arange(400) + 0.5) / 400)
    square = nodes * nodes
    sine = np.polynomial.Polynomial.fit(square, np.sin(np.pi * nodes) / nodes, 4, domain=[0, 0.25])
    cosine = np.polynomial.Polynomial.fit(square, np.cos(np.pi * nodes), 4, domain=[0, 0.25])
    return (
        [float(v) for v in sine.convert().coef],
        [float(v) for v in cosine.convert().coef],
    )


SINE, COSINE = half_turn_fits()


def horner(coefs, x):
    total = coefs[-1]
    for coef in coefs[-2::-1]:
        total = total * x + coef
    return total


def phase_factor(cells):
    turns = cells * (PHASE_SCALE / (2.0 * math.pi))
    rest = turns - jnp.floor(turns + 0.5)
    square = rest * rest
    sine = rest * horner(SINE, square)
    cosine = horner(COSINE, square)
    return 1.0 - 2.0 * sine * sine, 2.0 * sine * cosine


def dot(a, b):
    return jnp.dot(a, b, preferred_element_type=F32)


def dot_t(a, b):
    return lax.dot_general(a, b, (((1,), (1,)), ((), ())), preferred_element_type=F32)


def prepare_kernel(place, beams, right, back, chirp, chirp_t, phi, inverse, prop, final):
    index = lax.broadcasted_iota(jnp.int32, (BAND, G), 0).astype(F32)
    on_x = index == beams[0:1, :]
    on_y = jnp.where(index == beams[1:2, :], 1.0, 0.0).astype(BF16)
    grid_r = dot_t(jnp.where(on_x, beams[2:3, :], 0.0).astype(BF16), on_y)
    grid_i = dot_t(jnp.where(on_x, beams[3:4, :], 0.0).astype(BF16), on_y)
    grid = jnp.concatenate([grid_r, grid_i], 1).astype(BF16)
    by_r = dot(back[:, 0:BAND], grid)
    by_i = dot(back[:, NQ : NQ + BAND], grid)
    mid_r = by_r[:, :BAND] - by_i[:, BAND:]
    mid_i = by_r[:, BAND:] + by_i[:, :BAND]
    band_r = right[:, 0:BAND]
    band_i = right[:, NQ : NQ + BAND]
    both = jnp.concatenate([band_r, band_i], 1)
    phi[:, :G] = dot_t(jnp.concatenate([mid_r, mid_i], 1).astype(BF16), both)
    phi[:, G:] = dot_t(jnp.concatenate([mid_i, -mid_r], 1).astype(BF16), both)
    start = pl.multiple_of(place[0] * BLOCK, BLOCK)
    own_r = right[pl.ds(start, BLOCK), 0:NQ]
    own_i = right[pl.ds(start, BLOCK), NQ:]
    inverse[0:64, :NQ] = own_r
    inverse[0:64, NQ:] = own_i
    inverse[64:128, :NQ] = -own_i
    inverse[64:128, NQ:] = own_r
    inverse[128:192, :NQ] = own_i
    inverse[128:192, NQ:] = -own_r
    inverse[192:256, :NQ] = own_r
    inverse[192:256, NQ:] = own_i
    inside = chirp_t[:, 2:3] + chirp[2:3, :] < (G * G - 1) // 9 + 0.5
    xr = chirp_t[:, 0:1]
    xi = chirp_t[:, 1:2]
    yr = chirp[0:1, :]
    yi = chirp[1:2, :]
    prop[:, :NQ] = jnp.where(inside, xr * yr - xi * yi, 0.0)
    prop[:, NQ:] = jnp.where(inside, xr * yi + xi * yr, 0.0)
    for k in range(G // BLOCK):
        rows = slice(k * BLOCK, (k + 1) * BLOCK)
        top = slice(2 * k * BLOCK, (2 * k + 1) * BLOCK)
        low = slice((2 * k + 1) * BLOCK, (2 * k + 2) * BLOCK)
        final[top, :BAND] = right[rows, 0:BAND]
        final[top, BAND:] = right[rows, NQ : NQ + BAND]
        final[low, :BAND] = -right[rows, NQ : NQ + BAND]
        final[low, BAND:] = right[rows, 0:BAND]


def main_kernel(cells, phi, right, left, back, inverse, prop, out, wide, data, half, spec, fold):
    wide[...] = cells[...].astype(F32)
    for j in range(4):
        rows = slice(128 * j, 128 * j + 128)
        for h in range(4):
            cols = slice(128 * h, 128 * h + 128)
            cos, sin = phase_factor(wide[pl.ds(4 * j + h, 128, stride=ROWS), :])
            pr = phi[rows, 128 * h : 128 * h + 128]
            pi = phi[rows, G + 128 * h : G + 128 * h + 128]
            data[rows, cols] = (pr * cos - pi * sin).astype(BF16)
            data[rows, G + 128 * h : G + 128 * h + 128] = (pr * sin + pi * cos).astype(BF16)
        one = dot(data[rows, :G], right[...])
        two = dot(data[rows, G:], right[...])
        half[rows, :NQ] = (one[:, :NQ] - two[:, NQ:]).astype(BF16)
        half[rows, NQ:] = (one[:, NQ:] + two[:, :NQ]).astype(BF16)
    for j in range(3):
        rows = slice(128 * j, 128 * j + 128)
        one = dot(left[rows, :], half[...])
        two = dot(left[NQ + 128 * j : NQ + 128 * j + 128, :], half[...])
        re = one[:, :NQ] - two[:, NQ:]
        im = one[:, NQ:] + two[:, :NQ]
        pr = prop[rows, :NQ]
        pi = prop[rows, NQ:]
        spec[rows, :NQ] = (re * pr - im * pi).astype(BF16)
        spec[rows, NQ:] = (re * pi + im * pr).astype(BF16)
        turned = dot_t(spec[rows, :], inverse[...])
        low = slice(NQ + 128 * j, NQ + 128 * j + 128)
        fold[rows, :] = turned.astype(BF16)
        fold[low, :128] = turned[:, 128:].astype(BF16)
        fold[low, 128:] = (-turned[:, :128]).astype(BF16)
    lane = lax.broadcasted_iota(jnp.int32, (128, 128), 1) < BLOCK
    for j in range(4):
        rows = slice(128 * j, 128 * j + 128)
        pair = wide[pl.ds(16 + j // 2, 128, stride=ROWS), :]
        other = pltpu.roll(pair, BLOCK, 1)
        own = jnp.where(lane, pair, other) if j % 2 == 0 else jnp.where(lane, other, pair)
        cos, sin = phase_factor(own)
        wave = dot(back[rows, :], fold[...])
        data[rows, :128] = (wave[:, :128] * cos + wave[:, 128:] * sin).astype(BF16)
        data[rows, 128:256] = (wave[:, 128:] * cos - wave[:, :128] * sin).astype(BF16)
    total = dot(left[0:BAND, :], data[:, :128]) + dot(left[NQ : NQ + BAND, :], data[:, 128:256])
    out[...] = total.astype(BF16)


def final_kernel(parts, final, prop, out, total):
    acc = dot(parts[0:32, :], final[0:128, :])
    for k in range(1, 8):
        acc = acc + dot(parts[32 * k : 32 * k + 32, :], final[128 * k : 128 * k + 128, :])
    for k in range(4):
        total[32 * k : 32 * k + 32, :] = acc[:, 128 * k : 128 * k + 128]
    for row in range(2):
        for k in range(2):
            re = total[pl.ds(32 * k + row, 16, stride=2), :]
            im = total[pl.ds(64 + 32 * k + row, 16, stride=2), :]
            pr = prop[row : row + 1, 128 * k : 128 * k + 128]
            pi = prop[row : row + 1, BAND + 128 * k : BAND + 128 * k + 128]
            cols = slice(row * BAND + 128 * k, row * BAND + 128 * k + 128)
            out[0, :, cols] = re * pr - im * pi
            out[1, :, cols] = re * pi + im * pr


VMEM = pl.BlockSpec(memory_space=pltpu.VMEM)
LIMIT = pltpu.CompilerParams(vmem_limit_bytes=12 * 1024 * 1024)
SMEM = pl.BlockSpec(memory_space=pltpu.SMEM)


def prepare(place, beams, right, back, chirp):
    return pl.pallas_call(
        prepare_kernel,
        in_specs=[SMEM] + [VMEM] * 5,
        out_specs=[VMEM] * 4,
        out_shape=[
            jax.ShapeDtypeStruct((G, 2 * G), F32),
            jax.ShapeDtypeStruct((4 * BLOCK, 2 * NQ), BF16),
            jax.ShapeDtypeStruct((NQ, 2 * NQ), F32),
            jax.ShapeDtypeStruct((2 * G, 2 * BAND), BF16),
        ],
        compiler_params=LIMIT,
        name="prepare",
    )(place, beams, right, back, chirp, chirp.T)


def main(cells, phi, right, left, back, inverse, prop):
    return pl.pallas_call(
        main_kernel,
        in_specs=[VMEM] * 7,
        out_specs=VMEM,
        out_shape=jax.ShapeDtypeStruct((BAND, 2 * BLOCK), BF16),
        scratch_shapes=[
            pltpu.VMEM((cells.shape[0], 128), F32),
            pltpu.VMEM((G, 2 * G), BF16),
            pltpu.VMEM((G, 2 * NQ), BF16),
            pltpu.VMEM((NQ, 2 * NQ), BF16),
            pltpu.VMEM((2 * NQ, 4 * BLOCK), BF16),
        ],
        compiler_params=LIMIT,
        name="propagate",
    )(cells, phi, right, left, back, inverse, prop)


def finish(parts, final, prop):
    return pl.pallas_call(
        final_kernel,
        in_specs=[VMEM] * 3,
        out_specs=VMEM,
        out_shape=jax.ShapeDtypeStruct((2, 16, 2 * BAND), F32),
        scratch_shapes=[pltpu.VMEM((128, 128), F32)],
        compiler_params=LIMIT,
        name="finish",
    )(parts, final, prop)


def own_coefficients(vectors, site):
    wave_x = vectors[:, 0]
    wave_y = vectors[:, 1]
    phases = jnp.mod(site[0] * wave_x + site[1] * wave_y, G)
    angle = -2.0 * math.pi / G * phases.astype(F32)
    weight = jnp.exp(-(wave_x * wave_x + wave_y * wave_y).astype(F32) * (8.0 / (BAND * BAND)))
    weight = weight * (1.0 / math.sqrt(vectors.shape[0]))
    coef_r = (weight * jnp.cos(angle)).astype(BF16).astype(F32) * G
    coef_i = (weight * jnp.sin(angle)).astype(BF16).astype(F32) * G
    offset = BAND // 2
    rows = [(wave_x + offset).astype(F32), (wave_y + offset).astype(F32), coef_r, coef_i]
    return jnp.concatenate([jnp.stack(rows, 0), jnp.zeros((4, vectors.shape[0]), F32)], 0)


def band_rows(first):
    fx = first + jnp.arange(2, dtype=jnp.int32) - BAND // 2
    fy = jnp.arange(BAND, dtype=jnp.int32) - BAND // 2
    squared = fx[:, None] * fx[:, None] + fy[None, :] * fy[None, :]
    inside = (9 * squared < G * G).astype(F32)
    angle = -2.0 * math.pi / (G * G) * jnp.mod(CHIRP_RATE * squared, G * G).astype(F32)
    return jnp.concatenate([inside * jnp.cos(angle), inside * jnp.sin(angle)], 1)


def message(potential, peers):
    near = potential[0].reshape(1, 8, 2, 128)
    far = potential[1].reshape(4, 8, BLOCK).swapaxes(0, 1).reshape(8, 1, 2, 128)
    far = jnp.broadcast_to(far, (8, peers // 8, 2, 128)).reshape(peers, 1, 2, 128)
    return jnp.concatenate([jnp.broadcast_to(near, (peers, 8, 2, 128)), far], 1)


def local(potential, wave_vectors, probe_sites):
    right, left, back, chirp = (jnp.asarray(t) for t in constant_tables())
    peers = lax.axis_size("beam")
    position = lax.axis_index("beam")
    probes = peers // 8
    cells = lax.all_to_all(message(potential, peers), "beam", 0, 0, tiled=True)
    site = lax.dynamic_index_in_dim(
        probe_sites, lax.axis_index("grp") * probes + position % probes, 0, keepdims=False
    )
    beams = own_coefficients(wave_vectors, site)
    place = (position // probes).reshape(1)
    phi, inverse, prop, final = prepare(place, beams, right, back, chirp)
    sent = main(cells.reshape(peers * ROWS, 128), phi, right, left, back, inverse, prop)
    parts = lax.all_to_all(sent.reshape(peers, 2, 128), "beam", 0, 0, tiled=True)
    return finish(parts.reshape(2 * peers, 128), final, band_rows(2 * position))


def solution(mesh):
    in_specs = (P(None, "beam"), P(), P())
    out_specs = P(None, "grp", "beam")
    return jax.shard_map(local, mesh=mesh, in_specs=in_specs, out_specs=out_specs, check_vma=False)
```

time: 206 us -> 76.4 us (0.37)
  other arithmetic: 107 us -> 3.25 us
  waiting for transfers between devices: 36.2 us -> 23.5 us
  starting transfers between devices: 40 us -> 30.3 us
  matrix products: 8.07 us -> 0 us
  Pallas kernels: 0 us -> 7.32 us
  local copies, waits for them, and re-layouts: 14.6 us -> 11.4 us
    sin x1 -> x0, other arithmetic: 72.8 us -> none  [exit_wave(): passed = rounded(times(wave, (jnp.cos(shift), jnp.sin(shift))))]
    convert_element_type x12 -> x1, other arithmetic: 31 us -> 0.01 us  [own_coefficients(): (wave_y + offset).astype(F32)]
    all_to_all x4 -> x2, waiting for transfers between devices: 36.2 us -> 23.5 us  [the longest x1 12.1 us: local(): lax.all_to_all(sent.reshape(peers, 2, 128), 'beam', 0, 0, tiled=True)]
    all_to_all x4 -> x2, starting transfers between devices: 40 us -> 30.3 us  [the longest x1 20.8 us: local(): cells = lax.all_to_all(message(potential, peers), 'beam', 0, 0, tiled=True)]
    dot_general x7 -> x0, matrix products: 8.07 us -> none  [the longest x3 4.52 us: right_product(): jnp.dot(jnp.concatenate(data, 0), jnp.concatenate(table, 1), preferred_el...]
    unnamed x16 -> x28, local copies, waits for them, and re-layouts: 0.95 us -> 8.73 us
    pallas_call x0 -> x3, Pallas kernels: none -> 7.32 us  [the longest x1 4.98 us: main(): pl.pallas_call(main_kernel, in_specs=[VMEM] * 7, out_specs=VMEM, out_shap...]
    broadcast_in_dim x3 -> x4, local copies, waits for them, and re-layouts: 4.39 us -> 0.41 us  [the longest x1 0.27 us: message(): return jnp.concatenate([jnp.broadcast_to(near, (peers, 8, 2, 128)), far], 1)]
  transfers between devices with their start and end apart: 4 -> 2, of which waited for: 4 -> 2; matrix products, arithmetic and copies ran while one was open for 10% -> 4% of each run, Pallas kernels for 0% -> 2%
where the time goes in v1:
time: 76.4 us; the launch traced here: 76 us
  starting transfers between devices  30.3 us (40%)
  waiting for transfers between devices  23.5 us (31%)
  local copies, waits for them, and re-layouts  11.4 us (15%)
  Pallas kernels  7.32 us (10%)
  other arithmetic  3.25 us (4%)
    all_to_all x1, starting transfers between devices, local(): cells = lax.all_to_all(message(potential, peers), 'beam', 0, 0, tiled=True)  20.8 us
    all_to_all x1, waiting for transfers between devices, local(): lax.all_to_all(sent.reshape(peers, 2, 128), 'beam', 0, 0, tiled=True)  12.1 us
    all_to_all x1, waiting for transfers between devices, local(): cells = lax.all_to_all(message(potential, peers), 'beam', 0, 0, tiled=True)  11.4 us
    all_to_all x1, starting transfers between devices, local(): lax.all_to_all(sent.reshape(peers, 2, 128), 'beam', 0, 0, tiled=True)  9.53 us
    unnamed x28, local copies, waits for them, and re-layouts  8.73 us
    pallas_call x1, Pallas kernels, main(): pl.pallas_call(main_kernel, in_specs=[VMEM] * 7, out_specs=VMEM, out_shap...  4.98 us
    concatenate x1, other arithmetic, message(): return jnp.concatenate([jnp.broadcast_to(near, (peers, 8, 2, 128)), far], 1)  1.6 us
  transfers between devices with their start and end apart: 2, of which 2 were waited for; matrix products, arithmetic and copies ran while one was open for 4% of the time, Pallas kernels for 2%

profile of v1, /device:TPU:1, one launch (start us, length us, event | category | flops | bytes accessed | tf_op | source)
XLA Modules:
  0.0 76.0 jit_solution(14223617620521618504)
XLA Ops:
  0.0 0.0 copy-start
  0.0 0.0 copy-start.12
  0.0 0.0 copy-start.10
  0.0 0.9 %slice_reduce_fusion.1 = (bf16[2048]{0:T(1024)(128)(2,1)S(1)}, bf16[2048]{0:T(1024)(128)(2,1)S(1)}) fusion(bf16[2,2048]{1,0:T(2,128)(2,1)} %param.7), kind=kLoop, calls=%fused_computation.5 | loop fusion | bytes 16384 | tf_op jit(solution)/shard_map/slice | solution.py:283
  0.9 0.1 reshape_squeeze.4
  1.0 0.1 broadcast_in_dim.23
  1.2 0.3 broadcast_in_dim.22
  1.5 1.6 %pad_maximum_fusion = bf16[128,9,2,128]{3,2,1,0:T(2,128)(2,1)} fusion(bf16[128,1,2,128]{3,2,1,0:T(2,128)(2,1)S(1)} %bitcast.35, bf16[128,8,2,128]{3,2,1,0:T(2,128)(2,1)S(1)} %broadcast_in_dim.22), kind=kLoop, calls=%fused_computation | loop fusion | flops 294912 | bytes 1179648 | tf_op jit(solution)/shard_map/concatenate | solution.py:286
  3.1 20.8 %all-to-all-start = ((bf16[128,9,2,128]{3,2,1,0:T(2,128)(2,1)}), bf16[128,9,2,128]{3,2,1,0:T(2,128)(2,1)S(1)}, u32[]{:S(2)}, u32[]{:S(2)}) async-start(bf16[128,9,2,128]{3,2,1,0:T(2,128)(2,1)} %pad_maximum_fusion), calls=%async_computation | async-start | bytes 1179648 | tf_op jit(solution)/shard_map/all_to_all | solution.py:294
  23.9 0.0 copy-done
  23.9 0.1 constant_dynamic-slice_fusion
  24.0 0.6 fusion.14
  24.6 1.4 %fusion.12 = (f32[1,512]{1,0:T(1,128)S(1)}, f32[1,512]{1,0:T(1,128)S(1)}, f32[512,1]{0,1:T(1,128)S(1)}) fusion(s32[512,2]{0,1:T(2,128)S(1)} %copy-done.13, s32[]{:T(128)} %bitcast.8, s32[]{:T(128)} %bitcast.7), kind=kLoop, calls=%fused_computation.27 | loop fusion | flops 13824 | bytes 10248 | tf_op jit(solution)/shard_map/mul | solution.py:267
  26.0 0.1 fusion.9
  26.1 0.6 concatenate.10.beams
  26.7 0.0 copy-done.12
  26.8 0.0 copy-start.11
  26.8 0.7 copy-done.11
  27.5 1.4 %prepare.1 = (f32[512,1024]{1,0:T(8,128)S(1)}, bf16[256,768]{1,0:T(8,128)(2,1)S(1)}, f32[384,768]{1,0:T(8,128)S(1)}, bf16[1024,512]{1,0:T(8,128)(2,1)S(1)}) custom-call(s32[1]{0:T(128)} %bitcast.3.place, f32[8,512]{1,0:T(8,128)S(1)} %copy-done.11, bf16[512,768]{1,0:T(8,128)(2,1)S(1)} %copy-done.1, bf16[512,768]{1,0:T(8,128)(2,1)S(1)} %copy-done.2, ...), custom_call_target="tpu_custom_call" | custom-call | tf_op jit(solution)/shard_map/prepare/pallas_call | solution.py:214
  28.9 1.3 %copy-done.3 = f32[512,1024]{1,0:T(8,128)} copy-done((f32[512,1024]{1,0:T(8,128)}, f32[512,1024]{1,0:T(8,128)S(1)}, u32[]{:S(2)}) %copy-start.3) | copy-done | bytes 2097176
  30.2 1.0 %copy-done.5 = bf16[1024,512]{1,0:T(8,128)(2,1)} copy-done((bf16[1024,512]{1,0:T(8,128)(2,1)}, bf16[1024,512]{1,0:T(8,128)(2,1)S(1)}, u32[]{:S(2)}) %copy-start.5) | copy-done | bytes 1048600
  31.2 0.7 copy-done.8
  32.0 11.4 %all-to-all-done = bf16[128,9,2,128]{3,2,1,0:T(2,128)(2,1)S(1)} async-done(((bf16[128,9,2,128]{3,2,1,0:T(2,128)(2,1)}), bf16[128,9,2,128]{3,2,1,0:T(2,128)(2,1)S(1)}, u32[]{:S(2)}, u32[]{:S(2)}) %all-to-all-start) | async-done | bytes 589856 | tf_op jit(solution)/shard_map/all_to_all | solution.py:294
  43.3 1.6 %copy-done.4 = f32[512,1024]{1,0:T(8,128)S(1)} copy-done((f32[512,1024]{1,0:T(8,128)S(1)}, f32[512,1024]{1,0:T(8,128)}, u32[]{:S(2)}) %copy-start.4) | copy-done | bytes 2097176
  44.9 1.1 %copy-done.7 = bf16[768,512]{1,0:T(8,128)(2,1)S(1)} copy-done((bf16[768,512]{1,0:T(8,128)(2,1)S(1)}, bf16[768,512]{1,0:T(8,128)(2,1)}, u32[]{:S(2)}) %copy-start.7) | copy-done | bytes 786456
  46.1 1.0 %copy-done.9 = bf16[256,768]{1,0:T(8,128)(2,1)S(1)} copy-done((bf16[256,768]{1,0:T(8,128)(2,1)S(1)}, bf16[256,768]{1,0:T(8,128)(2,1)}, u32[]{:S(2)}) %copy-start.9) | copy-done | bytes 393240
  47.1 5.0 %propagate.1 = bf16[256,128]{1,0:T(8,128)(2,1)} custom-call(bf16[2304,128]{1,0:T(8,128)(2,1)S(1)} %bitcast.33, f32[512,1024]{1,0:T(8,128)S(1)} %copy-done.4, bf16[512,768]{1,0:T(8,128)(2,1)S(1)} %copy-done.1, bf16[768,512]{1,0:T(8,128)(2,1)S(1)} %copy-done.7, bf16[512,768]{1,0:T(8,128)(2,1)S(1)} %copy-done.2, bf16[256,768]{1,0:T(8,128)(2,1)S(1)} %copy-done.9, ...), custom_call_target="tpu_custom_call" | custom-call | tf_op jit(solution)/shard_map/propagate/pallas_call | solution.py:230
  52.0 9.5 %all-to-all-start.1 = ((bf16[128,2,128]{2,1,0:T(2,128)(2,1)}), bf16[128,2,128]{2,1,0:T(2,128)(2,1)S(1)}, u32[]{:S(2)}, u32[]{:S(2)}) async-start(bf16[128,2,128]{2,1,0:T(2,128)(2,1)} %bitcast.10), calls=%async_computation.1 | async-start | bytes 131072 | tf_op jit(solution)/shard_map/all_to_all | solution.py:302
  61.6 0.1 cosine_select_fusion
  61.7 12.1 %all-to-all-done.1 = bf16[128,2,128]{2,1,0:T(2,128)(2,1)S(1)} async-done(((bf16[128,2,128]{2,1,0:T(2,128)(2,1)}), bf16[128,2,128]{2,1,0:T(2,128)(2,1)S(1)}, u32[]{:S(2)}, u32[]{:S(2)}) %all-to-all-start.1) | async-done | bytes 65568 | tf_op jit(solution)/shard_map/all_to_all | solution.py:302
  73.9 1.2 %copy-done.6 = bf16[1024,512]{1,0:T(8,128)(2,1)S(1)} copy-done((bf16[1024,512]{1,0:T(8,128)(2,1)S(1)}, bf16[1024,512]{1,0:T(8,128)(2,1)}, u32[]{:S(2)}) %copy-start.6) | copy-done | bytes 1048600
  75.1 0.9 %finish.1 = f32[2,16,512]{2,1,0:T(8,128)} custom-call(bf16[256,128]{1,0:T(8,128)(2,1)S(1)} %bitcast.34, bf16[1024,512]{1,0:T(8,128)(2,1)S(1)} %copy-done.6, f32[2,512]{1,0:T(2,128)S(1)} %pad_maximum_fusion.1.prop), custom_call_target="tpu_custom_call" | custom-call | tf_op jit(solution)/shard_map/finish/pallas_call | solution.py:248
  (21 shorter events, 0.1 us)
Async XLA Ops:
  0.0 23.9 %copy-start = (s32[64,2]{0,1:T(2,128)S(1)}, s32[64,2]{0,1:T(2,128)}, u32[]{:S(2)}) copy-start(s32[64,2]{0,1:T(2,128)} %param.9) | copy-start | bytes 1540
  0.0 26.7 %copy-start.1 = (bf16[512,768]{1,0:T(8,128)(2,1)S(1)}, bf16[512,768]{1,0:T(8,128)(2,1)}, u32[]{:S(2)}) copy-start(bf16[512,768]{1,0:T(8,128)(2,1)} %constant.104.clone.right) | copy-start | bytes 2359300
  0.0 26.7 %copy-start.2 = (bf16[512,768]{1,0:T(8,128)(2,1)S(1)}, bf16[512,768]{1,0:T(8,128)(2,1)}, u32[]{:S(2)}) copy-start(bf16[512,768]{1,0:T(8,128)(2,1)} %constant.106.clone.back) | copy-start | bytes 2359300
  0.0 26.7 %copy-start.12 = (f32[8,384]{1,0:T(8,128)S(1)}, f32[8,384]{1,0:T(8,128)}, u32[]{:S(2)}) copy-start(f32[8,384]{1,0:T(8,128)} %constant.107.clone.chirp) | copy-start | bytes 36868
  0.0 26.7 %copy-start.10 = (f32[384,8]{1,0:T(8,128)S(1)}, f32[384,8]{1,0:T(8,128)}, u32[]{:S(2)}) copy-start(f32[384,8]{1,0:T(8,128)} %constant.108.chirp_t) | copy-start | bytes 36868
  0.0 24.5 %copy-start.13 = (s32[512,2]{0,1:T(2,128)S(1)}, s32[512,2]{0,1:T(2,128)}, u32[]{:S(2)}) copy-start(s32[512,2]{0,1:T(2,128)} %param.8) | copy-start | bytes 12292
  3.1 40.3 %all-to-all-start = ((bf16[128,9,2,128]{3,2,1,0:T(2,128)(2,1)}), bf16[128,9,2,128]{3,2,1,0:T(2,128)(2,1)S(1)}, u32[]{:S(2)}, u32[]{:S(2)}) async-start(bf16[128,9,2,128]{3,2,1,0:T(2,128)(2,1)} %pad_maximum_fusion), calls=%async_computation | async-start | bytes 1179648 | tf_op jit(solution)/shard_map/all_to_all | solution.py:294
  26.8 0.7 copy-start.11
  28.9 1.3 %copy-start.3 = (f32[512,1024]{1,0:T(8,128)}, f32[512,1024]{1,0:T(8,128)S(1)}, u32[]{:S(2)}) copy-start(f32[512,1024]{1,0:T(8,128)S(1)} %get-tuple-element.9.phi) | copy-start | bytes 6291460
  30.2 1.0 %copy-start.5 = (bf16[1024,512]{1,0:T(8,128)(2,1)}, bf16[1024,512]{1,0:T(8,128)(2,1)S(1)}, u32[]{:S(2)}) copy-start(bf16[1024,512]{1,0:T(8,128)(2,1)S(1)} %get-tuple-element.12.final) | copy-start | bytes 3145732
  31.2 0.7 copy-start.8
  43.3 1.6 %copy-start.4 = (f32[512,1024]{1,0:T(8,128)S(1)}, f32[512,1024]{1,0:T(8,128)}, u32[]{:S(2)}) copy-start(f32[512,1024]{1,0:T(8,128)} %copy-done.3) | copy-start | bytes 6291460
  44.9 1.1 %copy-start.7 = (bf16[768,512]{1,0:T(8,128)(2,1)S(1)}, bf16[768,512]{1,0:T(8,128)(2,1)}, u32[]{:S(2)}) copy-start(bf16[768,512]{1,0:T(8,128)(2,1)} %constant.105.clone.left) | copy-start | bytes 2359300
  46.1 1.0 %copy-start.9 = (bf16[256,768]{1,0:T(8,128)(2,1)S(1)}, bf16[256,768]{1,0:T(8,128)(2,1)}, u32[]{:S(2)}) copy-start(bf16[256,768]{1,0:T(8,128)(2,1)} %copy-done.8) | copy-start | bytes 1179652
  52.0 21.8 %all-to-all-start.1 = ((bf16[128,2,128]{2,1,0:T(2,128)(2,1)}), bf16[128,2,128]{2,1,0:T(2,128)(2,1)S(1)}, u32[]{:S(2)}, u32[]{:S(2)}) async-start(bf16[128,2,128]{2,1,0:T(2,128)(2,1)} %bitcast.10), calls=%async_computation.1 | async-start | bytes 131072 | tf_op jit(solution)/shard_map/all_to_all | solution.py:302
  73.9 1.2 %copy-start.6 = (bf16[1024,512]{1,0:T(8,128)(2,1)S(1)}, bf16[1024,512]{1,0:T(8,128)(2,1)}, u32[]{:S(2)}) copy-start(bf16[1024,512]{1,0:T(8,128)(2,1)} %copy-done.5) | copy-start | bytes 3145732

commit v2 on v1

--- a/solution.py
+++ b/solution.py
@@ -100,7 +100,7 @@
     return lax.dot_general(a, b, (((1,), (1,)), ((), ())), preferred_element_type=F32)
 
 
-def prepare_kernel(place, beams, right, back, chirp, chirp_t, phi, inverse, prop, final):
+def prepare_kernel(place, beams, right, back, chirp, chirp_t, phi, inverse, prop):
     index = lax.broadcasted_iota(jnp.int32, (BAND, G), 0).astype(F32)
     on_x = index == beams[0:1, :]
     on_y = jnp.where(index == beams[1:2, :], 1.0, 0.0).astype(BF16)
@@ -134,6 +134,9 @@
     yi = chirp[1:2, :]
     prop[:, :NQ] = jnp.where(inside, xr * yr - xi * yi, 0.0)
     prop[:, NQ:] = jnp.where(inside, xr * yi + xi * yr, 0.0)
+
+
+def finish_table_kernel(right, sent, final):
     for k in range(G // BLOCK):
         rows = slice(k * BLOCK, (k + 1) * BLOCK)
         top = slice(2 * k * BLOCK, (2 * k + 1) * BLOCK)
@@ -144,13 +147,32 @@
         final[low, BAND:] = right[rows, 0:BAND]
 
 
-def main_kernel(cells, phi, right, left, back, inverse, prop, out, wide, data, half, spec, fold):
+def main_kernel(
+    cells, right, phi_far, left_far, inverse_far, prop_far, back_far, out,
+    wide, data, half, spec, fold, phi, left, inverse, prop, back, phi_sems, sems,
+):
+    chunks = [
+        pltpu.make_async_copy(
+            phi_far.at[pl.ds(128 * j, 128), :], phi.at[pl.ds(128 * j, 128), :], phi_sems.at[j]
+        )
+        for j in range(4)
+    ]
+    for copy in chunks:
+        copy.start()
+    far = ((left_far, left), (prop_far, prop), (inverse_far, inverse), (back_far, back))
+    copies = [pltpu.make_async_copy(a, b, sems.at[k]) for k, (a, b) in enumerate(far)]
+    for copy in copies:
+        copy.start()
     wide[...] = cells[...].astype(F32)
     for j in range(4):
         rows = slice(128 * j, 128 * j + 128)
+        factors = [
+            phase_factor(wide[pl.ds(4 * j + h, 128, stride=ROWS), :]) for h in range(4)
+        ]
+        chunks[j].wait()
         for h in range(4):
             cols = slice(128 * h, 128 * h + 128)
-            cos, sin = phase_factor(wide[pl.ds(4 * j + h, 128, stride=ROWS), :])
+            cos, sin = factors[h]
             pr = phi[rows, 128 * h : 128 * h + 128]
             pi = phi[rows, G + 128 * h : G + 128 * h + 128]
             data[rows, cols] = (pr * cos - pi * sin).astype(BF16)
@@ -159,6 +181,8 @@
         two = dot(data[rows, G:], right[...])
         half[rows, :NQ] = (one[:, :NQ] - two[:, NQ:]).astype(BF16)
         half[rows, NQ:] = (one[:, NQ:] + two[:, :NQ]).astype(BF16)
+    for copy in copies:
+        copy.wait()
     for j in range(3):
         rows = slice(128 * j, 128 * j + 128)
         one = dot(left[rows, :], half[...])
@@ -206,7 +230,8 @@
 
 
 VMEM = pl.BlockSpec(memory_space=pltpu.VMEM)
-LIMIT = pltpu.CompilerParams(vmem_limit_bytes=12 * 1024 * 1024)
+LIMIT = pltpu.CompilerParams(vmem_limit_bytes=16 * 1024 * 1024)
+FAR = pl.BlockSpec(memory_space=pltpu.HBM)
 SMEM = pl.BlockSpec(memory_space=pltpu.SMEM)
 
 
@@ -214,22 +239,21 @@
     return pl.pallas_call(
         prepare_kernel,
         in_specs=[SMEM] + [VMEM] * 5,
-        out_specs=[VMEM] * 4,
+        out_specs=[VMEM] * 3,
         out_shape=[
-            jax.ShapeDtypeStruct((G, 2 * G), F32),
-            jax.ShapeDtypeStruct((4 * BLOCK, 2 * NQ), BF16),
-            jax.ShapeDtypeStruct((NQ, 2 * NQ), F32),
-            jax.ShapeDtypeStruct((2 * G, 2 * BAND), BF16),
+            pltpu.HBM((G, 2 * G), F32),
+            pltpu.HBM((4 * BLOCK, 2 * NQ), BF16),
+            pltpu.HBM((NQ, 2 * NQ), F32),
         ],
         compiler_params=LIMIT,
         name="prepare",
     )(place, beams, right, back, chirp, chirp.T)
 
 
-def main(cells, phi, right, left, back, inverse, prop):
+def main(cells, right, phi, left, inverse, prop, back):
     return pl.pallas_call(
         main_kernel,
-        in_specs=[VMEM] * 7,
+        in_specs=[VMEM] * 2 + [FAR] * 5,
         out_specs=VMEM,
         out_shape=jax.ShapeDtypeStruct((BAND, 2 * BLOCK), BF16),
         scratch_shapes=[
@@ -238,10 +262,31 @@
             pltpu.VMEM((G, 2 * NQ), BF16),
             pltpu.VMEM((NQ, 2 * NQ), BF16),
             pltpu.VMEM((2 * NQ, 4 * BLOCK), BF16),
+            pltpu.VMEM(phi.shape, F32),
+            pltpu.VMEM(left.shape, BF16),
+            pltpu.VMEM(inverse.shape, BF16),
+            pltpu.VMEM(prop.shape, F32),
+            pltpu.VMEM(back.shape, BF16),
+            pltpu.SemaphoreType.DMA((4,)),
+            pltpu.SemaphoreType.DMA((4,)),
         ],
         compiler_params=LIMIT,
         name="propagate",
-    )(cells, phi, right, left, back, inverse, prop)
+    )(cells, right, phi, left, inverse, prop, back)
+
+
+placed = pltpu.with_memory_space_constraint
+
+
+def finish_table(right, sent):
+    return pl.pallas_call(
+        finish_table_kernel,
+        in_specs=[VMEM, FAR],
+        out_specs=VMEM,
+        out_shape=jax.ShapeDtypeStruct((2 * G, 2 * BAND), BF16),
+        compiler_params=LIMIT,
+        name="finish_table",
+    )(right, sent)
 
 
 def finish(parts, final, prop):
@@ -279,11 +324,41 @@
     return jnp.concatenate([inside * jnp.cos(angle), inside * jnp.sin(angle)], 1)
 
 
-def message(potential, peers):
-    near = potential[0].reshape(1, 8, 2, 128)
-    far = potential[1].reshape(4, 8, BLOCK).swapaxes(0, 1).reshape(8, 1, 2, 128)
-    far = jnp.broadcast_to(far, (8, peers // 8, 2, 128)).reshape(peers, 1, 2, 128)
-    return jnp.concatenate([jnp.broadcast_to(near, (peers, 8, 2, 128)), far], 1)
+def message_kernel(cells, out, rows, block):
+    wide = cells[...].astype(F32)
+    for k in range(16):
+        rows[k : k + 1, :] = wide[0:1, 128 * k : 128 * k + 128]
+    near = rows[...]
+    for m in range(8):
+        block[ROWS * m : ROWS * m + 16, :] = near
+    low = lax.broadcasted_iota(jnp.int32, (1, 128), 1) < BLOCK
+    for r in range(8):
+        for h in range(2):
+            at = 128 * (8 * h + r // 2)
+            one = wide[1:2, at : at + 128]
+            two = wide[1:2, at + G : at + G + 128]
+            if r % 2 == 0:
+                own = jnp.where(low, one, pltpu.roll(two, BLOCK, 1))
+            else:
+                own = jnp.where(low, pltpu.roll(one, BLOCK, 1), two)
+            for m in range(8):
+                block[ROWS * m + 16 + h : ROWS * m + 17 + h, :] = own
+        copies = block[...].astype(BF16)
+        size = 8 * ROWS
+        out[2 * r * size : (2 * r + 1) * size, :] = copies
+        out[(2 * r + 1) * size : (2 * r + 2) * size, :] = copies
+
+
+def message(potential):
+    return pl.pallas_call(
+        message_kernel,
+        in_specs=[VMEM],
+        out_specs=VMEM,
+        out_shape=pltpu.VMEM((128 * ROWS, 128), BF16),
+        scratch_shapes=[pltpu.VMEM((16, 128), F32), pltpu.VMEM((8 * ROWS, 128), F32)],
+        compiler_params=LIMIT,
+        name="message",
+    )(potential)
 
 
 def local(potential, wave_vectors, probe_sites):
@@ -291,15 +366,19 @@
     peers = lax.axis_size("beam")
     position = lax.axis_index("beam")
     probes = peers // 8
-    cells = lax.all_to_all(message(potential, peers), "beam", 0, 0, tiled=True)
+    mine = message(potential).reshape(peers, ROWS // 2, 2, 128)
+    cells = lax.all_to_all(mine, "beam", 0, 0, tiled=True)
     site = lax.dynamic_index_in_dim(
         probe_sites, lax.axis_index("grp") * probes + position % probes, 0, keepdims=False
     )
     beams = own_coefficients(wave_vectors, site)
     place = (position // probes).reshape(1)
-    phi, inverse, prop, final = prepare(place, beams, right, back, chirp)
-    sent = main(cells.reshape(peers * ROWS, 128), phi, right, left, back, inverse, prop)
+    phi, inverse, prop = prepare(place, beams, right, back, chirp)
+    near = [placed(a, pltpu.VMEM) for a in (cells.reshape(peers * ROWS, 128), right)]
+    far = [placed(a, pltpu.HBM) for a in (phi, left, inverse, prop, back)]
+    sent = main(*near, *far)
     parts = lax.all_to_all(sent.reshape(peers, 2, 128), "beam", 0, 0, tiled=True)
+    final = finish_table(right, sent)
     return finish(parts.reshape(2 * peers, 128), final, band_rows(2 * position))
 
 

time: 76.4 us -> 71.7 us (0.938)
  local copies, waits for them, and re-layouts: 11.4 us -> 3.14 us
  Pallas kernels: 7.32 us -> 11.5 us
    unnamed x28 -> x12, local copies, waits for them, and re-layouts: 8.73 us -> 2.45 us
    pallas_call x1 -> x3, Pallas kernels: 4.98 us -> 7.42 us  [the longest x1 6.37 us: main(): pl.pallas_call(main_kernel, in_specs=[VMEM] * 2 + [FAR] * 5, out_specs=VM...]
    pallas_call x1, Pallas kernels: 1.42 us -> 3.15 us  [prepare(): pl.pallas_call(prepare_kernel, in_specs=[SMEM] + [VMEM] * 5, out_specs=[V...]
    concatenate x1 -> x0, other arithmetic: 1.6 us -> none  [message(): return jnp.concatenate([jnp.broadcast_to(near, (peers, 8, 2, 128)), far], 1)]
    slice x1 -> x0, local copies, waits for them, and re-layouts: 0.9 us -> none  [message(): near = potential[0].reshape(1, 8, 2, 128)]
    convert_element_type x1, other arithmetic: 0.01 us -> 0.77 us  [own_coefficients(): (wave_y + offset).astype(F32)]
  transfers between devices with their start and end apart: 2 -> 2, of which waited for: 2 -> 2; matrix products, arithmetic and copies ran while one was open for 4% -> 5% of each run, Pallas kernels for 2% -> 5%
where the time goes in v2:
time: 71.7 us; the launch traced here: 71.2 us
  starting transfers between devices  30.3 us (42%)
  waiting for transfers between devices  23 us (32%)
  Pallas kernels  11.5 us (16%)
  local copies, waits for them, and re-layouts  3.14 us (4%)
  other arithmetic  3.09 us (4%)
    all_to_all x1, starting transfers between devices, local(): cells = lax.all_to_all(mine, 'beam', 0, 0, tiled=True)  20.8 us
    all_to_all x1, waiting for transfers between devices, local(): lax.all_to_all(sent.reshape(peers, 2, 128), 'beam', 0, 0, tiled=True)  12.1 us
    all_to_all x1, waiting for transfers between devices, local(): cells = lax.all_to_all(mine, 'beam', 0, 0, tiled=True)  11 us
    all_to_all x1, starting transfers between devices, local(): lax.all_to_all(sent.reshape(peers, 2, 128), 'beam', 0, 0, tiled=True)  9.53 us
    pallas_call x1, Pallas kernels, main(): pl.pallas_call(main_kernel, in_specs=[VMEM] * 2 + [FAR] * 5, out_specs=VM...  6.37 us
    pallas_call x1, Pallas kernels, prepare(): pl.pallas_call(prepare_kernel, in_specs=[SMEM] + [VMEM] * 5, out_specs=[V...  3.15 us
    unnamed x12, local copies, waits for them, and re-layouts  2.45 us
    mul x1, other arithmetic, own_coefficients(): coef_i = (weight * jnp.sin(angle)).astype(BF16).astype(F32) * G  2.1 us
  transfers between devices with their start and end apart: 2, of which 2 were waited for; matrix products, arithmetic and copies ran while one was open for 5% of the time, Pallas kernels for 5%

profile of v2, /device:TPU:1, one launch (start us, length us, event | category | flops | bytes accessed | tf_op | source)
XLA Modules:
  0.0 71.2 jit_solution(3695869194456456003)
XLA Ops:
  0.0 0.0 copy-start
  0.0 0.0 copy-start.1
  0.0 0.0 copy-start.2
  0.0 0.0 copy-start.5
  0.0 0.8 %copy-done.5 = bf16[2,2048]{1,0:T(2,128)(2,1)S(1)} copy-done((bf16[2,2048]{1,0:T(2,128)(2,1)S(1)}, bf16[2,2048]{1,0:T(2,128)(2,1)}, u32[]{:S(2)}) %copy-start.5) | copy-done | bytes 8216
  0.8 1.0 %message.1 = bf16[2304,128]{1,0:T(8,128)(2,1)} custom-call(bf16[2,2048]{1,0:T(2,128)(2,1)S(1)} %copy-done.5), custom_call_target="tpu_custom_call" | custom-call | tf_op jit(solution)/shard_map/message/pallas_call | solution.py:353
  1.8 20.8 %all-to-all-start = ((bf16[128,9,2,128]{3,2,1,0:T(2,128)(2,1)}), bf16[128,9,2,128]{3,2,1,0:T(2,128)(2,1)S(1)}, u32[]{:S(2)}, u32[]{:S(2)}) async-start(bf16[128,9,2,128]{3,2,1,0:T(2,128)(2,1)} %bitcast), calls=%async_computation | async-start | bytes 1179648 | tf_op jit(solution)/shard_map/all_to_all | solution.py:370
  22.7 0.0 copy-done
  22.7 0.1 constant_dynamic-slice_fusion
  22.7 0.6 fusion.14
  23.3 2.1 %fusion.12 = (f32[1,512]{1,0:T(1,128)S(1)}, f32[1,512]{1,0:T(1,128)S(1)}, f32[512,1]{0,1:T(1,128)S(1)}) fusion(s32[512,2]{0,1:T(2,128)} %param.8, s32[]{:T(128)} %bitcast.7, s32[]{:T(128)} %bitcast.6), kind=kLoop, calls=%fused_computation.23 | loop fusion | flops 13824 | bytes 10248 | tf_op jit(solution)/shard_map/mul | solution.py:312
  25.4 0.1 fusion.9
  25.5 0.8 %convert_bitcast_fusion = (f32[1,512]{1,0:T(1,128)S(1)}, f32[1,512]{1,0:T(1,128)S(1)}) fusion(s32[512,2]{0,1:T(2,128)} %param.8), kind=kLoop, calls=%fused_computation.27 | loop fusion | flops 2048 | bytes 8192 | tf_op jit(solution)/shard_map/convert_element_type | solution.py:314
  26.3 0.0 copy-done.1
  26.3 0.0 copy-done.2
  26.3 0.0 copy-start.3
  26.3 0.9 %copy-done.3 = f32[384,8]{1,0:T(8,128)S(1)} copy-done((f32[384,8]{1,0:T(8,128)S(1)}, f32[384,8]{1,0:T(8,128)}, u32[]{:S(2)}) %copy-start.3) | copy-done | bytes 12312
  27.3 0.0 copy-start.4
  27.3 0.7 copy-done.4
  28.0 3.1 %prepare.1 = (f32[512,1024]{1,0:T(8,128)}, bf16[256,768]{1,0:T(8,128)(2,1)}, f32[384,768]{1,0:T(8,128)}) custom-call(s32[1]{0:T(128)} %bitcast.2.place, f32[8,512]{1,0:T(8,128)S(1)} %concatenate.6.beams, bf16[512,768]{1,0:T(8,128)(2,1)S(1)} %copy-done.1, bf16[512,768]{1,0:T(8,128)(2,1)S(1)} %copy-done.2, f32[8,384]{1,0:T(8,128)S(1)} %copy-done.4, ...), custom_call_target="tpu_custom_call" | custom-call | tf_op jit(solution)/shard_map/prepare/pallas_call | solution.py:239
  31.1 11.0 %all-to-all-done = bf16[128,9,2,128]{3,2,1,0:T(2,128)(2,1)S(1)} async-done(((bf16[128,9,2,128]{3,2,1,0:T(2,128)(2,1)}), bf16[128,9,2,128]{3,2,1,0:T(2,128)(2,1)S(1)}, u32[]{:S(2)}, u32[]{:S(2)}) %all-to-all-start) | async-done | bytes 589856 | tf_op jit(solution)/shard_map/all_to_all | solution.py:370
  42.1 6.4 %propagate.1.sent = bf16[256,128]{1,0:T(8,128)(2,1)} custom-call(bf16[2304,128]{1,0:T(8,128)(2,1)S(1)} %bitcast.29, bf16[512,768]{1,0:T(8,128)(2,1)S(1)} %copy-done.1, f32[512,1024]{1,0:T(8,128)} %get-tuple-element.8.phi_far, bf16[768,512]{1,0:T(8,128)(2,1)} %constant.105.clone.left_far, bf16[256,768]{1,0:T(8,128)(2,1)} %get-tuple-element.9.inverse_far, ...), custom_call_target="tpu_custom_call" | custom-call | tf_op jit(solution)/shard_map/propagate/pallas_call | solution.py:254
  48.5 9.5 %all-to-all-start.1 = ((bf16[128,2,128]{2,1,0:T(2,128)(2,1)}), bf16[128,2,128]{2,1,0:T(2,128)(2,1)S(1)}, u32[]{:S(2)}, u32[]{:S(2)}) async-start(bf16[128,2,128]{2,1,0:T(2,128)(2,1)} %bitcast.9), calls=%async_computation.1 | async-start | bytes 131072 | tf_op jit(solution)/shard_map/all_to_all | solution.py:380
  58.0 0.1 cosine_select_fusion
  58.2 0.1 finish_table.1.final
  58.2 12.1 %all-to-all-done.1 = bf16[128,2,128]{2,1,0:T(2,128)(2,1)S(1)} async-done(((bf16[128,2,128]{2,1,0:T(2,128)(2,1)}), bf16[128,2,128]{2,1,0:T(2,128)(2,1)S(1)}, u32[]{:S(2)}, u32[]{:S(2)}) %all-to-all-start.1) | async-done | bytes 65568 | tf_op jit(solution)/shard_map/all_to_all | solution.py:380
  70.3 0.9 %finish.1 = f32[2,16,512]{2,1,0:T(8,128)} custom-call(bf16[256,128]{1,0:T(8,128)(2,1)S(1)} %bitcast.30, bf16[1024,512]{1,0:T(8,128)(2,1)S(1)} %finish_table.1.final, f32[2,512]{1,0:T(2,128)S(1)} %pad_maximum_fusion.prop), custom_call_target="tpu_custom_call" | custom-call | tf_op jit(solution)/shard_map/finish/pallas_call | solution.py:293
  (5 shorter events, 0.0 us)
Async XLA Ops:
  0.0 22.7 %copy-start = (s32[64,2]{0,1:T(2,128)S(1)}, s32[64,2]{0,1:T(2,128)}, u32[]{:S(2)}) copy-start(s32[64,2]{0,1:T(2,128)} %param.9) | copy-start | bytes 1540
  0.0 26.3 %copy-start.1 = (bf16[512,768]{1,0:T(8,128)(2,1)S(1)}, bf16[512,768]{1,0:T(8,128)(2,1)}, u32[]{:S(2)}) copy-start(bf16[512,768]{1,0:T(8,128)(2,1)} %constant.104.clone.right) | copy-start | bytes 2359300
  0.0 26.3 %copy-start.2 = (bf16[512,768]{1,0:T(8,128)(2,1)S(1)}, bf16[512,768]{1,0:T(8,128)(2,1)}, u32[]{:S(2)}) copy-start(bf16[512,768]{1,0:T(8,128)(2,1)} %constant.106.clone.back.back_far) | copy-start | bytes 2359300
  0.0 0.8 %copy-start.5 = (bf16[2,2048]{1,0:T(2,128)(2,1)S(1)}, bf16[2,2048]{1,0:T(2,128)(2,1)}, u32[]{:S(2)}) copy-start(bf16[2,2048]{1,0:T(2,128)(2,1)} %cells.1) | copy-start | bytes 24580
  1.8 40.3 %all-to-all-start = ((bf16[128,9,2,128]{3,2,1,0:T(2,128)(2,1)}), bf16[128,9,2,128]{3,2,1,0:T(2,128)(2,1)S(1)}, u32[]{:S(2)}, u32[]{:S(2)}) async-start(bf16[128,9,2,128]{3,2,1,0:T(2,128)(2,1)} %bitcast), calls=%async_computation | async-start | bytes 1179648 | tf_op jit(solution)/shard_map/all_to_all | solution.py:370
  26.3 0.9 %copy-start.3 = (f32[384,8]{1,0:T(8,128)S(1)}, f32[384,8]{1,0:T(8,128)}, u32[]{:S(2)}) copy-start(f32[384,8]{1,0:T(8,128)} %constant.108.chirp_t) | copy-start | bytes 36868
  27.3 0.7 copy-start.4
  48.5 21.8 %all-to-all-start.1 = ((bf16[128,2,128]{2,1,0:T(2,128)(2,1)}), bf16[128,2,128]{2,1,0:T(2,128)(2,1)S(1)}, u32[]{:S(2)}, u32[]{:S(2)}) async-start(bf16[128,2,128]{2,1,0:T(2,128)(2,1)} %bitcast.9), calls=%async_computation.1 | async-start | bytes 131072 | tf_op jit(solution)/shard_map/all_to_all | solution.py:380

commit v3 on v2

--- a/solution.py
+++ b/solution.py
@@ -14,7 +14,7 @@
 PHASE_SCALE = 2.5
 CHIRP_RATE = 20
 BLOCK = 64
-ROWS = 18
+ROWS = 10
 
 F32 = jnp.float32
 BF16 = jnp.bfloat16
@@ -92,6 +92,10 @@
     return 1.0 - 2.0 * sine * sine, 2.0 * sine * cosine
 
 
+def own_core():
+    return lax.axis_index("grp") % 2
+
+
 def dot(a, b):
     return jnp.dot(a, b, preferred_element_type=F32)
 
@@ -100,7 +104,7 @@
     return lax.dot_general(a, b, (((1,), (1,)), ((), ())), preferred_element_type=F32)
 
 
-def prepare_kernel(place, beams, right, back, chirp, chirp_t, phi, inverse, prop):
+def prepare_kernel(beams, right, back, chirp, chirp_t, phi, inverse, prop):
     index = lax.broadcasted_iota(jnp.int32, (BAND, G), 0).astype(F32)
     on_x = index == beams[0:1, :]
     on_y = jnp.where(index == beams[1:2, :], 1.0, 0.0).astype(BF16)
@@ -114,9 +118,9 @@
     band_r = right[:, 0:BAND]
     band_i = right[:, NQ : NQ + BAND]
     both = jnp.concatenate([band_r, band_i], 1)
-    phi[:, :G] = dot_t(jnp.concatenate([mid_r, mid_i], 1).astype(BF16), both)
-    phi[:, G:] = dot_t(jnp.concatenate([mid_i, -mid_r], 1).astype(BF16), both)
-    start = pl.multiple_of(place[0] * BLOCK, BLOCK)
+    phi[:, :G] = dot_t(jnp.concatenate([mid_r, mid_i], 1).astype(BF16), both).astype(BF16)
+    phi[:, G:] = dot_t(jnp.concatenate([mid_i, -mid_r], 1).astype(BF16), both).astype(BF16)
+    start = pl.multiple_of(lax.axis_index("beam") // 16 * BLOCK, BLOCK)
     own_r = right[pl.ds(start, BLOCK), 0:NQ]
     own_i = right[pl.ds(start, BLOCK), NQ:]
     inverse[0:64, :NQ] = own_r
@@ -147,41 +151,42 @@
         final[low, BAND:] = right[rows, 0:BAND]
 
 
+def forward_rows(wide, phi, right, data, half, first, offset):
+    for j in range(2):
+        rows = slice(128 * j, 128 * j + 128)
+        probe = pl.ds(pl.multiple_of(first + 128 * j, 128), 128)
+        for h in range(4):
+            cos, sin = phase_factor(wide[pl.ds(4 * j + h, 128, stride=ROWS), :])
+            pr = phi[probe, 128 * h : 128 * h + 128].astype(F32)
+            pi = phi[probe, G + 128 * h : G + 128 * h + 128].astype(F32)
+            data[rows, 128 * h : 128 * h + 128] = (pr * cos - pi * sin).astype(BF16)
+            data[rows, G + 128 * h : G + 128 * h + 128] = (pr * sin + pi * cos).astype(BF16)
+        one = dot(data[rows, :G], right[...])
+        two = dot(data[rows, G:], right[...])
+        kept = pl.ds(pl.multiple_of(offset + 128 * j, 128), 128)
+        half[kept, :NQ] = (one[:, :NQ] - two[:, NQ:]).astype(BF16)
+        half[kept, NQ:] = (one[:, NQ:] + two[:, :NQ]).astype(BF16)
+
+
+def early_kernel(cells, phi, right, half, wide, data):
+    wide[...] = cells[...].astype(F32)
+    forward_rows(wide, phi, right, data, half, own_core() * 256, 0)
+
+
 def main_kernel(
-    cells, right, phi_far, left_far, inverse_far, prop_far, back_far, out,
-    wide, data, half, spec, fold, phi, left, inverse, prop, back, phi_sems, sems,
+    other, cells, early, right, phi, left_far, inverse_far, prop_far, back_far, out,
+    wide, data, half, spec, fold, last, left, inverse, prop, back, sems,
 ):
-    chunks = [
-        pltpu.make_async_copy(
-            phi_far.at[pl.ds(128 * j, 128), :], phi.at[pl.ds(128 * j, 128), :], phi_sems.at[j]
-        )
-        for j in range(4)
-    ]
-    for copy in chunks:
-        copy.start()
     far = ((left_far, left), (prop_far, prop), (inverse_far, inverse), (back_far, back))
     copies = [pltpu.make_async_copy(a, b, sems.at[k]) for k, (a, b) in enumerate(far)]
     for copy in copies:
         copy.start()
+    wide[...] = other[...].astype(F32)
+    start = own_core() * 256
+    half[pl.ds(pl.multiple_of(start, 256), 256), :] = early[...]
+    forward_rows(wide, phi, right, data, half, 256 - start, 256 - start)
     wide[...] = cells[...].astype(F32)
-    for j in range(4):
-        rows = slice(128 * j, 128 * j + 128)
-        factors = [
-            phase_factor(wide[pl.ds(4 * j + h, 128, stride=ROWS), :]) for h in range(4)
-        ]
-        chunks[j].wait()
-        for h in range(4):
-            cols = slice(128 * h, 128 * h + 128)
-            cos, sin = factors[h]
-            pr = phi[rows, 128 * h : 128 * h + 128]
-            pi = phi[rows, G + 128 * h : G + 128 * h + 128]
-            data[rows, cols] = (pr * cos - pi * sin).astype(BF16)
-            data[rows, G + 128 * h : G + 128 * h + 128] = (pr * sin + pi * cos).astype(BF16)
-        one = dot(data[rows, :G], right[...])
-        two = dot(data[rows, G:], right[...])
-        half[rows, :NQ] = (one[:, :NQ] - two[:, NQ:]).astype(BF16)
-        half[rows, NQ:] = (one[:, NQ:] + two[:, :NQ]).astype(BF16)
-    for copy in copies:
+    for copy in copies[:3]:
         copy.wait()
     for j in range(3):
         rows = slice(128 * j, 128 * j + 128)
@@ -199,16 +204,17 @@
         fold[low, :128] = turned[:, 128:].astype(BF16)
         fold[low, 128:] = (-turned[:, :128]).astype(BF16)
     lane = lax.broadcasted_iota(jnp.int32, (128, 128), 1) < BLOCK
+    copies[3].wait()
     for j in range(4):
         rows = slice(128 * j, 128 * j + 128)
-        pair = wide[pl.ds(16 + j // 2, 128, stride=ROWS), :]
-        other = pltpu.roll(pair, BLOCK, 1)
-        own = jnp.where(lane, pair, other) if j % 2 == 0 else jnp.where(lane, other, pair)
+        pair = wide[pl.ds(8 + j // 2, 128, stride=ROWS), :]
+        swapped = pltpu.roll(pair, BLOCK, 1)
+        own = jnp.where(lane, pair, swapped) if j % 2 == 0 else jnp.where(lane, swapped, pair)
         cos, sin = phase_factor(own)
         wave = dot(back[rows, :], fold[...])
-        data[rows, :128] = (wave[:, :128] * cos + wave[:, 128:] * sin).astype(BF16)
-        data[rows, 128:256] = (wave[:, 128:] * cos - wave[:, :128] * sin).astype(BF16)
-    total = dot(left[0:BAND, :], data[:, :128]) + dot(left[NQ : NQ + BAND, :], data[:, 128:256])
+        last[rows, :128] = (wave[:, :128] * cos + wave[:, 128:] * sin).astype(BF16)
+        last[rows, 128:] = (wave[:, 128:] * cos - wave[:, :128] * sin).astype(BF16)
+    total = dot(left[0:BAND, :], last[:, :128]) + dot(left[NQ : NQ + BAND, :], last[:, 128:])
     out[...] = total.astype(BF16)
 
 
@@ -232,50 +238,58 @@
 VMEM = pl.BlockSpec(memory_space=pltpu.VMEM)
 LIMIT = pltpu.CompilerParams(vmem_limit_bytes=16 * 1024 * 1024)
 FAR = pl.BlockSpec(memory_space=pltpu.HBM)
-SMEM = pl.BlockSpec(memory_space=pltpu.SMEM)
-
-
-def prepare(place, beams, right, back, chirp):
+
+
+def prepare(beams, right, back, chirp):
     return pl.pallas_call(
         prepare_kernel,
-        in_specs=[SMEM] + [VMEM] * 5,
+        in_specs=[VMEM] * 5,
         out_specs=[VMEM] * 3,
         out_shape=[
-            pltpu.HBM((G, 2 * G), F32),
+            pltpu.VMEM((G, 2 * G), BF16),
             pltpu.HBM((4 * BLOCK, 2 * NQ), BF16),
             pltpu.HBM((NQ, 2 * NQ), F32),
         ],
         compiler_params=LIMIT,
         name="prepare",
-    )(place, beams, right, back, chirp, chirp.T)
-
-
-def main(cells, right, phi, left, inverse, prop, back):
+    )(beams, right, back, chirp, chirp.T)
+
+
+def early(cells, phi, right):
+    return pl.pallas_call(
+        early_kernel,
+        in_specs=[VMEM] * 3,
+        out_specs=VMEM,
+        out_shape=pltpu.VMEM((G // 2, 2 * NQ), BF16),
+        scratch_shapes=[
+            pltpu.VMEM((cells.shape[0], 128), F32),
+            pltpu.VMEM((G // 2, 2 * G), BF16),
+        ],
+        compiler_params=LIMIT,
+        name="early",
+    )(cells, phi, right)
+
+
+def main(near, far):
+    rows = near[0].shape[0]
     return pl.pallas_call(
         main_kernel,
-        in_specs=[VMEM] * 2 + [FAR] * 5,
+        in_specs=[VMEM] * 5 + [FAR] * 4,
         out_specs=VMEM,
         out_shape=jax.ShapeDtypeStruct((BAND, 2 * BLOCK), BF16),
         scratch_shapes=[
-            pltpu.VMEM((cells.shape[0], 128), F32),
-            pltpu.VMEM((G, 2 * G), BF16),
+            pltpu.VMEM((rows, 128), F32),
+            pltpu.VMEM((G // 2, 2 * G), BF16),
             pltpu.VMEM((G, 2 * NQ), BF16),
             pltpu.VMEM((NQ, 2 * NQ), BF16),
             pltpu.VMEM((2 * NQ, 4 * BLOCK), BF16),
-            pltpu.VMEM(phi.shape, F32),
-            pltpu.VMEM(left.shape, BF16),
-            pltpu.VMEM(inverse.shape, BF16),
-            pltpu.VMEM(prop.shape, F32),
-            pltpu.VMEM(back.shape, BF16),
-            pltpu.SemaphoreType.DMA((4,)),
-            pltpu.SemaphoreType.DMA((4,)),
-        ],
+            pltpu.VMEM((G, 4 * BLOCK), BF16),
+        ]
+        + [pltpu.VMEM(a.shape, a.dtype) for a in far]
+        + [pltpu.SemaphoreType.DMA((4,))],
         compiler_params=LIMIT,
         name="propagate",
-    )(cells, right, phi, left, inverse, prop, back)
-
-
-placed = pltpu.with_memory_space_constraint
+    )(*near, *far)
 
 
 def finish_table(right, sent):
@@ -287,6 +301,9 @@
         compiler_params=LIMIT,
         name="finish_table",
     )(right, sent)
+
+
+placed = pltpu.with_memory_space_constraint
 
 
 def finish(parts, final, prop):
@@ -326,11 +343,12 @@
 
 def message_kernel(cells, out, rows, block):
     wide = cells[...].astype(F32)
-    for k in range(16):
-        rows[k : k + 1, :] = wide[0:1, 128 * k : 128 * k + 128]
+    near = jnp.where(own_core() == 0, wide[0:1, : 2 * G], wide[0:1, 2 * G :])
+    for k in range(8):
+        rows[k : k + 1, :] = near[:, 128 * k : 128 * k + 128]
     near = rows[...]
     for m in range(8):
-        block[ROWS * m : ROWS * m + 16, :] = near
+        block[ROWS * m : ROWS * m + 8, :] = near
     low = lax.broadcasted_iota(jnp.int32, (1, 128), 1) < BLOCK
     for r in range(8):
         for h in range(2):
@@ -342,7 +360,7 @@
             else:
                 own = jnp.where(low, pltpu.roll(one, BLOCK, 1), two)
             for m in range(8):
-                block[ROWS * m + 16 + h : ROWS * m + 17 + h, :] = own
+                block[ROWS * m + 8 + h : ROWS * m + 9 + h, :] = own
         copies = block[...].astype(BF16)
         size = 8 * ROWS
         out[2 * r * size : (2 * r + 1) * size, :] = copies
@@ -354,11 +372,19 @@
         message_kernel,
         in_specs=[VMEM],
         out_specs=VMEM,
-        out_shape=pltpu.VMEM((128 * ROWS, 128), BF16),
-        scratch_shapes=[pltpu.VMEM((16, 128), F32), pltpu.VMEM((8 * ROWS, 128), F32)],
+        out_shape=jax.ShapeDtypeStruct((128 * ROWS, 128), BF16),
+        scratch_shapes=[pltpu.VMEM((8, 128), F32), pltpu.VMEM((8 * ROWS, 128), F32)],
         compiler_params=LIMIT,
         name="message",
     )(potential)
+
+
+def near_groups(peers):
+    groups = []
+    for turn in range(2):
+        for core in range(2):
+            groups.append([4 * k + 2 * ((k + turn) % 2) + core for k in range(peers)])
+    return groups
 
 
 def local(potential, wave_vectors, probe_sites):
@@ -366,17 +392,24 @@
     peers = lax.axis_size("beam")
     position = lax.axis_index("beam")
     probes = peers // 8
+    group = lax.axis_index("grp")
     mine = message(potential).reshape(peers, ROWS // 2, 2, 128)
-    cells = lax.all_to_all(mine, "beam", 0, 0, tiled=True)
+    cells = lax.all_to_all(
+        mine, ("beam", "grp"), 0, 0, tiled=True, axis_index_groups=near_groups(peers)
+    )
     site = lax.dynamic_index_in_dim(
-        probe_sites, lax.axis_index("grp") * probes + position % probes, 0, keepdims=False
+        probe_sites, group * probes + position % probes, 0, keepdims=False
     )
     beams = own_coefficients(wave_vectors, site)
-    place = (position // probes).reshape(1)
-    phi, inverse, prop = prepare(place, beams, right, back, chirp)
-    near = [placed(a, pltpu.VMEM) for a in (cells.reshape(peers * ROWS, 128), right)]
-    far = [placed(a, pltpu.HBM) for a in (phi, left, inverse, prop, back)]
-    sent = main(*near, *far)
+    made = prepare(beams, right, back, chirp)
+    cells, phi, inverse, prop = lax.optimization_barrier((cells, *made))
+    cells = cells.reshape(peers * ROWS, 128)
+    other = lax.ppermute(cells, "grp", [(0, 1), (1, 0), (2, 3), (3, 2)])
+    cells, right_near, phi = (placed(a, pltpu.VMEM) for a in (cells, right, phi))
+    first = placed(early(cells, phi, right_near), pltpu.VMEM)
+    near = (placed(other, pltpu.VMEM), cells, first, right_near, phi)
+    far = [placed(a, pltpu.HBM) for a in (left, inverse, prop, back)]
+    sent = main(near, far)
     parts = lax.all_to_all(sent.reshape(peers, 2, 128), "beam", 0, 0, tiled=True)
     final = finish_table(right, sent)
     return finish(parts.reshape(2 * peers, 128), final, band_rows(2 * position))

time: 71.7 us -> 68.2 us (0.951)
  waiting for transfers between devices: 23 us -> 18.8 us
  starting transfers between devices: 30.3 us -> 31.9 us
  Pallas kernels: 11.5 us -> 10.4 us
    ppermute x0 -> x1, starting transfers between devices: none -> 5.18 us  [local(): other = lax.ppermute(cells, 'grp', [(0, 1), (1, 0), (2, 3), (3, 2)])]
    all_to_all x1, waiting for transfers between devices: 11 us -> 6.71 us  [local(): lax.all_to_all(mine, ('beam', 'grp'), 0, 0, tiled=True, axis_index_groups...]
    all_to_all x1, starting transfers between devices: 9.53 us -> 6.16 us  [local(): lax.all_to_all(sent.reshape(peers, 2, 128), 'beam', 0, 0, tiled=True)]
    pallas_call x2 -> x3, Pallas kernels: 9.51 us -> 8.52 us  [the longest x1 4.92 us: main(): pl.pallas_call(main_kernel, in_specs=[VMEM] * 5 + [FAR] * 4, out_specs=VM...]
  transfers between devices with their start and end apart: 2 -> 3, of which waited for: 2 -> 2; matrix products, arithmetic and copies ran while one was open for 5% -> 6% of each run, Pallas kernels for 5% -> 5%
where the time goes in v3:
time: 68.2 us; the launch traced here: 67.6 us
  starting transfers between devices  31.9 us (47%)
  waiting for transfers between devices  18.8 us (28%)
  Pallas kernels  10.4 us (15%)
  local copies, waits for them, and re-layouts  3.31 us (5%)
  other arithmetic  3.11 us (5%)
    all_to_all x1, starting transfers between devices, local(): lax.all_to_all(mine, ('beam', 'grp'), 0, 0, tiled=True, axis_index_groups...  20.5 us
    all_to_all x1, waiting for transfers between devices, local(): lax.all_to_all(sent.reshape(peers, 2, 128), 'beam', 0, 0, tiled=True)  12.1 us
    all_to_all x1, waiting for transfers between devices, local(): lax.all_to_all(mine, ('beam', 'grp'), 0, 0, tiled=True, axis_index_groups...  6.71 us
    all_to_all x1, starting transfers between devices, local(): lax.all_to_all(sent.reshape(peers, 2, 128), 'beam', 0, 0, tiled=True)  6.16 us
    ppermute x1, starting transfers between devices, local(): other = lax.ppermute(cells, 'grp', [(0, 1), (1, 0), (2, 3), (3, 2)])  5.18 us
    pallas_call x1, Pallas kernels, main(): pl.pallas_call(main_kernel, in_specs=[VMEM] * 5 + [FAR] * 4, out_specs=VM...  4.92 us
    unnamed x12, local copies, waits for them, and re-layouts  2.62 us
    pallas_call x1, Pallas kernels, prepare(): pl.pallas_call(prepare_kernel, in_specs=[VMEM] * 5, out_specs=[VMEM] * 3,...  2.44 us
  transfers between devices with their start and end apart: 3, of which 2 were waited for; matrix products, arithmetic and copies ran while one was open for 6% of the time, Pallas kernels for 5%

profile of v3, /device:TPU:1, one launch (start us, length us, event | category | flops | bytes accessed | tf_op | source)
XLA Modules:
  0.0 67.6 jit_solution(7772188806756443957)
XLA Ops:
  0.0 0.0 copy-start
  0.0 0.0 copy-start.1
  0.0 0.0 copy-start.3
  0.0 0.0 copy-start.5
  0.0 0.8 %copy-done.5 = bf16[2,2048]{1,0:T(2,128)(2,1)S(1)} copy-done((bf16[2,2048]{1,0:T(2,128)(2,1)S(1)}, bf16[2,2048]{1,0:T(2,128)(2,1)}, u32[]{:S(2)}) %copy-start.5) | copy-done | bytes 8216
  0.8 0.9 %message.1 = bf16[1280,128]{1,0:T(8,128)(2,1)} custom-call(bf16[2,2048]{1,0:T(2,128)(2,1)S(1)} %copy-done.5), custom_call_target="tpu_custom_call" | custom-call | tf_op jit(solution)/shard_map/message/pallas_call | solution.py:371
  1.7 20.5 %all-to-all-start = ((bf16[128,5,2,128]{3,2,1,0:T(2,128)(2,1)}), bf16[128,5,2,128]{3,2,1,0:T(2,128)(2,1)S(1)}, u32[]{:S(2)}, u32[]{:S(2)}) async-start(bf16[128,5,2,128]{3,2,1,0:T(2,128)(2,1)} %bitcast), calls=%async_computation | async-start | bytes 655360 | tf_op jit(solution)/shard_map/all_to_all | solution.py:397
  22.2 0.0 copy-done
  22.2 0.1 constant_dynamic-slice_fusion
  22.3 0.6 fusion.14
  22.9 2.1 %fusion.12 = (f32[1,512]{1,0:T(1,128)S(1)}, f32[1,512]{1,0:T(1,128)S(1)}, f32[512,1]{0,1:T(1,128)S(1)}) fusion(s32[512,2]{0,1:T(2,128)} %param.8, s32[]{:T(128)} %bitcast.5, s32[]{:T(128)} %bitcast.4), kind=kLoop, calls=%fused_computation.23 | loop fusion | flops 13824 | bytes 10248 | tf_op jit(solution)/shard_map/mul | solution.py:329
  25.0 0.1 fusion.9
  25.1 0.8 %convert_bitcast_fusion = (f32[1,512]{1,0:T(1,128)S(1)}, f32[1,512]{1,0:T(1,128)S(1)}) fusion(s32[512,2]{0,1:T(2,128)} %param.8), kind=kLoop, calls=%fused_computation.27 | loop fusion | flops 2048 | bytes 8192 | tf_op jit(solution)/shard_map/convert_element_type | solution.py:331
  25.9 0.0 copy-done.1
  25.9 0.0 copy-done.3
  25.9 0.0 copy-start.2
  25.9 1.1 %copy-done.2 = bf16[512,768]{1,0:T(8,128)(2,1)S(1)} copy-done((bf16[512,768]{1,0:T(8,128)(2,1)S(1)}, bf16[512,768]{1,0:T(8,128)(2,1)}, u32[]{:S(2)}) %copy-start.2) | copy-done | bytes 786456
  27.1 0.0 copy-start.4
  27.1 0.7 %copy-done.4 = f32[8,384]{1,0:T(8,128)S(1)} copy-done((f32[8,384]{1,0:T(8,128)S(1)}, f32[8,384]{1,0:T(8,128)}, u32[]{:S(2)}) %copy-start.4) | copy-done | bytes 12312
  27.8 2.4 %prepare.1 = (bf16[512,1024]{1,0:T(8,128)(2,1)S(1)}, bf16[256,768]{1,0:T(8,128)(2,1)}, f32[384,768]{1,0:T(8,128)}) custom-call(f32[8,512]{1,0:T(8,128)S(1)} %concatenate.6.beams, bf16[512,768]{1,0:T(8,128)(2,1)S(1)} %copy-done.1, bf16[512,768]{1,0:T(8,128)(2,1)S(1)} %copy-done.2, f32[8,384]{1,0:T(8,128)S(1)} %copy-done.4, f32[384,8]{1,0:T(8,128)S(1)} %copy-done.3), custom_call_target="tpu_custom_call" | custom-call | tf_op jit(solution)/shard_map/prepare/pallas_call | solution.py:244
  30.2 6.7 %all-to-all-done = bf16[128,5,2,128]{3,2,1,0:T(2,128)(2,1)S(1)} async-done(((bf16[128,5,2,128]{3,2,1,0:T(2,128)(2,1)}), bf16[128,5,2,128]{3,2,1,0:T(2,128)(2,1)S(1)}, u32[]{:S(2)}, u32[]{:S(2)}) %all-to-all-start) | async-done | bytes 327712 | tf_op jit(solution)/shard_map/all_to_all | solution.py:397
  36.9 5.2 %collective-permute-start = (bf16[1280,128]{1,0:T(8,128)(2,1)S(1)}, bf16[1280,128]{1,0:T(8,128)(2,1)S(1)}, u32[]{:S(2)}, u32[]{:S(2)}) collective-permute-start(bf16[1280,128]{1,0:T(8,128)(2,1)S(1)} %bitcast.28), channel_id=1, source_target_pairs={{0,1},{1,0},{2,3},{3,2},{4,5},{5,4},{6,7},{7,6},{8,9},{9,8},{10,11... | collective-permute-start | bytes 983048 | tf_op jit(solution)/shard_map/ppermute | solution.py:407
  42.1 1.2 %early.1 = bf16[256,768]{1,0:T(8,128)(2,1)S(1)} custom-call(bf16[1280,128]{1,0:T(8,128)(2,1)S(1)} %bitcast.29, bf16[512,1024]{1,0:T(8,128)(2,1)S(1)} %get-tuple-element.16.phi, bf16[512,768]{1,0:T(8,128)(2,1)S(1)} %copy-done.1), custom_call_target="tpu_custom_call" | custom-call | tf_op jit(solution)/shard_map/early/pallas_call | solution.py:259
  43.3 0.0 collective-permute-done.other
  43.4 4.9 %propagate.1.sent = bf16[256,128]{1,0:T(8,128)(2,1)} custom-call(bf16[1280,128]{1,0:T(8,128)(2,1)S(1)} %collective-permute-done.other, bf16[1280,128]{1,0:T(8,128)(2,1)S(1)} %bitcast.30, bf16[256,768]{1,0:T(8,128)(2,1)S(1)} %early.1, bf16[512,768]{1,0:T(8,128)(2,1)S(1)} %copy-done.1, bf16[512,1024]{1,0:T(8,128)(2,1)S(1)} %get-tuple-element.16.phi, ...), custom_call_target="tpu_custom_call" | custom-call | tf_op jit(solution)/shard_map/propagate/pallas_call | solution.py:275
  48.3 6.2 %all-to-all-start.1 = ((bf16[128,2,128]{2,1,0:T(2,128)(2,1)}), bf16[128,2,128]{2,1,0:T(2,128)(2,1)S(1)}, u32[]{:S(2)}, u32[]{:S(2)}) async-start(bf16[128,2,128]{2,1,0:T(2,128)(2,1)} %bitcast.8), calls=%async_computation.1 | async-start | bytes 131072 | tf_op jit(solution)/shard_map/all_to_all | solution.py:413
  54.4 0.1 cosine_select_fusion
  54.6 0.1 finish_table.1.final
  54.7 12.1 %all-to-all-done.1 = bf16[128,2,128]{2,1,0:T(2,128)(2,1)S(1)} async-done(((bf16[128,2,128]{2,1,0:T(2,128)(2,1)}), bf16[128,2,128]{2,1,0:T(2,128)(2,1)S(1)}, u32[]{:S(2)}, u32[]{:S(2)}) %all-to-all-start.1) | async-done | bytes 65568 | tf_op jit(solution)/shard_map/all_to_all | solution.py:413
  66.7 0.9 %finish.1 = f32[2,16,512]{2,1,0:T(8,128)} custom-call(bf16[256,128]{1,0:T(8,128)(2,1)S(1)} %bitcast.31, bf16[1024,512]{1,0:T(8,128)(2,1)S(1)} %finish_table.1.final, f32[2,512]{1,0:T(2,128)S(1)} %pad_maximum_fusion.prop), custom_call_target="tpu_custom_call" | custom-call | tf_op jit(solution)/shard_map/finish/pallas_call | solution.py:310
  (5 shorter events, 0.0 us)
Async XLA Ops:
  0.0 22.2 %copy-start = (s32[64,2]{0,1:T(2,128)S(1)}, s32[64,2]{0,1:T(2,128)}, u32[]{:S(2)}) copy-start(s32[64,2]{0,1:T(2,128)} %param.9) | copy-start | bytes 1540
  0.0 25.9 %copy-start.1 = (bf16[512,768]{1,0:T(8,128)(2,1)S(1)}, bf16[512,768]{1,0:T(8,128)(2,1)}, u32[]{:S(2)}) copy-start(bf16[512,768]{1,0:T(8,128)(2,1)} %constant.91.clone.right) | copy-start | bytes 2359300
  0.0 25.9 %copy-start.3 = (f32[384,8]{1,0:T(8,128)S(1)}, f32[384,8]{1,0:T(8,128)}, u32[]{:S(2)}) copy-start(f32[384,8]{1,0:T(8,128)} %constant.95.chirp_t) | copy-start | bytes 36868
  0.0 0.8 %copy-start.5 = (bf16[2,2048]{1,0:T(2,128)(2,1)S(1)}, bf16[2,2048]{1,0:T(2,128)(2,1)}, u32[]{:S(2)}) copy-start(bf16[2,2048]{1,0:T(2,128)(2,1)} %cells.1) | copy-start | bytes 24580
  1.7 35.3 %all-to-all-start = ((bf16[128,5,2,128]{3,2,1,0:T(2,128)(2,1)}), bf16[128,5,2,128]{3,2,1,0:T(2,128)(2,1)S(1)}, u32[]{:S(2)}, u32[]{:S(2)}) async-start(bf16[128,5,2,128]{3,2,1,0:T(2,128)(2,1)} %bitcast), calls=%async_computation | async-start | bytes 655360 | tf_op jit(solution)/shard_map/all_to_all | solution.py:397
  25.9 1.1 %copy-start.2 = (bf16[512,768]{1,0:T(8,128)(2,1)S(1)}, bf16[512,768]{1,0:T(8,128)(2,1)}, u32[]{:S(2)}) copy-start(bf16[512,768]{1,0:T(8,128)(2,1)} %constant.93.clone.back.back_far) | copy-start | bytes 2359300
  27.1 0.7 %copy-start.4 = (f32[8,384]{1,0:T(8,128)S(1)}, f32[8,384]{1,0:T(8,128)}, u32[]{:S(2)}) copy-start(f32[8,384]{1,0:T(8,128)} %constant.94.clone.chirp) | copy-start | bytes 36868
  36.9 6.4 %collective-permute-start = (bf16[1280,128]{1,0:T(8,128)(2,1)S(1)}, bf16[1280,128]{1,0:T(8,128)(2,1)S(1)}, u32[]{:S(2)}, u32[]{:S(2)}) collective-permute-start(bf16[1280,128]{1,0:T(8,128)(2,1)S(1)} %bitcast.28), channel_id=1, source_target_pairs={{0,1},{1,0},{2,3},{3,2},{4,5},{5,4},{6,7},{7,6},{8,9},{9,8},{10,11... | collective-permute-start | bytes 983048 | tf_op jit(solution)/shard_map/ppermute | solution.py:407
  48.3 18.5 %all-to-all-start.1 = ((bf16[128,2,128]{2,1,0:T(2,128)(2,1)}), bf16[128,2,128]{2,1,0:T(2,128)(2,1)S(1)}, u32[]{:S(2)}, u32[]{:S(2)}) async-start(bf16[128,2,128]{2,1,0:T(2,128)(2,1)} %bitcast.8), calls=%async_computation.1 | async-start | bytes 131072 | tf_op jit(solution)/shard_map/all_to_all | solution.py:413

commit v4 on v3

--- a/solution.py
+++ b/solution.py
@@ -13,8 +13,9 @@
 NQ = 384
 PHASE_SCALE = 2.5
 CHIRP_RATE = 20
-BLOCK = 64
-ROWS = 10
+PEERS = 32
+HALF = 256
+ROWS = 12
 
 F32 = jnp.float32
 BF16 = jnp.bfloat16
@@ -104,7 +105,7 @@
     return lax.dot_general(a, b, (((1,), (1,)), ((), ())), preferred_element_type=F32)
 
 
-def prepare_kernel(beams, right, back, chirp, chirp_t, phi, inverse, prop):
+def prepare_kernel(beams, right, back, chirp, chirp_t, phi, prop):
     index = lax.broadcasted_iota(jnp.int32, (BAND, G), 0).astype(F32)
     on_x = index == beams[0:1, :]
     on_y = jnp.where(index == beams[1:2, :], 1.0, 0.0).astype(BF16)
@@ -120,17 +121,6 @@
     both = jnp.concatenate([band_r, band_i], 1)
     phi[:, :G] = dot_t(jnp.concatenate([mid_r, mid_i], 1).astype(BF16), both).astype(BF16)
     phi[:, G:] = dot_t(jnp.concatenate([mid_i, -mid_r], 1).astype(BF16), both).astype(BF16)
-    start = pl.multiple_of(lax.axis_index("beam") // 16 * BLOCK, BLOCK)
-    own_r = right[pl.ds(start, BLOCK), 0:NQ]
-    own_i = right[pl.ds(start, BLOCK), NQ:]
-    inverse[0:64, :NQ] = own_r
-    inverse[0:64, NQ:] = own_i
-    inverse[64:128, :NQ] = -own_i
-    inverse[64:128, NQ:] = own_r
-    inverse[128:192, :NQ] = own_i
-    inverse[128:192, NQ:] = -own_r
-    inverse[192:256, :NQ] = own_r
-    inverse[192:256, NQ:] = own_i
     inside = chirp_t[:, 2:3] + chirp[2:3, :] < (G * G - 1) // 9 + 0.5
     xr = chirp_t[:, 0:1]
     xi = chirp_t[:, 1:2]
@@ -141,10 +131,10 @@
 
 
 def finish_table_kernel(right, sent, final):
-    for k in range(G // BLOCK):
-        rows = slice(k * BLOCK, (k + 1) * BLOCK)
-        top = slice(2 * k * BLOCK, (2 * k + 1) * BLOCK)
-        low = slice((2 * k + 1) * BLOCK, (2 * k + 2) * BLOCK)
+    for h in range(2):
+        rows = slice(h * HALF, h * HALF + HALF)
+        top = slice(2 * h * HALF, (2 * h + 1) * HALF)
+        low = slice((2 * h + 1) * HALF, (2 * h + 2) * HALF)
         final[top, :BAND] = right[rows, 0:BAND]
         final[top, BAND:] = right[rows, NQ : NQ + BAND]
         final[low, :BAND] = -right[rows, NQ : NQ + BAND]
@@ -174,65 +164,84 @@
 
 
 def main_kernel(
-    other, cells, early, right, phi, left_far, inverse_far, prop_far, back_far, out,
-    wide, data, half, spec, fold, last, left, inverse, prop, back, sems,
+    other, cells, early, right, phi, left, prop_far, back_far, out,
+    wide, data, half, spec, turn, fold, last, rows_in, rows_out, prop, back, sems,
 ):
-    far = ((left_far, left), (prop_far, prop), (inverse_far, inverse), (back_far, back))
+    far = ((prop_far, prop), (back_far, back))
     copies = [pltpu.make_async_copy(a, b, sems.at[k]) for k, (a, b) in enumerate(far)]
     for copy in copies:
         copy.start()
+    place = lax.axis_index("beam")
+    core = own_core()
     wide[...] = other[...].astype(F32)
-    start = own_core() * 256
+    start = core * 256
     half[pl.ds(pl.multiple_of(start, 256), 256), :] = early[...]
     forward_rows(wide, phi, right, data, half, 256 - start, 256 - start)
-    wide[...] = cells[...].astype(F32)
-    for copy in copies[:3]:
-        copy.wait()
+    side = pl.ds(pl.multiple_of(place // 16 % 2 * HALF, HALF), HALF)
+    copies[0].wait()
     for j in range(3):
         rows = slice(128 * j, 128 * j + 128)
+        low = slice(NQ + 128 * j, NQ + 128 * j + 128)
         one = dot(left[rows, :], half[...])
-        two = dot(left[NQ + 128 * j : NQ + 128 * j + 128, :], half[...])
+        two = dot(left[low, :], half[...])
         re = one[:, :NQ] - two[:, NQ:]
         im = one[:, NQ:] + two[:, :NQ]
         pr = prop[rows, :NQ]
         pi = prop[rows, NQ:]
-        spec[rows, :NQ] = (re * pr - im * pi).astype(BF16)
-        spec[rows, NQ:] = (re * pi + im * pr).astype(BF16)
-        turned = dot_t(spec[rows, :], inverse[...])
-        low = slice(NQ + 128 * j, NQ + 128 * j + 128)
-        fold[rows, :] = turned.astype(BF16)
-        fold[low, :128] = turned[:, 128:].astype(BF16)
-        fold[low, 128:] = (-turned[:, :128]).astype(BF16)
-    lane = lax.broadcasted_iota(jnp.int32, (128, 128), 1) < BLOCK
-    copies[3].wait()
-    for j in range(4):
-        rows = slice(128 * j, 128 * j + 128)
-        pair = wide[pl.ds(8 + j // 2, 128, stride=ROWS), :]
-        swapped = pltpu.roll(pair, BLOCK, 1)
-        own = jnp.where(lane, pair, swapped) if j % 2 == 0 else jnp.where(lane, swapped, pair)
-        cos, sin = phase_factor(own)
-        wave = dot(back[rows, :], fold[...])
-        last[rows, :128] = (wave[:, :128] * cos + wave[:, 128:] * sin).astype(BF16)
-        last[rows, 128:] = (wave[:, 128:] * cos - wave[:, :128] * sin).astype(BF16)
-    total = dot(left[0:BAND, :], last[:, :128]) + dot(left[NQ : NQ + BAND, :], last[:, 128:])
-    out[...] = total.astype(BF16)
-
-
-def final_kernel(parts, final, prop, out, total):
-    acc = dot(parts[0:32, :], final[0:128, :])
-    for k in range(1, 8):
-        acc = acc + dot(parts[32 * k : 32 * k + 32, :], final[128 * k : 128 * k + 128, :])
-    for k in range(4):
-        total[32 * k : 32 * k + 32, :] = acc[:, 128 * k : 128 * k + 128]
+        new_r = re * pr - im * pi
+        new_i = re * pi + im * pr
+        spec[rows, :NQ] = new_r.astype(BF16)
+        spec[rows, NQ:] = new_i.astype(BF16)
+        turn[rows, :NQ] = new_i.astype(BF16)
+        turn[rows, NQ:] = (-new_r).astype(BF16)
+        at_r = dot_t(spec[rows, :], right[side, :])
+        at_i = dot_t(turn[rows, :], right[side, :])
+        fold[rows, :HALF] = at_r.astype(BF16)
+        fold[rows, HALF:] = at_i.astype(BF16)
+        fold[low, :HALF] = (-at_i).astype(BF16)
+        fold[low, HALF:] = at_r.astype(BF16)
+    copies[1].wait()
+    for source in range(2):
+        if source == 1:
+            wide[...] = cells[...].astype(F32)
+        first = 256 - start if source == 0 else start
+        for j in range(2):
+            rows = pl.ds(pl.multiple_of(first + 128 * j, 128), 128)
+            wave = dot(back[rows, :], fold[...])
+            for q in range(2):
+                cos, sin = phase_factor(wide[pl.ds(8 + 2 * j + q, 128, stride=ROWS), :])
+                re = wave[:, 128 * q : 128 * q + 128]
+                im = wave[:, HALF + 128 * q : HALF + 128 * q + 128]
+                last[rows, 128 * q : 128 * q + 128] = (re * cos - im * sin).astype(BF16)
+                last[rows, HALF + 128 * q : HALF + 128 * q + 128] = (re * sin + im * cos).astype(BF16)
+    band = pl.multiple_of(place // PEERS * 2 * PEERS, 2 * PEERS)
+    one = dot(left[pl.ds(band, 2 * PEERS), :], last[...])
+    two = dot(left[pl.ds(NQ + band, 2 * PEERS), :], last[...])
+    parts = (one[:, :HALF] - two[:, HALF:], one[:, HALF:] + two[:, :HALF])
+    for q in range(4):
+        rows_in[...] = parts[q // 2][:, 128 * (q % 2) : 128 * (q % 2) + 128]
+        for row in range(2):
+            rows_out[pl.ds(2 * q + row, PEERS, stride=8), :] = rows_in[pl.ds(row, PEERS, stride=2), :]
+    out[...] = rows_out[...].astype(BF16)
+
+
+def final_kernel(parts, final, prop, out, wide, data):
+    wide[...] = parts[...].astype(F32)
+    for h in range(2):
+        for q in range(4):
+            for row in range(2):
+                own = wide[pl.ds(128 * h + 2 * q + row, 16, stride=8), :]
+                cols = slice(512 * h + 128 * q, 512 * h + 128 * q + 128)
+                data[16 * row : 16 * row + 16, cols] = own.astype(BF16)
+    acc = dot(data[...], final[...])
     for row in range(2):
-        for k in range(2):
-            re = total[pl.ds(32 * k + row, 16, stride=2), :]
-            im = total[pl.ds(64 + 32 * k + row, 16, stride=2), :]
-            pr = prop[row : row + 1, 128 * k : 128 * k + 128]
-            pi = prop[row : row + 1, BAND + 128 * k : BAND + 128 * k + 128]
-            cols = slice(row * BAND + 128 * k, row * BAND + 128 * k + 128)
-            out[0, :, cols] = re * pr - im * pi
-            out[1, :, cols] = re * pi + im * pr
+        re = acc[16 * row : 16 * row + 16, :BAND]
+        im = acc[16 * row : 16 * row + 16, BAND:]
+        pr = prop[row : row + 1, :BAND]
+        pi = prop[row : row + 1, BAND:]
+        cols = slice(row * BAND, row * BAND + BAND)
+        out[0, :, cols] = re * pr - im * pi
+        out[1, :, cols] = re * pi + im * pr
 
 
 VMEM = pl.BlockSpec(memory_space=pltpu.VMEM)
@@ -244,10 +253,9 @@
     return pl.pallas_call(
         prepare_kernel,
         in_specs=[VMEM] * 5,
-        out_specs=[VMEM] * 3,
+        out_specs=[VMEM] * 2,
         out_shape=[
             pltpu.VMEM((G, 2 * G), BF16),
-            pltpu.HBM((4 * BLOCK, 2 * NQ), BF16),
             pltpu.HBM((NQ, 2 * NQ), F32),
         ],
         compiler_params=LIMIT,
@@ -274,19 +282,22 @@
     rows = near[0].shape[0]
     return pl.pallas_call(
         main_kernel,
-        in_specs=[VMEM] * 5 + [FAR] * 4,
+        in_specs=[VMEM] * 6 + [FAR] * 2,
         out_specs=VMEM,
-        out_shape=jax.ShapeDtypeStruct((BAND, 2 * BLOCK), BF16),
+        out_shape=jax.ShapeDtypeStruct((8 * PEERS, 128), BF16),
         scratch_shapes=[
             pltpu.VMEM((rows, 128), F32),
             pltpu.VMEM((G // 2, 2 * G), BF16),
             pltpu.VMEM((G, 2 * NQ), BF16),
             pltpu.VMEM((NQ, 2 * NQ), BF16),
-            pltpu.VMEM((2 * NQ, 4 * BLOCK), BF16),
-            pltpu.VMEM((G, 4 * BLOCK), BF16),
+            pltpu.VMEM((NQ, 2 * NQ), BF16),
+            pltpu.VMEM((2 * NQ, 2 * HALF), BF16),
+            pltpu.VMEM((G, 2 * HALF), BF16),
+            pltpu.VMEM((2 * PEERS, 128), F32),
+            pltpu.VMEM((8 * PEERS, 128), F32),
         ]
         + [pltpu.VMEM(a.shape, a.dtype) for a in far]
-        + [pltpu.SemaphoreType.DMA((4,))],
+        + [pltpu.SemaphoreType.DMA((2,))],
         compiler_params=LIMIT,
         name="propagate",
     )(*near, *far)
@@ -312,7 +323,7 @@
         in_specs=[VMEM] * 3,
         out_specs=VMEM,
         out_shape=jax.ShapeDtypeStruct((2, 16, 2 * BAND), F32),
-        scratch_shapes=[pltpu.VMEM((128, 128), F32)],
+        scratch_shapes=[pltpu.VMEM((8 * PEERS, 128), F32), pltpu.VMEM((32, 1024), BF16)],
         compiler_params=LIMIT,
         name="finish",
     )(parts, final, prop)
@@ -343,28 +354,20 @@
 
 def message_kernel(cells, out, rows, block):
     wide = cells[...].astype(F32)
-    near = jnp.where(own_core() == 0, wide[0:1, : 2 * G], wide[0:1, 2 * G :])
+    own = jnp.where(own_core() == 0, wide[:, : 2 * G], wide[:, 2 * G :])
     for k in range(8):
-        rows[k : k + 1, :] = near[:, 128 * k : 128 * k + 128]
-    near = rows[...]
-    for m in range(8):
-        block[ROWS * m : ROWS * m + 8, :] = near
-    low = lax.broadcasted_iota(jnp.int32, (1, 128), 1) < BLOCK
-    for r in range(8):
-        for h in range(2):
-            at = 128 * (8 * h + r // 2)
-            one = wide[1:2, at : at + 128]
-            two = wide[1:2, at + G : at + G + 128]
-            if r % 2 == 0:
-                own = jnp.where(low, one, pltpu.roll(two, BLOCK, 1))
-            else:
-                own = jnp.where(low, pltpu.roll(one, BLOCK, 1), two)
-            for m in range(8):
-                block[ROWS * m + 8 + h : ROWS * m + 9 + h, :] = own
+        rows[k : k + 1, :] = own[0:1, 128 * k : 128 * k + 128]
+    size = 8 * ROWS
+    for h in range(2):
+        for k in range(4):
+            at = G * (k // 2) + HALF * h + 128 * (k % 2)
+            rows[8 + k : 9 + k, :] = own[1:2, at : at + 128]
+        for m in range(8):
+            block[ROWS * m : ROWS * m + ROWS, :] = rows[...]
         copies = block[...].astype(BF16)
-        size = 8 * ROWS
-        out[2 * r * size : (2 * r + 1) * size, :] = copies
-        out[(2 * r + 1) * size : (2 * r + 2) * size, :] = copies
+        for t in range(h, 8, 2):
+            out[2 * t * size : (2 * t + 1) * size, :] = copies
+            out[(2 * t + 1) * size : (2 * t + 2) * size, :] = copies
 
 
 def message(potential):
@@ -373,7 +376,7 @@
         in_specs=[VMEM],
         out_specs=VMEM,
         out_shape=jax.ShapeDtypeStruct((128 * ROWS, 128), BF16),
-        scratch_shapes=[pltpu.VMEM((8, 128), F32), pltpu.VMEM((8 * ROWS, 128), F32)],
+        scratch_shapes=[pltpu.VMEM((ROWS, 128), F32), pltpu.VMEM((8 * ROWS, 128), F32)],
         compiler_params=LIMIT,
         name="message",
     )(potential)
@@ -391,28 +394,28 @@
     right, left, back, chirp = (jnp.asarray(t) for t in constant_tables())
     peers = lax.axis_size("beam")
     position = lax.axis_index("beam")
-    probes = peers // 8
     group = lax.axis_index("grp")
     mine = message(potential).reshape(peers, ROWS // 2, 2, 128)
     cells = lax.all_to_all(
         mine, ("beam", "grp"), 0, 0, tiled=True, axis_index_groups=near_groups(peers)
     )
-    site = lax.dynamic_index_in_dim(
-        probe_sites, group * probes + position % probes, 0, keepdims=False
-    )
+    site = lax.dynamic_index_in_dim(probe_sites, group * 16 + position % 16, 0, keepdims=False)
     beams = own_coefficients(wave_vectors, site)
     made = prepare(beams, right, back, chirp)
-    cells, phi, inverse, prop = lax.optimization_barrier((cells, *made))
+    cells, phi, prop = lax.optimization_barrier((cells, *made))
     cells = cells.reshape(peers * ROWS, 128)
     other = lax.ppermute(cells, "grp", [(0, 1), (1, 0), (2, 3), (3, 2)])
-    cells, right_near, phi = (placed(a, pltpu.VMEM) for a in (cells, right, phi))
+    cells, right_near, phi, left = (placed(a, pltpu.VMEM) for a in (cells, right, phi, left))
     first = placed(early(cells, phi, right_near), pltpu.VMEM)
-    near = (placed(other, pltpu.VMEM), cells, first, right_near, phi)
-    far = [placed(a, pltpu.HBM) for a in (left, inverse, prop, back)]
+    near = (placed(other, pltpu.VMEM), cells, first, right_near, phi, left)
+    far = [placed(a, pltpu.HBM) for a in (prop, back)]
     sent = main(near, far)
-    parts = lax.all_to_all(sent.reshape(peers, 2, 128), "beam", 0, 0, tiled=True)
+    runs = [list(range(k, k + PEERS)) for k in range(0, peers, PEERS)]
+    parts = lax.all_to_all(
+        sent.reshape(PEERS, 8, 128), "beam", 0, 0, tiled=True, axis_index_groups=runs
+    )
     final = finish_table(right, sent)
-    return finish(parts.reshape(2 * peers, 128), final, band_rows(2 * position))
+    return finish(parts.reshape(8 * PEERS, 128), final, band_rows(2 * position))
 
 
 def solution(mesh):

time: 68.2 us -> 64.9 us (0.952)
  starting transfers between devices: 31.9 us -> 29.9 us
  other arithmetic: 3.11 us -> 1.51 us
  waiting for transfers between devices: 18.8 us -> 20 us
  local copies, waits for them, and re-layouts: 3.31 us -> 2.56 us
    all_to_all x1, waiting for transfers between devices: 6.71 us -> 10.2 us  [local(): lax.all_to_all(mine, ('beam', 'grp'), 0, 0, tiled=True, axis_index_groups...]
    all_to_all x1, waiting for transfers between devices: 12.1 us -> 9.69 us  [local(): lax.all_to_all(sent.reshape(PEERS, 8, 128), 'beam', 0, 0, tiled=True, axi...]
    all_to_all x1, starting transfers between devices: 6.16 us -> 3.9 us  [local(): lax.all_to_all(sent.reshape(PEERS, 8, 128), 'beam', 0, 0, tiled=True, axi...]
    mul x1, other arithmetic: 2.12 us -> 1.28 us  [own_coefficients(): coef_i = (weight * jnp.sin(angle)).astype(BF16).astype(F32) * G]
    convert_element_type x1, other arithmetic: 0.77 us -> 0.01 us  [own_coefficients(): (wave_y + offset).astype(F32)]
    unnamed x12 -> x16, local copies, waits for them, and re-layouts: 2.62 us -> 1.93 us
  transfers between devices with their start and end apart: 3 -> 3, of which waited for: 2 -> 3; matrix products, arithmetic and copies ran while one was open for 6% -> 3% of each run, Pallas kernels for 5% -> 6%
where the time goes in v4:
time: 64.9 us; the launch traced here: 64.6 us
  starting transfers between devices  29.9 us (46%)
  waiting for transfers between devices  20 us (31%)
  Pallas kernels  10.5 us (16%)
  local copies, waits for them, and re-layouts  2.56 us (4%)
  other arithmetic  1.51 us (2%)
    all_to_all x1, starting transfers between devices, local(): lax.all_to_all(mine, ('beam', 'grp'), 0, 0, tiled=True, axis_index_groups...  20.5 us
    all_to_all x1, waiting for transfers between devices, local(): lax.all_to_all(mine, ('beam', 'grp'), 0, 0, tiled=True, axis_index_groups...  10.2 us
    all_to_all x1, waiting for transfers between devices, local(): lax.all_to_all(sent.reshape(PEERS, 8, 128), 'beam', 0, 0, tiled=True, axi...  9.69 us
    ppermute x1, starting transfers between devices, local(): other = lax.ppermute(cells, 'grp', [(0, 1), (1, 0), (2, 3), (3, 2)])  5.46 us
    pallas_call x1, Pallas kernels, main(): pl.pallas_call(main_kernel, in_specs=[VMEM] * 6 + [FAR] * 2, out_specs=VM...  5.19 us
    all_to_all x1, starting transfers between devices, local(): lax.all_to_all(sent.reshape(PEERS, 8, 128), 'beam', 0, 0, tiled=True, axi...  3.9 us
    pallas_call x1, Pallas kernels, prepare(): pl.pallas_call(prepare_kernel, in_specs=[VMEM] * 5, out_specs=[VMEM] * 2,...  2.32 us
    unnamed x16, local copies, waits for them, and re-layouts  1.93 us
  transfers between devices with their start and end apart: 3, of which 3 were waited for; matrix products, arithmetic and copies ran while one was open for 3% of the time, Pallas kernels for 6%

profile of v4, /device:TPU:1, one launch (start us, length us, event | category | flops | bytes accessed | tf_op | source)
XLA Modules:
  0.0 64.6 jit_solution(16126254311442382808)
XLA Ops:
  0.0 0.0 copy-start
  0.0 0.0 copy-start.1
  0.0 0.0 copy-start.5
  0.0 0.0 copy-start.4
  0.0 0.0 copy-start.6
  0.0 0.8 %copy-done.6 = bf16[2,2048]{1,0:T(2,128)(2,1)S(1)} copy-done((bf16[2,2048]{1,0:T(2,128)(2,1)S(1)}, bf16[2,2048]{1,0:T(2,128)(2,1)}, u32[]{:S(2)}) %copy-start.6) | copy-done | bytes 8216
  0.8 0.8 %message.1 = bf16[1536,128]{1,0:T(8,128)(2,1)} custom-call(bf16[2,2048]{1,0:T(2,128)(2,1)S(1)} %copy-done.6), custom_call_target="tpu_custom_call" | custom-call | tf_op jit(solution)/shard_map/message/pallas_call | solution.py:374
  1.6 20.5 %all-to-all-start = ((bf16[128,6,2,128]{3,2,1,0:T(2,128)(2,1)}), bf16[128,6,2,128]{3,2,1,0:T(2,128)(2,1)S(1)}, u32[]{:S(2)}, u32[]{:S(2)}) async-start(bf16[128,6,2,128]{3,2,1,0:T(2,128)(2,1)} %bitcast), calls=%async_computation | async-start | bytes 786432 | tf_op jit(solution)/shard_map/all_to_all | solution.py:399
  22.2 0.0 copy-done
  22.2 0.1 constant_dynamic-slice_fusion
  22.3 0.5 fusion.14
  22.8 0.0 copy-done.7
  22.8 1.3 %fusion.12 = (f32[1,512]{1,0:T(1,128)S(1)}, f32[1,512]{1,0:T(1,128)S(1)}, f32[512,1]{0,1:T(1,128)S(1)}) fusion(s32[512,2]{0,1:T(2,128)S(1)} %copy-done.7, s32[]{:T(128)} %bitcast.5, s32[]{:T(128)} %bitcast.4), kind=kLoop, calls=%fused_computation.23 | loop fusion | flops 13824 | bytes 10248 | tf_op jit(solution)/shard_map/mul | solution.py:340
  24.1 0.1 fusion.9
  24.2 0.0 copy-done.1
  24.2 0.0 copy-done.5
  24.2 0.0 copy-done.4
  24.2 0.0 copy-start.2
  24.2 1.1 %copy-done.2 = bf16[512,768]{1,0:T(8,128)(2,1)S(1)} copy-done((bf16[512,768]{1,0:T(8,128)(2,1)S(1)}, bf16[512,768]{1,0:T(8,128)(2,1)}, u32[]{:S(2)}) %copy-start.2) | copy-done | bytes 786456
  25.4 2.3 %prepare.1 = (bf16[512,1024]{1,0:T(8,128)(2,1)S(1)}, f32[384,768]{1,0:T(8,128)}) custom-call(f32[8,512]{1,0:T(8,128)S(1)} %concatenate.6.beams, bf16[512,768]{1,0:T(8,128)(2,1)S(1)} %copy-done.1, bf16[512,768]{1,0:T(8,128)(2,1)S(1)} %copy-done.2, f32[8,384]{1,0:T(8,128)S(1)} %copy-done.5, f32[384,8]{1,0:T(8,128)S(1)} %copy-done.4), custom_call_target="tpu_custom_call" | custom-call | tf_op jit(solution)/shard_map/prepare/pallas_call | solution.py:253
  27.7 10.2 %all-to-all-done = bf16[128,6,2,128]{3,2,1,0:T(2,128)(2,1)S(1)} async-done(((bf16[128,6,2,128]{3,2,1,0:T(2,128)(2,1)}), bf16[128,6,2,128]{3,2,1,0:T(2,128)(2,1)S(1)}, u32[]{:S(2)}, u32[]{:S(2)}) %all-to-all-start) | async-done | bytes 393248 | tf_op jit(solution)/shard_map/all_to_all | solution.py:399
  37.8 5.5 %collective-permute-start = (bf16[1536,128]{1,0:T(8,128)(2,1)S(1)}, bf16[1536,128]{1,0:T(8,128)(2,1)S(1)}, u32[]{:S(2)}, u32[]{:S(2)}) collective-permute-start(bf16[1536,128]{1,0:T(8,128)(2,1)S(1)} %bitcast.28), channel_id=1, source_target_pairs={{0,1},{1,0},{2,3},{3,2},{4,5},{5,4},{6,7},{7,6},{8,9},{9,8},{10,11... | collective-permute-start | bytes 1179656 | tf_op jit(solution)/shard_map/ppermute | solution.py:407
  43.3 0.0 copy-start.3
  43.3 1.2 %early.1 = bf16[256,768]{1,0:T(8,128)(2,1)S(1)} custom-call(bf16[1536,128]{1,0:T(8,128)(2,1)S(1)} %bitcast.29, bf16[512,1024]{1,0:T(8,128)(2,1)S(1)} %get-tuple-element.13.phi, bf16[512,768]{1,0:T(8,128)(2,1)S(1)} %copy-done.1), custom_call_target="tpu_custom_call" | custom-call | tf_op jit(solution)/shard_map/early/pallas_call | solution.py:267
  44.5 0.1 collective-permute-done.other
  44.6 0.0 copy-done.3
  44.6 5.2 %propagate.1.sent = bf16[256,128]{1,0:T(8,128)(2,1)} custom-call(bf16[1536,128]{1,0:T(8,128)(2,1)S(1)} %collective-permute-done.other, bf16[1536,128]{1,0:T(8,128)(2,1)S(1)} %bitcast.30, bf16[256,768]{1,0:T(8,128)(2,1)S(1)} %early.1, bf16[512,768]{1,0:T(8,128)(2,1)S(1)} %copy-done.1, bf16[512,1024]{1,0:T(8,128)(2,1)S(1)} %get-tuple-element.13.phi, ...), custom_call_target="tpu_custom_call" | custom-call | tf_op jit(solution)/shard_map/propagate/pallas_call | solution.py:283
  49.8 3.9 %all-to-all-start.1 = ((bf16[32,8,128]{2,1,0:T(8,128)(2,1)}), bf16[32,8,128]{2,1,0:T(8,128)(2,1)S(1)}, u32[]{:S(2)}, u32[]{:S(2)}) async-start(bf16[32,8,128]{2,1,0:T(8,128)(2,1)} %bitcast.8), calls=%async_computation.1 | async-start | bytes 131072 | tf_op jit(solution)/shard_map/all_to_all | solution.py:414
  53.7 0.1 cosine_select_fusion
  53.9 0.1 finish_table.1.final
  54.0 9.7 %all-to-all-done.1 = bf16[32,8,128]{2,1,0:T(8,128)(2,1)S(1)} async-done(((bf16[32,8,128]{2,1,0:T(8,128)(2,1)}), bf16[32,8,128]{2,1,0:T(8,128)(2,1)S(1)}, u32[]{:S(2)}, u32[]{:S(2)}) %all-to-all-start.1) | async-done | bytes 65568 | tf_op jit(solution)/shard_map/all_to_all | solution.py:414
  63.7 0.9 %finish.1 = f32[2,16,512]{2,1,0:T(8,128)} custom-call(bf16[256,128]{1,0:T(8,128)(2,1)S(1)} %bitcast.31, bf16[1024,512]{1,0:T(8,128)(2,1)S(1)} %finish_table.1.final, f32[2,512]{1,0:T(2,128)S(1)} %pad_maximum_fusion.prop), custom_call_target="tpu_custom_call" | custom-call | tf_op jit(solution)/shard_map/finish/pallas_call | solution.py:321
  (7 shorter events, 0.1 us)
Async XLA Ops:
  0.0 22.2 %copy-start = (s32[64,2]{0,1:T(2,128)S(1)}, s32[64,2]{0,1:T(2,128)}, u32[]{:S(2)}) copy-start(s32[64,2]{0,1:T(2,128)} %param.9) | copy-start | bytes 1540
  0.0 24.2 %copy-start.1 = (bf16[512,768]{1,0:T(8,128)(2,1)S(1)}, bf16[512,768]{1,0:T(8,128)(2,1)}, u32[]{:S(2)}) copy-start(bf16[512,768]{1,0:T(8,128)(2,1)} %constant.91.clone.right) | copy-start | bytes 2359300
  0.0 24.2 %copy-start.5 = (f32[8,384]{1,0:T(8,128)S(1)}, f32[8,384]{1,0:T(8,128)}, u32[]{:S(2)}) copy-start(f32[8,384]{1,0:T(8,128)} %constant.94.clone.chirp) | copy-start | bytes 36868
  0.0 24.2 %copy-start.4 = (f32[384,8]{1,0:T(8,128)S(1)}, f32[384,8]{1,0:T(8,128)}, u32[]{:S(2)}) copy-start(f32[384,8]{1,0:T(8,128)} %constant.95.chirp_t) | copy-start | bytes 36868
  0.0 0.8 %copy-start.6 = (bf16[2,2048]{1,0:T(2,128)(2,1)S(1)}, bf16[2,2048]{1,0:T(2,128)(2,1)}, u32[]{:S(2)}) copy-start(bf16[2,2048]{1,0:T(2,128)(2,1)} %cells.1) | copy-start | bytes 24580
  0.8 22.0 %copy-start.7 = (s32[512,2]{0,1:T(2,128)S(1)}, s32[512,2]{0,1:T(2,128)}, u32[]{:S(2)}) copy-start(s32[512,2]{0,1:T(2,128)} %param.8) | copy-start | bytes 12292
  1.6 36.2 %all-to-all-start = ((bf16[128,6,2,128]{3,2,1,0:T(2,128)(2,1)}), bf16[128,6,2,128]{3,2,1,0:T(2,128)(2,1)S(1)}, u32[]{:S(2)}, u32[]{:S(2)}) async-start(bf16[128,6,2,128]{3,2,1,0:T(2,128)(2,1)} %bitcast), calls=%async_computation | async-start | bytes 786432 | tf_op jit(solution)/shard_map/all_to_all | solution.py:399
  24.2 1.1 %copy-start.2 = (bf16[512,768]{1,0:T(8,128)(2,1)S(1)}, bf16[512,768]{1,0:T(8,128)(2,1)}, u32[]{:S(2)}) copy-start(bf16[512,768]{1,0:T(8,128)(2,1)} %constant.93.clone.back.back_far) | copy-start | bytes 2359300
  37.8 6.8 %collective-permute-start = (bf16[1536,128]{1,0:T(8,128)(2,1)S(1)}, bf16[1536,128]{1,0:T(8,128)(2,1)S(1)}, u32[]{:S(2)}, u32[]{:S(2)}) collective-permute-start(bf16[1536,128]{1,0:T(8,128)(2,1)S(1)} %bitcast.28), channel_id=1, source_target_pairs={{0,1},{1,0},{2,3},{3,2},{4,5},{5,4},{6,7},{7,6},{8,9},{9,8},{10,11... | collective-permute-start | bytes 1179656 | tf_op jit(solution)/shard_map/ppermute | solution.py:407
  43.3 1.3 %copy-start.3 = (bf16[768,512]{1,0:T(8,128)(2,1)S(1)}, bf16[768,512]{1,0:T(8,128)(2,1)}, u32[]{:S(2)}) copy-start(bf16[768,512]{1,0:T(8,128)(2,1)} %constant.92.clone.left) | copy-start | bytes 2359300
  49.8 13.8 %all-to-all-start.1 = ((bf16[32,8,128]{2,1,0:T(8,128)(2,1)}), bf16[32,8,128]{2,1,0:T(8,128)(2,1)S(1)}, u32[]{:S(2)}, u32[]{:S(2)}) async-start(bf16[32,8,128]{2,1,0:T(8,128)(2,1)} %bitcast.8), calls=%async_computation.1 | async-start | bytes 131072 | tf_op jit(solution)/shard_map/all_to_all | solution.py:414

commit v5 on v4

--- a/solution.py
+++ b/solution.py
@@ -45,7 +45,8 @@
     natural = forward_table(places)
     shuffled = forward_table(permuted)
     right = np.concatenate([natural[0], natural[1]], 1)
-    left = np.concatenate([shuffled[0].T, shuffled[1].T], 0)
+    left = np.stack([shuffled[0].T, shuffled[1].T], 0).reshape(2, 3, 128, G)
+    left = left.swapaxes(0, 1).reshape(2 * NQ, G)
     back = np.concatenate([shuffled[0], -shuffled[1]], 1)
     freqs = frequencies()
     squared = np.full((NQ,), 1.0e9)
@@ -66,11 +67,13 @@
 def half_turn_fits():
     nodes = 0.5 * np.cos(np.pi * (np.arange(400) + 0.5) / 400)
     square = nodes * nodes
-    sine = np.polynomial.Polynomial.fit(square, np.sin(np.pi * nodes) / nodes, 4, domain=[0, 0.25])
-    cosine = np.polynomial.Polynomial.fit(square, np.cos(np.pi * nodes), 4, domain=[0, 0.25])
+    root = math.sqrt(2.0)
+    sine = root * np.sin(np.pi * nodes) / nodes
+    cosine = root * np.cos(np.pi * nodes)
+    fit = np.polynomial.Polynomial.fit
     return (
-        [float(v) for v in sine.convert().coef],
-        [float(v) for v in cosine.convert().coef],
+        [float(v) for v in fit(square, sine, 4, domain=[0, 0.25]).convert().coef],
+        [float(v) for v in fit(square, cosine, 4, domain=[0, 0.25]).convert().coef],
     )
 
 
@@ -86,11 +89,11 @@
 
 def phase_factor(cells):
     turns = cells * (PHASE_SCALE / (2.0 * math.pi))
-    rest = turns - jnp.floor(turns + 0.5)
+    rest = turns - jnp.round(turns)
     square = rest * rest
     sine = rest * horner(SINE, square)
     cosine = horner(COSINE, square)
-    return 1.0 - 2.0 * sine * sine, 2.0 * sine * cosine
+    return 1.0 - sine * sine, sine * cosine
 
 
 def own_core():
@@ -143,34 +146,42 @@
 
 def forward_rows(wide, phi, right, data, half, first, offset):
     for j in range(2):
-        rows = slice(128 * j, 128 * j + 128)
+        rows = slice(256 * j, 256 * j + 128)
+        low = slice(256 * j + 128, 256 * j + 256)
         probe = pl.ds(pl.multiple_of(first + 128 * j, 128), 128)
         for h in range(4):
             cos, sin = phase_factor(wide[pl.ds(4 * j + h, 128, stride=ROWS), :])
             pr = phi[probe, 128 * h : 128 * h + 128].astype(F32)
             pi = phi[probe, G + 128 * h : G + 128 * h + 128].astype(F32)
             data[rows, 128 * h : 128 * h + 128] = (pr * cos - pi * sin).astype(BF16)
-            data[rows, G + 128 * h : G + 128 * h + 128] = (pr * sin + pi * cos).astype(BF16)
-        one = dot(data[rows, :G], right[...])
-        two = dot(data[rows, G:], right[...])
+            data[low, 128 * h : 128 * h + 128] = (pr * sin + pi * cos).astype(BF16)
+        both = dot(data[256 * j : 256 * j + 256, :], right[...])
         kept = pl.ds(pl.multiple_of(offset + 128 * j, 128), 128)
-        half[kept, :NQ] = (one[:, :NQ] - two[:, NQ:]).astype(BF16)
-        half[kept, NQ:] = (one[:, NQ:] + two[:, :NQ]).astype(BF16)
-
-
-def early_kernel(cells, phi, right, half, wide, data):
+        half[kept, :NQ] = (both[:128, :NQ] - both[128:, NQ:]).astype(BF16)
+        half[kept, NQ:] = (both[:128, NQ:] + both[128:, :NQ]).astype(BF16)
+
+
+def second_factors(wide, factors, j):
+    rows = slice(128 * j, 128 * j + 128)
+    for q in range(2):
+        cos, sin = phase_factor(wide[pl.ds(8 + 2 * j + q, 128, stride=ROWS), :])
+        factors[rows, 128 * q : 128 * q + 128] = cos
+        factors[rows, HALF + 128 * q : HALF + 128 * q + 128] = sin
+
+
+def early_kernel(cells, phi, right, half, factors, wide, data):
     wide[...] = cells[...].astype(F32)
     forward_rows(wide, phi, right, data, half, own_core() * 256, 0)
+    for j in range(2):
+        second_factors(wide, factors, j)
 
 
 def main_kernel(
-    other, cells, early, right, phi, left, prop_far, back_far, out,
-    wide, data, half, spec, turn, fold, last, rows_in, rows_out, prop, back, sems,
+    other, early, own_factors, right, phi, prop, back, left_far, out,
+    wide, data, half, spec, fold, last, factors, rows_in, rows_out, left, sem,
 ):
-    far = ((prop_far, prop), (back_far, back))
-    copies = [pltpu.make_async_copy(a, b, sems.at[k]) for k, (a, b) in enumerate(far)]
-    for copy in copies:
-        copy.start()
+    copy = pltpu.make_async_copy(left_far, left, sem)
+    copy.start()
     place = lax.axis_index("beam")
     core = own_core()
     wide[...] = other[...].astype(F32)
@@ -178,45 +189,39 @@
     half[pl.ds(pl.multiple_of(start, 256), 256), :] = early[...]
     forward_rows(wide, phi, right, data, half, 256 - start, 256 - start)
     side = pl.ds(pl.multiple_of(place // 16 % 2 * HALF, HALF), HALF)
-    copies[0].wait()
+    copy.wait()
     for j in range(3):
         rows = slice(128 * j, 128 * j + 128)
         low = slice(NQ + 128 * j, NQ + 128 * j + 128)
-        one = dot(left[rows, :], half[...])
-        two = dot(left[low, :], half[...])
-        re = one[:, :NQ] - two[:, NQ:]
-        im = one[:, NQ:] + two[:, :NQ]
+        both = dot(left[256 * j : 256 * j + 256, :], half[...])
+        if j < 2:
+            second_factors(wide, factors, j)
+        re = both[:128, :NQ] - both[128:, NQ:]
+        im = both[:128, NQ:] + both[128:, :NQ]
         pr = prop[rows, :NQ]
         pi = prop[rows, NQ:]
         new_r = re * pr - im * pi
         new_i = re * pi + im * pr
-        spec[rows, :NQ] = new_r.astype(BF16)
-        spec[rows, NQ:] = new_i.astype(BF16)
-        turn[rows, :NQ] = new_i.astype(BF16)
-        turn[rows, NQ:] = (-new_r).astype(BF16)
-        at_r = dot_t(spec[rows, :], right[side, :])
-        at_i = dot_t(turn[rows, :], right[side, :])
-        fold[rows, :HALF] = at_r.astype(BF16)
-        fold[rows, HALF:] = at_i.astype(BF16)
-        fold[low, :HALF] = (-at_i).astype(BF16)
-        fold[low, HALF:] = at_r.astype(BF16)
-    copies[1].wait()
-    for source in range(2):
-        if source == 1:
-            wide[...] = cells[...].astype(F32)
-        first = 256 - start if source == 0 else start
-        for j in range(2):
-            rows = pl.ds(pl.multiple_of(first + 128 * j, 128), 128)
-            wave = dot(back[rows, :], fold[...])
-            for q in range(2):
-                cos, sin = phase_factor(wide[pl.ds(8 + 2 * j + q, 128, stride=ROWS), :])
-                re = wave[:, 128 * q : 128 * q + 128]
-                im = wave[:, HALF + 128 * q : HALF + 128 * q + 128]
-                last[rows, 128 * q : 128 * q + 128] = (re * cos - im * sin).astype(BF16)
-                last[rows, HALF + 128 * q : HALF + 128 * q + 128] = (re * sin + im * cos).astype(BF16)
-    band = pl.multiple_of(place // PEERS * 2 * PEERS, 2 * PEERS)
+        spec[256 * j : 256 * j + 128, :NQ] = new_r.astype(BF16)
+        spec[256 * j : 256 * j + 128, NQ:] = new_i.astype(BF16)
+        spec[256 * j + 128 : 256 * j + 256, :NQ] = new_i.astype(BF16)
+        spec[256 * j + 128 : 256 * j + 256, NQ:] = (-new_r).astype(BF16)
+        both = dot_t(spec[256 * j : 256 * j + 256, :], right[side, :])
+        fold[rows, :HALF] = both[:128].astype(BF16)
+        fold[rows, HALF:] = both[128:].astype(BF16)
+        fold[low, :HALF] = (-both[128:]).astype(BF16)
+        fold[low, HALF:] = both[:128].astype(BF16)
+    for table, first in ((factors, 256 - start), (own_factors, start)):
+        rows = pl.ds(pl.multiple_of(first, 256), 256)
+        wave = dot(back[rows, :], fold[...])
+        cos = table[:, :HALF]
+        sin = table[:, HALF:]
+        last[rows, :HALF] = (wave[:, :HALF] * cos - wave[:, HALF:] * sin).astype(BF16)
+        last[rows, HALF:] = (wave[:, :HALF] * sin + wave[:, HALF:] * cos).astype(BF16)
+    part = place // PEERS
+    band = pl.multiple_of(part // 2 * 256 + part % 2 * 64, 2 * PEERS)
     one = dot(left[pl.ds(band, 2 * PEERS), :], last[...])
-    two = dot(left[pl.ds(NQ + band, 2 * PEERS), :], last[...])
+    two = dot(left[pl.ds(band + 128, 2 * PEERS), :], last[...])
     parts = (one[:, :HALF] - two[:, HALF:], one[:, HALF:] + two[:, :HALF])
     for q in range(4):
         rows_in[...] = parts[q // 2][:, 128 * (q % 2) : 128 * (q % 2) + 128]
@@ -267,40 +272,40 @@
     return pl.pallas_call(
         early_kernel,
         in_specs=[VMEM] * 3,
-        out_specs=VMEM,
-        out_shape=pltpu.VMEM((G // 2, 2 * NQ), BF16),
+        out_specs=[VMEM] * 2,
+        out_shape=[pltpu.VMEM((G // 2, 2 * NQ), BF16), pltpu.VMEM((G // 2, 2 * HALF), F32)],
         scratch_shapes=[
             pltpu.VMEM((cells.shape[0], 128), F32),
-            pltpu.VMEM((G // 2, 2 * G), BF16),
+            pltpu.VMEM((G, G), BF16),
         ],
         compiler_params=LIMIT,
         name="early",
     )(cells, phi, right)
 
 
-def main(near, far):
+def main(near, left):
     rows = near[0].shape[0]
     return pl.pallas_call(
         main_kernel,
-        in_specs=[VMEM] * 6 + [FAR] * 2,
+        in_specs=[VMEM] * 7 + [FAR],
         out_specs=VMEM,
         out_shape=jax.ShapeDtypeStruct((8 * PEERS, 128), BF16),
         scratch_shapes=[
             pltpu.VMEM((rows, 128), F32),
-            pltpu.VMEM((G // 2, 2 * G), BF16),
+            pltpu.VMEM((G, G), BF16),
             pltpu.VMEM((G, 2 * NQ), BF16),
-            pltpu.VMEM((NQ, 2 * NQ), BF16),
-            pltpu.VMEM((NQ, 2 * NQ), BF16),
+            pltpu.VMEM((2 * NQ, 2 * NQ), BF16),
             pltpu.VMEM((2 * NQ, 2 * HALF), BF16),
             pltpu.VMEM((G, 2 * HALF), BF16),
+            pltpu.VMEM((G // 2, 2 * HALF), F32),
             pltpu.VMEM((2 * PEERS, 128), F32),
             pltpu.VMEM((8 * PEERS, 128), F32),
-        ]
-        + [pltpu.VMEM(a.shape, a.dtype) for a in far]
-        + [pltpu.SemaphoreType.DMA((2,))],
+            pltpu.VMEM(left.shape, BF16),
+            pltpu.SemaphoreType.DMA,
+        ],
         compiler_params=LIMIT,
         name="propagate",
-    )(*near, *far)
+    )(*near, left)
 
 
 def finish_table(right, sent):
@@ -405,11 +410,11 @@
     cells, phi, prop = lax.optimization_barrier((cells, *made))
     cells = cells.reshape(peers * ROWS, 128)
     other = lax.ppermute(cells, "grp", [(0, 1), (1, 0), (2, 3), (3, 2)])
-    cells, right_near, phi, left = (placed(a, pltpu.VMEM) for a in (cells, right, phi, left))
-    first = placed(early(cells, phi, right_near), pltpu.VMEM)
-    near = (placed(other, pltpu.VMEM), cells, first, right_near, phi, left)
-    far = [placed(a, pltpu.HBM) for a in (prop, back)]
-    sent = main(near, far)
+    cells, right_near, phi = (placed(a, pltpu.VMEM) for a in (cells, right, phi))
+    first, factors = (placed(a, pltpu.VMEM) for a in early(cells, phi, right_near))
+    other, prop, back = (placed(a, pltpu.VMEM) for a in (other, prop, back))
+    near = (other, first, factors, right_near, phi, prop, back)
+    sent = main(near, placed(left, pltpu.HBM))
     runs = [list(range(k, k + PEERS)) for k in range(0, peers, PEERS)]
     parts = lax.all_to_all(
         sent.reshape(PEERS, 8, 128), "beam", 0, 0, tiled=True, axis_index_groups=runs

time: 64.9 us -> 64.4 us (level)
    unnamed x16 -> x18, local copies, waits for them, and re-layouts: 1.93 us -> 1.93 us
  transfers between devices with their start and end apart: 3 -> 3, of which waited for: 3 -> 2; matrix products, arithmetic and copies ran while one was open for 3% -> 4% of each run, Pallas kernels for 6% -> 6%
where the time goes in v5:
time: 64.4 us; the launch traced here: 64.1 us
  starting transfers between devices  29.9 us (46%)
  waiting for transfers between devices  19.6 us (30%)
  Pallas kernels  10 us (16%)
  local copies, waits for them, and re-layouts  2.64 us (4%)
  other arithmetic  1.65 us (3%)
    all_to_all x1, starting transfers between devices, local(): lax.all_to_all(mine, ('beam', 'grp'), 0, 0, tiled=True, axis_index_groups...  20.5 us
    all_to_all x1, waiting for transfers between devices, local(): lax.all_to_all(mine, ('beam', 'grp'), 0, 0, tiled=True, axis_index_groups...  9.92 us
    all_to_all x1, waiting for transfers between devices, local(): lax.all_to_all(sent.reshape(PEERS, 8, 128), 'beam', 0, 0, tiled=True, axi...  9.68 us
    ppermute x1, starting transfers between devices, local(): other = lax.ppermute(cells, 'grp', [(0, 1), (1, 0), (2, 3), (3, 2)])  5.46 us
    pallas_call x1, Pallas kernels, main(): pl.pallas_call(main_kernel, in_specs=[VMEM] * 7 + [FAR], out_specs=VMEM,...  4.6 us
    all_to_all x1, starting transfers between devices, local(): lax.all_to_all(sent.reshape(PEERS, 8, 128), 'beam', 0, 0, tiled=True, axi...  3.9 us
    pallas_call x1, Pallas kernels, prepare(): pl.pallas_call(prepare_kernel, in_specs=[VMEM] * 5, out_specs=[VMEM] * 2,...  2.32 us
    unnamed x18, local copies, waits for them, and re-layouts  1.93 us
  transfers between devices with their start and end apart: 3, of which 2 were waited for; matrix products, arithmetic and copies ran while one was open for 4% of the time, Pallas kernels for 6%

profile of v5, /device:TPU:1, one launch (start us, length us, event | category | flops | bytes accessed | tf_op | source)
XLA Modules:
  0.0 64.1 jit_solution(2819367540160869306)
XLA Ops:
  0.0 0.0 copy-start
  0.0 0.0 copy-start.1
  0.0 0.0 copy-start.5
  0.0 0.0 copy-start.7
  0.0 0.8 %copy-done.7 = bf16[2,2048]{1,0:T(2,128)(2,1)S(1)} copy-done((bf16[2,2048]{1,0:T(2,128)(2,1)S(1)}, bf16[2,2048]{1,0:T(2,128)(2,1)}, u32[]{:S(2)}) %copy-start.7) | copy-done | bytes 8216
  0.8 0.8 %message.1 = bf16[1536,128]{1,0:T(8,128)(2,1)} custom-call(bf16[2,2048]{1,0:T(2,128)(2,1)S(1)} %copy-done.7), custom_call_target="tpu_custom_call" | custom-call | tf_op jit(solution)/shard_map/message/pallas_call | solution.py:379
  1.6 20.5 %all-to-all-start = ((bf16[128,6,2,128]{3,2,1,0:T(2,128)(2,1)}), bf16[128,6,2,128]{3,2,1,0:T(2,128)(2,1)S(1)}, u32[]{:S(2)}, u32[]{:S(2)}) async-start(bf16[128,6,2,128]{3,2,1,0:T(2,128)(2,1)} %bitcast), calls=%async_computation | async-start | bytes 786432 | tf_op jit(solution)/shard_map/all_to_all | solution.py:404
  22.2 0.0 copy-done
  22.2 0.1 constant_dynamic-slice_fusion
  22.3 0.6 fusion.14
  22.9 0.0 copy-done.8
  22.9 1.4 %fusion.12 = (f32[1,512]{1,0:T(1,128)S(1)}, f32[1,512]{1,0:T(1,128)S(1)}, f32[512,1]{0,1:T(1,128)S(1)}) fusion(s32[512,2]{0,1:T(2,128)S(1)} %copy-done.8, s32[]{:T(128)} %bitcast.5, s32[]{:T(128)} %bitcast.4), kind=kLoop, calls=%fused_computation.23 | loop fusion | flops 13824 | bytes 10248 | tf_op jit(solution)/shard_map/mul | solution.py:345
  24.3 0.1 fusion.9
  24.4 0.0 copy-done.1
  24.4 0.0 copy-done.6
  24.4 0.0 copy-done.5
  24.5 0.0 copy-start.2
  24.5 1.1 %copy-done.2 = bf16[512,768]{1,0:T(8,128)(2,1)S(1)} copy-done((bf16[512,768]{1,0:T(8,128)(2,1)S(1)}, bf16[512,768]{1,0:T(8,128)(2,1)}, u32[]{:S(2)}) %copy-start.2) | copy-done | bytes 786456
  25.6 2.3 %prepare.1 = (bf16[512,1024]{1,0:T(8,128)(2,1)S(1)}, f32[384,768]{1,0:T(8,128)}) custom-call(f32[8,512]{1,0:T(8,128)S(1)} %concatenate.6.beams, bf16[512,768]{1,0:T(8,128)(2,1)S(1)} %copy-done.1, bf16[512,768]{1,0:T(8,128)(2,1)S(1)} %copy-done.2, f32[8,384]{1,0:T(8,128)S(1)} %copy-done.6, f32[384,8]{1,0:T(8,128)S(1)} %copy-done.5), custom_call_target="tpu_custom_call" | custom-call | tf_op jit(solution)/shard_map/prepare/pallas_call | solution.py:258
  27.9 9.9 %all-to-all-done = bf16[128,6,2,128]{3,2,1,0:T(2,128)(2,1)S(1)} async-done(((bf16[128,6,2,128]{3,2,1,0:T(2,128)(2,1)}), bf16[128,6,2,128]{3,2,1,0:T(2,128)(2,1)S(1)}, u32[]{:S(2)}, u32[]{:S(2)}) %all-to-all-start) | async-done | bytes 393248 | tf_op jit(solution)/shard_map/all_to_all | solution.py:404
  37.8 5.5 %collective-permute-start = (bf16[1536,128]{1,0:T(8,128)(2,1)S(1)}, bf16[1536,128]{1,0:T(8,128)(2,1)S(1)}, u32[]{:S(2)}, u32[]{:S(2)}) collective-permute-start(bf16[1536,128]{1,0:T(8,128)(2,1)S(1)} %bitcast.28), channel_id=1, source_target_pairs={{0,1},{1,0},{2,3},{3,2},{4,5},{5,4},{6,7},{7,6},{8,9},{9,8},{10,11... | collective-permute-start | bytes 1179656 | tf_op jit(solution)/shard_map/ppermute | solution.py:412
  43.3 0.0 copy-start.4
  43.3 1.3 %early.1 = (bf16[256,768]{1,0:T(8,128)(2,1)S(1)}, f32[256,512]{1,0:T(8,128)S(1)}) custom-call(bf16[1536,128]{1,0:T(8,128)(2,1)S(1)} %bitcast.29, bf16[512,1024]{1,0:T(8,128)(2,1)S(1)} %get-tuple-element.15.phi, bf16[512,768]{1,0:T(8,128)(2,1)S(1)} %copy-done.1), custom_call_target="tpu_custom_call" | custom-call | tf_op jit(solution)/shard_map/early/pallas_call | solution.py:272
  44.7 0.0 collective-permute-done.other
  44.7 0.0 copy-done.3
  44.7 0.0 copy-done.4
  44.7 4.6 %propagate.1.sent = bf16[256,128]{1,0:T(8,128)(2,1)} custom-call(bf16[1536,128]{1,0:T(8,128)(2,1)S(1)} %collective-permute-done.other, bf16[256,768]{1,0:T(8,128)(2,1)S(1)} %get-tuple-element.16.early, f32[256,512]{1,0:T(8,128)S(1)} %get-tuple-element.17.own_factors, bf16[512,768]{1,0:T(8,128)(2,1)S(1)} %copy-done.1, ...), custom_call_target="tpu_custom_call" | custom-call | tf_op jit(solution)/shard_map/propagate/pallas_call | solution.py:288
  49.3 3.9 %all-to-all-start.1 = ((bf16[32,8,128]{2,1,0:T(8,128)(2,1)}), bf16[32,8,128]{2,1,0:T(8,128)(2,1)S(1)}, u32[]{:S(2)}, u32[]{:S(2)}) async-start(bf16[32,8,128]{2,1,0:T(8,128)(2,1)} %bitcast.8), calls=%async_computation.1 | async-start | bytes 131072 | tf_op jit(solution)/shard_map/all_to_all | solution.py:419
  53.2 0.1 cosine_select_fusion
  53.4 0.1 finish_table.1.final
  53.4 9.7 %all-to-all-done.1 = bf16[32,8,128]{2,1,0:T(8,128)(2,1)S(1)} async-done(((bf16[32,8,128]{2,1,0:T(8,128)(2,1)}), bf16[32,8,128]{2,1,0:T(8,128)(2,1)S(1)}, u32[]{:S(2)}, u32[]{:S(2)}) %all-to-all-start.1) | async-done | bytes 65568 | tf_op jit(solution)/shard_map/all_to_all | solution.py:419
  63.1 0.9 %finish.1 = f32[2,16,512]{2,1,0:T(8,128)} custom-call(bf16[256,128]{1,0:T(8,128)(2,1)S(1)} %bitcast.30, bf16[1024,512]{1,0:T(8,128)(2,1)S(1)} %finish_table.1.final, f32[2,512]{1,0:T(2,128)S(1)} %pad_maximum_fusion.prop), custom_call_target="tpu_custom_call" | custom-call | tf_op jit(solution)/shard_map/finish/pallas_call | solution.py:326
  (9 shorter events, 0.1 us)
Async XLA Ops:
  0.0 22.2 %copy-start = (s32[64,2]{0,1:T(2,128)S(1)}, s32[64,2]{0,1:T(2,128)}, u32[]{:S(2)}) copy-start(s32[64,2]{0,1:T(2,128)} %param.9) | copy-start | bytes 1540
  0.0 24.4 %copy-start.1 = (bf16[512,768]{1,0:T(8,128)(2,1)S(1)}, bf16[512,768]{1,0:T(8,128)(2,1)}, u32[]{:S(2)}) copy-start(bf16[512,768]{1,0:T(8,128)(2,1)} %constant.91.clone.right) | copy-start | bytes 2359300
  0.0 24.4 %copy-start.6 = (f32[8,384]{1,0:T(8,128)S(1)}, f32[8,384]{1,0:T(8,128)}, u32[]{:S(2)}) copy-start(f32[8,384]{1,0:T(8,128)} %constant.94.clone.chirp) | copy-start | bytes 36868
  0.0 24.4 %copy-start.5 = (f32[384,8]{1,0:T(8,128)S(1)}, f32[384,8]{1,0:T(8,128)}, u32[]{:S(2)}) copy-start(f32[384,8]{1,0:T(8,128)} %constant.95.chirp_t) | copy-start | bytes 36868
  0.0 0.8 %copy-start.7 = (bf16[2,2048]{1,0:T(2,128)(2,1)S(1)}, bf16[2,2048]{1,0:T(2,128)(2,1)}, u32[]{:S(2)}) copy-start(bf16[2,2048]{1,0:T(2,128)(2,1)} %cells.1) | copy-start | bytes 24580
  0.8 22.0 %copy-start.8 = (s32[512,2]{0,1:T(2,128)S(1)}, s32[512,2]{0,1:T(2,128)}, u32[]{:S(2)}) copy-start(s32[512,2]{0,1:T(2,128)} %param.8) | copy-start | bytes 12292
  1.6 36.2 %all-to-all-start = ((bf16[128,6,2,128]{3,2,1,0:T(2,128)(2,1)}), bf16[128,6,2,128]{3,2,1,0:T(2,128)(2,1)S(1)}, u32[]{:S(2)}, u32[]{:S(2)}) async-start(bf16[128,6,2,128]{3,2,1,0:T(2,128)(2,1)} %bitcast), calls=%async_computation | async-start | bytes 786432 | tf_op jit(solution)/shard_map/all_to_all | solution.py:404
  24.5 1.1 %copy-start.2 = (bf16[512,768]{1,0:T(8,128)(2,1)S(1)}, bf16[512,768]{1,0:T(8,128)(2,1)}, u32[]{:S(2)}) copy-start(bf16[512,768]{1,0:T(8,128)(2,1)} %constant.93.clone.back) | copy-start | bytes 2359300
  27.9 16.8 %copy-start.3 = (bf16[512,768]{1,0:T(8,128)(2,1)S(1)}, bf16[512,768]{1,0:T(8,128)(2,1)}, u32[]{:S(2)}) copy-start(bf16[512,768]{1,0:T(8,128)(2,1)} %constant.93.clone.back) | copy-start | bytes 2359300
  37.8 6.8 %collective-permute-start = (bf16[1536,128]{1,0:T(8,128)(2,1)S(1)}, bf16[1536,128]{1,0:T(8,128)(2,1)S(1)}, u32[]{:S(2)}, u32[]{:S(2)}) collective-permute-start(bf16[1536,128]{1,0:T(8,128)(2,1)S(1)} %bitcast.28), channel_id=1, source_target_pairs={{0,1},{1,0},{2,3},{3,2},{4,5},{5,4},{6,7},{7,6},{8,9},{9,8},{10,11... | collective-permute-start | bytes 1179656 | tf_op jit(solution)/shard_map/ppermute | solution.py:412
  43.3 1.4 %copy-start.4 = (f32[384,768]{1,0:T(8,128)S(1)}, f32[384,768]{1,0:T(8,128)}, u32[]{:S(2)}) copy-start(f32[384,768]{1,0:T(8,128)} %get-tuple-element.18.prop) | copy-start | bytes 3538948
  49.3 13.8 %all-to-all-start.1 = ((bf16[32,8,128]{2,1,0:T(8,128)(2,1)}), bf16[32,8,128]{2,1,0:T(8,128)(2,1)S(1)}, u32[]{:S(2)}, u32[]{:S(2)}) async-start(bf16[32,8,128]{2,1,0:T(8,128)(2,1)} %bitcast.8), calls=%async_computation.1 | async-start | bytes 131072 | tf_op jit(solution)/shard_map/all_to_all | solution.py:419

commit v6 on v5

--- a/solution.py
+++ b/solution.py
@@ -108,7 +108,7 @@
     return lax.dot_general(a, b, (((1,), (1,)), ((), ())), preferred_element_type=F32)
 
 
-def prepare_kernel(beams, right, back, chirp, chirp_t, phi, prop):
+def prepare_kernel(beams, right, back, chirp, chirp_t, phi, prop, final):
     index = lax.broadcasted_iota(jnp.int32, (BAND, G), 0).astype(F32)
     on_x = index == beams[0:1, :]
     on_y = jnp.where(index == beams[1:2, :], 1.0, 0.0).astype(BF16)
@@ -131,9 +131,6 @@
     yi = chirp[1:2, :]
     prop[:, :NQ] = jnp.where(inside, xr * yr - xi * yi, 0.0)
     prop[:, NQ:] = jnp.where(inside, xr * yi + xi * yr, 0.0)
-
-
-def finish_table_kernel(right, sent, final):
     for h in range(2):
         rows = slice(h * HALF, h * HALF + HALF)
         top = slice(2 * h * HALF, (2 * h + 1) * HALF)
@@ -252,16 +249,18 @@
 VMEM = pl.BlockSpec(memory_space=pltpu.VMEM)
 LIMIT = pltpu.CompilerParams(vmem_limit_bytes=16 * 1024 * 1024)
 FAR = pl.BlockSpec(memory_space=pltpu.HBM)
+placed = pltpu.with_memory_space_constraint
 
 
 def prepare(beams, right, back, chirp):
     return pl.pallas_call(
         prepare_kernel,
         in_specs=[VMEM] * 5,
-        out_specs=[VMEM] * 2,
+        out_specs=[VMEM] * 3,
         out_shape=[
             pltpu.VMEM((G, 2 * G), BF16),
             pltpu.HBM((NQ, 2 * NQ), F32),
+            pltpu.VMEM((2 * G, 2 * BAND), BF16),
         ],
         compiler_params=LIMIT,
         name="prepare",
@@ -308,20 +307,6 @@
     )(*near, left)
 
 
-def finish_table(right, sent):
-    return pl.pallas_call(
-        finish_table_kernel,
-        in_specs=[VMEM, FAR],
-        out_specs=VMEM,
-        out_shape=jax.ShapeDtypeStruct((2 * G, 2 * BAND), BF16),
-        compiler_params=LIMIT,
-        name="finish_table",
-    )(right, sent)
-
-
-placed = pltpu.with_memory_space_constraint
-
-
 def finish(parts, final, prop):
     return pl.pallas_call(
         final_kernel,
@@ -407,7 +392,8 @@
     site = lax.dynamic_index_in_dim(probe_sites, group * 16 + position % 16, 0, keepdims=False)
     beams = own_coefficients(wave_vectors, site)
     made = prepare(beams, right, back, chirp)
-    cells, phi, prop = lax.optimization_barrier((cells, *made))
+    band = band_rows(2 * position)
+    cells, phi, prop, final, band = lax.optimization_barrier((cells, *made, band))
     cells = cells.reshape(peers * ROWS, 128)
     other = lax.ppermute(cells, "grp", [(0, 1), (1, 0), (2, 3), (3, 2)])
     cells, right_near, phi = (placed(a, pltpu.VMEM) for a in (cells, right, phi))
@@ -419,8 +405,7 @@
     parts = lax.all_to_all(
         sent.reshape(PEERS, 8, 128), "beam", 0, 0, tiled=True, axis_index_groups=runs
     )
-    final = finish_table(right, sent)
-    return finish(parts.reshape(8 * PEERS, 128), final, band_rows(2 * position))
+    return finish(parts.reshape(8 * PEERS, 128), placed(final, pltpu.VMEM), band)
 
 
 def solution(mesh):

time: 64.4 us -> 63.7 us (0.989)
  blocking collectives: 0 us -> 13.5 us
  waiting for transfers between devices: 19.6 us -> 8.75 us
  starting transfers between devices: 29.9 us -> 26.1 us
  local copies, waits for them, and re-layouts: 2.64 us -> 3.59 us
    all_to_all x0 -> x1, blocking collectives: none -> 13.5 us  [local(): lax.all_to_all(sent.reshape(PEERS, 8, 128), 'beam', 0, 0, tiled=True, axi...]
    all_to_all x1 -> x0, waiting for transfers between devices: 9.68 us -> none  [local(): lax.all_to_all(sent.reshape(PEERS, 8, 128), 'beam', 0, 0, tiled=True, axi...]
    all_to_all x1 -> x0, starting transfers between devices: 3.9 us -> none  [local(): lax.all_to_all(sent.reshape(PEERS, 8, 128), 'beam', 0, 0, tiled=True, axi...]
    all_to_all x1, waiting for transfers between devices: 9.92 us -> 8.75 us  [local(): lax.all_to_all(mine, ('beam', 'grp'), 0, 0, tiled=True, axis_index_groups...]
    unnamed x18 -> x22, local copies, waits for them, and re-layouts: 1.93 us -> 2.88 us
    pallas_call x2 -> x1, Pallas kernels: 2.39 us -> 2.4 us  [prepare(): pl.pallas_call(prepare_kernel, in_specs=[VMEM] * 5, out_specs=[VMEM] * 3,...]
  transfers between devices with their start and end apart: 3 -> 2, of which waited for: 2 -> 1; matrix products, arithmetic and copies ran while one was open for 4% -> 4% of each run, Pallas kernels for 6% -> 6%
where the time goes in v6:
time: 63.7 us; the launch traced here: 63.4 us
  starting transfers between devices  26.1 us (41%)
  blocking collectives  13.5 us (21%)
  Pallas kernels  9.52 us (15%)
  waiting for transfers between devices  8.75 us (14%)
  local copies, waits for them, and re-layouts  3.59 us (6%)
  other arithmetic  1.65 us (3%)
    all_to_all x1, starting transfers between devices, local(): lax.all_to_all(mine, ('beam', 'grp'), 0, 0, tiled=True, axis_index_groups...  20.5 us
    all_to_all x1, blocking collectives, local(): lax.all_to_all(sent.reshape(PEERS, 8, 128), 'beam', 0, 0, tiled=True, axi...  13.5 us
    all_to_all x1, waiting for transfers between devices, local(): lax.all_to_all(mine, ('beam', 'grp'), 0, 0, tiled=True, axis_index_groups...  8.75 us
    ppermute x1, starting transfers between devices, local(): other = lax.ppermute(cells, 'grp', [(0, 1), (1, 0), (2, 3), (3, 2)])  5.59 us
    pallas_call x1, Pallas kernels, main(): pl.pallas_call(main_kernel, in_specs=[VMEM] * 7 + [FAR], out_specs=VMEM,...  4.09 us
    unnamed x22, local copies, waits for them, and re-layouts  2.88 us
    pallas_call x1, Pallas kernels, prepare(): pl.pallas_call(prepare_kernel, in_specs=[VMEM] * 5, out_specs=[VMEM] * 3,...  2.4 us
    mul x1, other arithmetic, own_coefficients(): coef_i = (weight * jnp.sin(angle)).astype(BF16).astype(F32) * G  1.43 us
  transfers between devices with their start and end apart: 2, of which 1 were waited for; matrix products, arithmetic and copies ran while one was open for 4% of the time, Pallas kernels for 6%

profile of v6, /device:TPU:1, one launch (start us, length us, event | category | flops | bytes accessed | tf_op | source)
XLA Modules:
  0.0 63.4 jit_solution(7385737277899094657)
XLA Ops:
  0.0 0.0 copy-start
  0.0 0.0 copy-start.1
  0.0 0.0 copy-start.8
  0.0 0.0 copy-start.9
  0.0 0.8 %copy-done.9 = bf16[2,2048]{1,0:T(2,128)(2,1)S(1)} copy-done((bf16[2,2048]{1,0:T(2,128)(2,1)S(1)}, bf16[2,2048]{1,0:T(2,128)(2,1)}, u32[]{:S(2)}) %copy-start.9) | copy-done | bytes 8216
  0.8 0.8 %message.1 = bf16[1536,128]{1,0:T(8,128)(2,1)} custom-call(bf16[2,2048]{1,0:T(2,128)(2,1)S(1)} %copy-done.9), custom_call_target="tpu_custom_call" | custom-call | tf_op jit(solution)/shard_map/message/pallas_call | solution.py:364
  1.6 20.5 %all-to-all-start = ((bf16[128,6,2,128]{3,2,1,0:T(2,128)(2,1)}), bf16[128,6,2,128]{3,2,1,0:T(2,128)(2,1)S(1)}, u32[]{:S(2)}, u32[]{:S(2)}) async-start(bf16[128,6,2,128]{3,2,1,0:T(2,128)(2,1)} %bitcast), calls=%async_computation | async-start | bytes 786432 | tf_op jit(solution)/shard_map/all_to_all | solution.py:389
  22.2 0.0 copy-done
  22.2 0.1 constant_dynamic-slice_fusion
  22.3 0.6 fusion.14
  22.8 0.0 copy-done.10
  22.9 1.4 %fusion.12 = (f32[1,512]{1,0:T(1,128)S(1)}, f32[1,512]{1,0:T(1,128)S(1)}, f32[512,1]{0,1:T(1,128)S(1)}) fusion(s32[512,2]{0,1:T(2,128)S(1)} %copy-done.10, s32[]{:T(128)} %bitcast.5, s32[]{:T(128)} %bitcast.4), kind=kLoop, calls=%fused_computation.23 | loop fusion | flops 13824 | bytes 10248 | tf_op jit(solution)/shard_map/mul | solution.py:330
  24.3 0.1 fusion.9
  24.4 0.0 copy-done.1
  24.4 0.0 copy-done.7
  24.4 0.0 copy-done.8
  24.4 0.0 copy-start.2
  24.5 1.1 %copy-done.2 = bf16[512,768]{1,0:T(8,128)(2,1)S(1)} copy-done((bf16[512,768]{1,0:T(8,128)(2,1)S(1)}, bf16[512,768]{1,0:T(8,128)(2,1)}, u32[]{:S(2)}) %copy-start.2) | copy-done | bytes 786456
  25.6 2.4 %prepare.1 = (bf16[512,1024]{1,0:T(8,128)(2,1)S(1)}, f32[384,768]{1,0:T(8,128)}, bf16[1024,512]{1,0:T(8,128)(2,1)S(1)}) custom-call(f32[8,512]{1,0:T(8,128)S(1)} %concatenate.6.beams, bf16[512,768]{1,0:T(8,128)(2,1)S(1)} %copy-done.1, bf16[512,768]{1,0:T(8,128)(2,1)S(1)} %copy-done.2, f32[8,384]{1,0:T(8,128)S(1)} %copy-done.8, f32[384,8]{1,0:T(8,128)S(1)} %copy-done.7), custom_call_target="tpu_custom_call" | custom-call | tf_op jit(solution)/shard_map/prepare/pallas_call | solution.py:256
  28.0 0.9 %copy-done.5 = bf16[1024,512]{1,0:T(8,128)(2,1)} copy-done((bf16[1024,512]{1,0:T(8,128)(2,1)}, bf16[1024,512]{1,0:T(8,128)(2,1)S(1)}, u32[]{:S(2)}) %copy-start.5) | copy-done | bytes 1048600
  28.9 0.1 cosine_select_fusion
  29.1 8.7 %all-to-all-done = bf16[128,6,2,128]{3,2,1,0:T(2,128)(2,1)S(1)} async-done(((bf16[128,6,2,128]{3,2,1,0:T(2,128)(2,1)}), bf16[128,6,2,128]{3,2,1,0:T(2,128)(2,1)S(1)}, u32[]{:S(2)}, u32[]{:S(2)}) %all-to-all-start) | async-done | bytes 393248 | tf_op jit(solution)/shard_map/all_to_all | solution.py:389
  37.8 5.6 %collective-permute-start = (bf16[1536,128]{1,0:T(8,128)(2,1)S(1)}, bf16[1536,128]{1,0:T(8,128)(2,1)S(1)}, u32[]{:S(2)}, u32[]{:S(2)}) collective-permute-start(bf16[1536,128]{1,0:T(8,128)(2,1)S(1)} %bitcast.28), channel_id=1, source_target_pairs={{0,1},{1,0},{2,3},{3,2},{4,5},{5,4},{6,7},{7,6},{8,9},{9,8},{10,11... | collective-permute-start | bytes 1179656 | tf_op jit(solution)/shard_map/ppermute | solution.py:398
  43.4 1.3 %early.1 = (bf16[256,768]{1,0:T(8,128)(2,1)S(1)}, f32[256,512]{1,0:T(8,128)S(1)}) custom-call(bf16[1536,128]{1,0:T(8,128)(2,1)S(1)} %bitcast.29, bf16[512,1024]{1,0:T(8,128)(2,1)S(1)} %get-tuple-element.19.phi, bf16[512,768]{1,0:T(8,128)(2,1)S(1)} %copy-done.1), custom_call_target="tpu_custom_call" | custom-call | tf_op jit(solution)/shard_map/early/pallas_call | solution.py:271
  44.8 0.0 collective-permute-done.other
  44.8 0.0 copy-done.3
  44.8 0.0 copy-done.4
  44.8 0.0 copy-start.6
  44.8 4.1 %propagate.1 = bf16[256,128]{1,0:T(8,128)(2,1)S(1)} custom-call(bf16[1536,128]{1,0:T(8,128)(2,1)S(1)} %collective-permute-done.other, bf16[256,768]{1,0:T(8,128)(2,1)S(1)} %get-tuple-element.20.early, f32[256,512]{1,0:T(8,128)S(1)} %get-tuple-element.21.own_factors, bf16[512,768]{1,0:T(8,128)(2,1)S(1)} %copy-done.1, ...), custom_call_target="tpu_custom_call" | custom-call | tf_op jit(solution)/shard_map/propagate/pallas_call | solution.py:287
  48.9 13.5 %all_to_all.10 = bf16[32,8,128]{2,1,0:T(8,128)(2,1)S(1)} all-to-all(bf16[32,8,128]{2,1,0:T(8,128)(2,1)S(1)} %bitcast.30), channel_id=1, replica_groups={{0,4,8,12,16,20,24,28,32,36,40,44,48,52,56,60,64,68,72,76,80,84,88,92,9..., dimensions={0} | all-to-all | bytes 131072 | tf_op jit(solution)/shard_map/all_to_all | solution.py:405
  62.4 0.0 copy-done.6
  62.4 0.9 %finish.1 = f32[2,16,512]{2,1,0:T(8,128)} custom-call(bf16[256,128]{1,0:T(8,128)(2,1)S(1)} %bitcast.31, bf16[1024,512]{1,0:T(8,128)(2,1)S(1)} %copy-done.6, f32[2,512]{1,0:T(2,128)S(1)} %pad_maximum_fusion.prop), custom_call_target="tpu_custom_call" | custom-call | tf_op jit(solution)/shard_map/finish/pallas_call | solution.py:311
  (11 shorter events, 0.1 us)
Async XLA Ops:
  0.0 22.2 %copy-start = (s32[64,2]{0,1:T(2,128)S(1)}, s32[64,2]{0,1:T(2,128)}, u32[]{:S(2)}) copy-start(s32[64,2]{0,1:T(2,128)} %param.9) | copy-start | bytes 1540
  0.0 24.4 %copy-start.1 = (bf16[512,768]{1,0:T(8,128)(2,1)S(1)}, bf16[512,768]{1,0:T(8,128)(2,1)}, u32[]{:S(2)}) copy-start(bf16[512,768]{1,0:T(8,128)(2,1)} %constant.91.clone.right) | copy-start | bytes 2359300
  0.0 24.4 %copy-start.7 = (f32[384,8]{1,0:T(8,128)S(1)}, f32[384,8]{1,0:T(8,128)}, u32[]{:S(2)}) copy-start(f32[384,8]{1,0:T(8,128)} %constant.95.chirp_t) | copy-start | bytes 36868
  0.0 24.4 %copy-start.8 = (f32[8,384]{1,0:T(8,128)S(1)}, f32[8,384]{1,0:T(8,128)}, u32[]{:S(2)}) copy-start(f32[8,384]{1,0:T(8,128)} %constant.94.clone.chirp) | copy-start | bytes 36868
  0.0 0.8 %copy-start.9 = (bf16[2,2048]{1,0:T(2,128)(2,1)S(1)}, bf16[2,2048]{1,0:T(2,128)(2,1)}, u32[]{:S(2)}) copy-start(bf16[2,2048]{1,0:T(2,128)(2,1)} %cells.1) | copy-start | bytes 24580
  0.8 22.0 %copy-start.10 = (s32[512,2]{0,1:T(2,128)S(1)}, s32[512,2]{0,1:T(2,128)}, u32[]{:S(2)}) copy-start(s32[512,2]{0,1:T(2,128)} %param.8) | copy-start | bytes 12292
  1.6 36.2 %all-to-all-start = ((bf16[128,6,2,128]{3,2,1,0:T(2,128)(2,1)}), bf16[128,6,2,128]{3,2,1,0:T(2,128)(2,1)S(1)}, u32[]{:S(2)}, u32[]{:S(2)}) async-start(bf16[128,6,2,128]{3,2,1,0:T(2,128)(2,1)} %bitcast), calls=%async_computation | async-start | bytes 786432 | tf_op jit(solution)/shard_map/all_to_all | solution.py:389
  24.4 1.1 %copy-start.2 = (bf16[512,768]{1,0:T(8,128)(2,1)S(1)}, bf16[512,768]{1,0:T(8,128)(2,1)}, u32[]{:S(2)}) copy-start(bf16[512,768]{1,0:T(8,128)(2,1)} %constant.93.clone.back) | copy-start | bytes 2359300
  28.0 0.9 %copy-start.5 = (bf16[1024,512]{1,0:T(8,128)(2,1)}, bf16[1024,512]{1,0:T(8,128)(2,1)S(1)}, u32[]{:S(2)}) copy-start(bf16[1024,512]{1,0:T(8,128)(2,1)S(1)} %get-tuple-element.23.final) | copy-start | bytes 3145732
  28.9 15.8 %copy-start.3 = (bf16[512,768]{1,0:T(8,128)(2,1)S(1)}, bf16[512,768]{1,0:T(8,128)(2,1)}, u32[]{:S(2)}) copy-start(bf16[512,768]{1,0:T(8,128)(2,1)} %constant.93.clone.back) | copy-start | bytes 2359300
  37.8 6.9 %copy-start.4 = (f32[384,768]{1,0:T(8,128)S(1)}, f32[384,768]{1,0:T(8,128)}, u32[]{:S(2)}) copy-start(f32[384,768]{1,0:T(8,128)} %get-tuple-element.22.prop) | copy-start | bytes 3538948
  37.8 6.9 %collective-permute-start = (bf16[1536,128]{1,0:T(8,128)(2,1)S(1)}, bf16[1536,128]{1,0:T(8,128)(2,1)S(1)}, u32[]{:S(2)}, u32[]{:S(2)}) collective-permute-start(bf16[1536,128]{1,0:T(8,128)(2,1)S(1)} %bitcast.28), channel_id=1, source_target_pairs={{0,1},{1,0},{2,3},{3,2},{4,5},{5,4},{6,7},{7,6},{8,9},{9,8},{10,11... | collective-permute-start | bytes 1179656 | tf_op jit(solution)/shard_map/ppermute | solution.py:398
  44.8 17.7 %copy-start.6 = (bf16[1024,512]{1,0:T(8,128)(2,1)S(1)}, bf16[1024,512]{1,0:T(8,128)(2,1)}, u32[]{:S(2)}) copy-start(bf16[1024,512]{1,0:T(8,128)(2,1)} %copy-done.5) | copy-start | bytes 3145732

commit v7 on v6

--- a/solution.py
+++ b/solution.py
@@ -15,6 +15,7 @@
 CHIRP_RATE = 20
 PEERS = 32
 HALF = 256
+HIGH = 96
 ROWS = 12
 
 F32 = jnp.float32
@@ -45,8 +46,8 @@
     natural = forward_table(places)
     shuffled = forward_table(permuted)
     right = np.concatenate([natural[0], natural[1]], 1)
-    left = np.stack([shuffled[0].T, shuffled[1].T], 0).reshape(2, 3, 128, G)
-    left = left.swapaxes(0, 1).reshape(2 * NQ, G)
+    runs = [slice(0, 128), slice(128, 256), slice(256, 256 + HIGH)]
+    left = np.concatenate([shuffled[k][:, rows].T for rows in runs for k in range(2)], 0)
     back = np.concatenate([shuffled[0], -shuffled[1]], 1)
     freqs = frequencies()
     squared = np.full((NQ,), 1.0e9)
@@ -185,14 +186,13 @@
     start = core * 256
     half[pl.ds(pl.multiple_of(start, 256), 256), :] = early[...]
     forward_rows(wide, phi, right, data, half, 256 - start, 256 - start)
-    side = pl.ds(pl.multiple_of(place // 16 % 2 * HALF, HALF), HALF)
+    side = pl.ds(pl.multiple_of(place // 32 % 2 * HALF, HALF), HALF)
     copy.wait()
-    for j in range(3):
+    for j in range(2):
         rows = slice(128 * j, 128 * j + 128)
         low = slice(NQ + 128 * j, NQ + 128 * j + 128)
         both = dot(left[256 * j : 256 * j + 256, :], half[...])
-        if j < 2:
-            second_factors(wide, factors, j)
+        second_factors(wide, factors, j)
         re = both[:128, :NQ] - both[128:, NQ:]
         im = both[:128, NQ:] + both[128:, :NQ]
         pr = prop[rows, :NQ]
@@ -208,6 +208,26 @@
         fold[rows, HALF:] = both[128:].astype(BF16)
         fold[low, :HALF] = (-both[128:]).astype(BF16)
         fold[low, HALF:] = both[:128].astype(BF16)
+    rows = slice(256, 256 + HIGH)
+    low = slice(NQ + 256, NQ + 256 + HIGH)
+    one = dot(left[512 : 512 + 2 * HIGH, :], half[:, :BAND])
+    two = dot(left[512 : 512 + 2 * HIGH, :], half[:, NQ : NQ + BAND])
+    re = one[:HIGH] - two[HIGH:]
+    im = two[:HIGH] + one[HIGH:]
+    pr = prop[rows, :BAND]
+    pi = prop[rows, NQ : NQ + BAND]
+    new_r = re * pr - im * pi
+    new_i = re * pi + im * pr
+    one = jnp.concatenate([new_r, new_i], 0).astype(BF16)
+    two = jnp.concatenate([new_i, -new_r], 0).astype(BF16)
+    both = dot_t(one, right[side, :BAND]) + dot_t(two, right[side, NQ : NQ + BAND])
+    fold[rows, :HALF] = both[:HIGH].astype(BF16)
+    fold[rows, HALF:] = both[HIGH:].astype(BF16)
+    fold[low, :HALF] = (-both[HIGH:]).astype(BF16)
+    fold[low, HALF:] = both[:HIGH].astype(BF16)
+    rest = jnp.zeros((NQ - 256 - HIGH, 2 * HALF), BF16)
+    fold[256 + HIGH : NQ, :] = rest
+    fold[NQ + 256 + HIGH :, :] = rest
     for table, first in ((factors, 256 - start), (own_factors, start)):
         rows = pl.ds(pl.multiple_of(first, 256), 256)
         wave = dot(back[rows, :], fold[...])
@@ -215,15 +235,13 @@
         sin = table[:, HALF:]
         last[rows, :HALF] = (wave[:, :HALF] * cos - wave[:, HALF:] * sin).astype(BF16)
         last[rows, HALF:] = (wave[:, :HALF] * sin + wave[:, HALF:] * cos).astype(BF16)
-    part = place // PEERS
-    band = pl.multiple_of(part // 2 * 256 + part % 2 * 64, 2 * PEERS)
-    one = dot(left[pl.ds(band, 2 * PEERS), :], last[...])
-    two = dot(left[pl.ds(band + 128, 2 * PEERS), :], last[...])
-    parts = (one[:, :HALF] - two[:, HALF:], one[:, HALF:] + two[:, :HALF])
+    both = dot(left[pl.ds(pl.multiple_of(place // 64 * 256, 256), 256), :], last[...])
+    parts = (both[:128, :HALF] - both[128:, HALF:], both[:128, HALF:] + both[128:, :HALF])
     for q in range(4):
         rows_in[...] = parts[q // 2][:, 128 * (q % 2) : 128 * (q % 2) + 128]
         for row in range(2):
-            rows_out[pl.ds(2 * q + row, PEERS, stride=8), :] = rows_in[pl.ds(row, PEERS, stride=2), :]
+            own = rows_in[pl.ds(place % 2 * 2 + row, PEERS, stride=4), :]
+            rows_out[pl.ds(2 * q + row, PEERS, stride=8), :] = own
     out[...] = rows_out[...].astype(BF16)
 
 
@@ -293,11 +311,11 @@
             pltpu.VMEM((rows, 128), F32),
             pltpu.VMEM((G, G), BF16),
             pltpu.VMEM((G, 2 * NQ), BF16),
-            pltpu.VMEM((2 * NQ, 2 * NQ), BF16),
+            pltpu.VMEM((512, 2 * NQ), BF16),
             pltpu.VMEM((2 * NQ, 2 * HALF), BF16),
             pltpu.VMEM((G, 2 * HALF), BF16),
             pltpu.VMEM((G // 2, 2 * HALF), F32),
-            pltpu.VMEM((2 * PEERS, 128), F32),
+            pltpu.VMEM((4 * PEERS, 128), F32),
             pltpu.VMEM((8 * PEERS, 128), F32),
             pltpu.VMEM(left.shape, BF16),
             pltpu.SemaphoreType.DMA,
@@ -355,9 +373,9 @@
         for m in range(8):
             block[ROWS * m : ROWS * m + ROWS, :] = rows[...]
         copies = block[...].astype(BF16)
-        for t in range(h, 8, 2):
-            out[2 * t * size : (2 * t + 1) * size, :] = copies
-            out[(2 * t + 1) * size : (2 * t + 2) * size, :] = copies
+        for t in range(16):
+            if t // 4 % 2 == h:
+                out[t * size : (t + 1) * size, :] = copies
 
 
 def message(potential):
@@ -389,7 +407,8 @@
     cells = lax.all_to_all(
         mine, ("beam", "grp"), 0, 0, tiled=True, axis_index_groups=near_groups(peers)
     )
-    site = lax.dynamic_index_in_dim(probe_sites, group * 16 + position % 16, 0, keepdims=False)
+    probe = position // 16 % 2 * 8 + position // 2 % 8
+    site = lax.dynamic_index_in_dim(probe_sites, group * 16 + probe, 0, keepdims=False)
     beams = own_coefficients(wave_vectors, site)
     made = prepare(beams, right, back, chirp)
     band = band_rows(2 * position)
@@ -401,7 +420,11 @@
     other, prop, back = (placed(a, pltpu.VMEM) for a in (other, prop, back))
     near = (other, first, factors, right_near, phi, prop, back)
     sent = main(near, placed(left, pltpu.HBM))
-    runs = [list(range(k, k + PEERS)) for k in range(0, peers, PEERS)]
+    runs = [
+        [64 * far + 16 * z + 2 * y + x for z in range(4) for y in range(8)]
+        for far in range(2)
+        for x in range(2)
+    ]
     parts = lax.all_to_all(
         sent.reshape(PEERS, 8, 128), "beam", 0, 0, tiled=True, axis_index_groups=runs
     )

time: 63.7 us -> 62.9 us (0.987)
  no operation moved by 1% of the time
where the time goes in v7:
time: 62.9 us; the launch traced here: 62.6 us
  starting transfers between devices  26.1 us (41%)
  blocking collectives  13.1 us (21%)
  Pallas kernels  9.23 us (15%)
  waiting for transfers between devices  8.71 us (14%)
  local copies, waits for them, and re-layouts  3.59 us (6%)
  other arithmetic  1.65 us (3%)
    all_to_all x1, starting transfers between devices, local(): lax.all_to_all(mine, ('beam', 'grp'), 0, 0, tiled=True, axis_index_groups...  20.5 us
    all_to_all x1, blocking collectives, local(): lax.all_to_all(sent.reshape(PEERS, 8, 128), 'beam', 0, 0, tiled=True, axi...  13.1 us
    all_to_all x1, waiting for transfers between devices, local(): lax.all_to_all(mine, ('beam', 'grp'), 0, 0, tiled=True, axis_index_groups...  8.71 us
    ppermute x1, starting transfers between devices, local(): other = lax.ppermute(cells, 'grp', [(0, 1), (1, 0), (2, 3), (3, 2)])  5.59 us
    pallas_call x1, Pallas kernels, main(): pl.pallas_call(main_kernel, in_specs=[VMEM] * 7 + [FAR], out_specs=VMEM,...  3.79 us
    unnamed x22, local copies, waits for them, and re-layouts  2.88 us
    pallas_call x1, Pallas kernels, prepare(): pl.pallas_call(prepare_kernel, in_specs=[VMEM] * 5, out_specs=[VMEM] * 3,...  2.4 us
    mul x1, other arithmetic, own_coefficients(): coef_i = (weight * jnp.sin(angle)).astype(BF16).astype(F32) * G  1.43 us
  transfers between devices with their start and end apart: 2, of which 1 were waited for; matrix products, arithmetic and copies ran while one was open for 4% of the time, Pallas kernels for 6%

profile of v7, /device:TPU:1, one launch (start us, length us, event | category | flops | bytes accessed | tf_op | source)
XLA Modules:
  0.0 62.6 jit_solution(1176166724471441001)
XLA Ops:
  0.0 0.0 copy-start
  0.0 0.0 copy-start.1
  0.0 0.0 copy-start.8
  0.0 0.0 copy-start.9
  0.0 0.8 %copy-done.9 = bf16[2,2048]{1,0:T(2,128)(2,1)S(1)} copy-done((bf16[2,2048]{1,0:T(2,128)(2,1)S(1)}, bf16[2,2048]{1,0:T(2,128)(2,1)}, u32[]{:S(2)}) %copy-start.9) | copy-done | bytes 8216
  0.8 0.8 %message.1 = bf16[1536,128]{1,0:T(8,128)(2,1)} custom-call(bf16[2,2048]{1,0:T(2,128)(2,1)S(1)} %copy-done.9), custom_call_target="tpu_custom_call" | custom-call | tf_op jit(solution)/shard_map/message/pallas_call | solution.py:382
  1.6 20.5 %all-to-all-start = ((bf16[128,6,2,128]{3,2,1,0:T(2,128)(2,1)}), bf16[128,6,2,128]{3,2,1,0:T(2,128)(2,1)S(1)}, u32[]{:S(2)}, u32[]{:S(2)}) async-start(bf16[128,6,2,128]{3,2,1,0:T(2,128)(2,1)} %bitcast), calls=%async_computation | async-start | bytes 786432 | tf_op jit(solution)/shard_map/all_to_all | solution.py:407
  22.2 0.0 copy-done
  22.2 0.1 constant_dynamic-slice_fusion
  22.3 0.6 fusion.14
  22.9 0.0 copy-done.10
  22.9 1.4 %fusion.12 = (f32[1,512]{1,0:T(1,128)S(1)}, f32[1,512]{1,0:T(1,128)S(1)}, f32[512,1]{0,1:T(1,128)S(1)}) fusion(s32[512,2]{0,1:T(2,128)S(1)} %copy-done.10, s32[]{:T(128)} %bitcast.5, s32[]{:T(128)} %bitcast.4), kind=kLoop, calls=%fused_computation.23 | loop fusion | flops 13824 | bytes 10248 | tf_op jit(solution)/shard_map/mul | solution.py:348
  24.3 0.1 fusion.9
  24.5 0.0 copy-done.1
  24.5 0.0 copy-done.7
  24.5 0.0 copy-done.8
  24.5 0.0 copy-start.2
  24.5 1.1 %copy-done.2 = bf16[512,768]{1,0:T(8,128)(2,1)S(1)} copy-done((bf16[512,768]{1,0:T(8,128)(2,1)S(1)}, bf16[512,768]{1,0:T(8,128)(2,1)}, u32[]{:S(2)}) %copy-start.2) | copy-done | bytes 786456
  25.6 2.4 %prepare.1 = (bf16[512,1024]{1,0:T(8,128)(2,1)S(1)}, f32[384,768]{1,0:T(8,128)}, bf16[1024,512]{1,0:T(8,128)(2,1)S(1)}) custom-call(f32[8,512]{1,0:T(8,128)S(1)} %concatenate.6.beams, bf16[512,768]{1,0:T(8,128)(2,1)S(1)} %copy-done.1, bf16[512,768]{1,0:T(8,128)(2,1)S(1)} %copy-done.2, f32[8,384]{1,0:T(8,128)S(1)} %copy-done.8, f32[384,8]{1,0:T(8,128)S(1)} %copy-done.7), custom_call_target="tpu_custom_call" | custom-call | tf_op jit(solution)/shard_map/prepare/pallas_call | solution.py:274
  28.0 0.9 %copy-done.5 = bf16[1024,512]{1,0:T(8,128)(2,1)} copy-done((bf16[1024,512]{1,0:T(8,128)(2,1)}, bf16[1024,512]{1,0:T(8,128)(2,1)S(1)}, u32[]{:S(2)}) %copy-start.5) | copy-done | bytes 1048600
  29.0 0.1 cosine_select_fusion
  29.1 8.7 %all-to-all-done = bf16[128,6,2,128]{3,2,1,0:T(2,128)(2,1)S(1)} async-done(((bf16[128,6,2,128]{3,2,1,0:T(2,128)(2,1)}), bf16[128,6,2,128]{3,2,1,0:T(2,128)(2,1)S(1)}, u32[]{:S(2)}, u32[]{:S(2)}) %all-to-all-start) | async-done | bytes 393248 | tf_op jit(solution)/shard_map/all_to_all | solution.py:407
  37.8 5.6 %collective-permute-start = (bf16[1536,128]{1,0:T(8,128)(2,1)S(1)}, bf16[1536,128]{1,0:T(8,128)(2,1)S(1)}, u32[]{:S(2)}, u32[]{:S(2)}) collective-permute-start(bf16[1536,128]{1,0:T(8,128)(2,1)S(1)} %bitcast.28), channel_id=1, source_target_pairs={{0,1},{1,0},{2,3},{3,2},{4,5},{5,4},{6,7},{7,6},{8,9},{9,8},{10,11... | collective-permute-start | bytes 1179656 | tf_op jit(solution)/shard_map/ppermute | solution.py:417
  43.4 1.3 %early.1 = (bf16[256,768]{1,0:T(8,128)(2,1)S(1)}, f32[256,512]{1,0:T(8,128)S(1)}) custom-call(bf16[1536,128]{1,0:T(8,128)(2,1)S(1)} %bitcast.29, bf16[512,1024]{1,0:T(8,128)(2,1)S(1)} %get-tuple-element.19.phi, bf16[512,768]{1,0:T(8,128)(2,1)S(1)} %copy-done.1), custom_call_target="tpu_custom_call" | custom-call | tf_op jit(solution)/shard_map/early/pallas_call | solution.py:289
  44.8 0.0 collective-permute-done.other
  44.8 0.0 copy-done.3
  44.8 0.0 copy-done.4
  44.8 0.0 copy-start.6
  44.8 3.8 %propagate.1 = bf16[256,128]{1,0:T(8,128)(2,1)S(1)} custom-call(bf16[1536,128]{1,0:T(8,128)(2,1)S(1)} %collective-permute-done.other, bf16[256,768]{1,0:T(8,128)(2,1)S(1)} %get-tuple-element.20.early, f32[256,512]{1,0:T(8,128)S(1)} %get-tuple-element.21.own_factors, bf16[512,768]{1,0:T(8,128)(2,1)S(1)} %copy-done.1, ...), custom_call_target="tpu_custom_call" | custom-call | tf_op jit(solution)/shard_map/propagate/pallas_call | solution.py:305
  48.6 13.1 %all_to_all.10 = bf16[32,8,128]{2,1,0:T(8,128)(2,1)S(1)} all-to-all(bf16[32,8,128]{2,1,0:T(8,128)(2,1)S(1)} %bitcast.30), channel_id=1, replica_groups={{0,8,16,24,32,40,48,56,64,72,80,88,96,104,112,120,128,136,144,152,160,1..., dimensions={0} | all-to-all | bytes 131072 | tf_op jit(solution)/shard_map/all_to_all | solution.py:428
  61.7 0.0 copy-done.6
  61.7 0.9 %finish.1 = f32[2,16,512]{2,1,0:T(8,128)} custom-call(bf16[256,128]{1,0:T(8,128)(2,1)S(1)} %bitcast.31, bf16[1024,512]{1,0:T(8,128)(2,1)S(1)} %copy-done.6, f32[2,512]{1,0:T(2,128)S(1)} %pad_maximum_fusion.prop), custom_call_target="tpu_custom_call" | custom-call | tf_op jit(solution)/shard_map/finish/pallas_call | solution.py:329
  (11 shorter events, 0.1 us)
Async XLA Ops:
  0.0 22.2 %copy-start = (s32[64,2]{0,1:T(2,128)S(1)}, s32[64,2]{0,1:T(2,128)}, u32[]{:S(2)}) copy-start(s32[64,2]{0,1:T(2,128)} %param.9) | copy-start | bytes 1540
  0.0 24.4 %copy-start.1 = (bf16[512,768]{1,0:T(8,128)(2,1)S(1)}, bf16[512,768]{1,0:T(8,128)(2,1)}, u32[]{:S(2)}) copy-start(bf16[512,768]{1,0:T(8,128)(2,1)} %constant.122.clone.right) | copy-start | bytes 2359300
  0.0 24.5 %copy-start.7 = (f32[384,8]{1,0:T(8,128)S(1)}, f32[384,8]{1,0:T(8,128)}, u32[]{:S(2)}) copy-start(f32[384,8]{1,0:T(8,128)} %constant.126.chirp_t) | copy-start | bytes 36868
  0.0 24.5 %copy-start.8 = (f32[8,384]{1,0:T(8,128)S(1)}, f32[8,384]{1,0:T(8,128)}, u32[]{:S(2)}) copy-start(f32[8,384]{1,0:T(8,128)} %constant.125.clone.chirp) | copy-start | bytes 36868
  0.0 0.8 %copy-start.9 = (bf16[2,2048]{1,0:T(2,128)(2,1)S(1)}, bf16[2,2048]{1,0:T(2,128)(2,1)}, u32[]{:S(2)}) copy-start(bf16[2,2048]{1,0:T(2,128)(2,1)} %cells.1) | copy-start | bytes 24580
  0.8 22.1 %copy-start.10 = (s32[512,2]{0,1:T(2,128)S(1)}, s32[512,2]{0,1:T(2,128)}, u32[]{:S(2)}) copy-start(s32[512,2]{0,1:T(2,128)} %param.8) | copy-start | bytes 12292
  1.6 36.2 %all-to-all-start = ((bf16[128,6,2,128]{3,2,1,0:T(2,128)(2,1)}), bf16[128,6,2,128]{3,2,1,0:T(2,128)(2,1)S(1)}, u32[]{:S(2)}, u32[]{:S(2)}) async-start(bf16[128,6,2,128]{3,2,1,0:T(2,128)(2,1)} %bitcast), calls=%async_computation | async-start | bytes 786432 | tf_op jit(solution)/shard_map/all_to_all | solution.py:407
  24.5 1.1 %copy-start.2 = (bf16[512,768]{1,0:T(8,128)(2,1)S(1)}, bf16[512,768]{1,0:T(8,128)(2,1)}, u32[]{:S(2)}) copy-start(bf16[512,768]{1,0:T(8,128)(2,1)} %constant.124.clone.back) | copy-start | bytes 2359300
  28.0 0.9 %copy-start.5 = (bf16[1024,512]{1,0:T(8,128)(2,1)}, bf16[1024,512]{1,0:T(8,128)(2,1)S(1)}, u32[]{:S(2)}) copy-start(bf16[1024,512]{1,0:T(8,128)(2,1)S(1)} %get-tuple-element.23.final) | copy-start | bytes 3145732
  29.0 15.8 %copy-start.3 = (bf16[512,768]{1,0:T(8,128)(2,1)S(1)}, bf16[512,768]{1,0:T(8,128)(2,1)}, u32[]{:S(2)}) copy-start(bf16[512,768]{1,0:T(8,128)(2,1)} %constant.124.clone.back) | copy-start | bytes 2359300
  37.8 6.9 %copy-start.4 = (f32[384,768]{1,0:T(8,128)S(1)}, f32[384,768]{1,0:T(8,128)}, u32[]{:S(2)}) copy-start(f32[384,768]{1,0:T(8,128)} %get-tuple-element.22.prop) | copy-start | bytes 3538948
  37.8 6.9 %collective-permute-start = (bf16[1536,128]{1,0:T(8,128)(2,1)S(1)}, bf16[1536,128]{1,0:T(8,128)(2,1)S(1)}, u32[]{:S(2)}, u32[]{:S(2)}) collective-permute-start(bf16[1536,128]{1,0:T(8,128)(2,1)S(1)} %bitcast.28), channel_id=1, source_target_pairs={{0,1},{1,0},{2,3},{3,2},{4,5},{5,4},{6,7},{7,6},{8,9},{9,8},{10,11... | collective-permute-start | bytes 1179656 | tf_op jit(solution)/shard_map/ppermute | solution.py:417
  44.8 16.9 %copy-start.6 = (bf16[1024,512]{1,0:T(8,128)(2,1)S(1)}, bf16[1024,512]{1,0:T(8,128)(2,1)}, u32[]{:S(2)}) copy-start(bf16[1024,512]{1,0:T(8,128)(2,1)} %copy-done.5) | copy-start | bytes 3145732

commit v8 on v7

--- a/solution.py
+++ b/solution.py
@@ -167,19 +167,20 @@
         factors[rows, HALF + 128 * q : HALF + 128 * q + 128] = sin
 
 
-def early_kernel(cells, phi, right, half, factors, wide, data):
+def early_kernel(cells, phi, right, left_far, half, factors, left, wide, data, sem):
+    copy = pltpu.make_async_copy(left_far, left, sem)
+    copy.start()
     wide[...] = cells[...].astype(F32)
     forward_rows(wide, phi, right, data, half, own_core() * 256, 0)
     for j in range(2):
         second_factors(wide, factors, j)
+    copy.wait()
 
 
 def main_kernel(
-    other, early, own_factors, right, phi, prop, back, left_far, out,
-    wide, data, half, spec, fold, last, factors, rows_in, rows_out, left, sem,
+    other, early, own_factors, right, phi, prop, back, left, out,
+    wide, data, half, spec, fold, last, factors, rows_in, rows_out,
 ):
-    copy = pltpu.make_async_copy(left_far, left, sem)
-    copy.start()
     place = lax.axis_index("beam")
     core = own_core()
     wide[...] = other[...].astype(F32)
@@ -187,7 +188,6 @@
     half[pl.ds(pl.multiple_of(start, 256), 256), :] = early[...]
     forward_rows(wide, phi, right, data, half, 256 - start, 256 - start)
     side = pl.ds(pl.multiple_of(place // 32 % 2 * HALF, HALF), HALF)
-    copy.wait()
     for j in range(2):
         rows = slice(128 * j, 128 * j + 128)
         low = slice(NQ + 128 * j, NQ + 128 * j + 128)
@@ -285,26 +285,31 @@
     )(beams, right, back, chirp, chirp.T)
 
 
-def early(cells, phi, right):
+def early(cells, phi, right, left):
     return pl.pallas_call(
         early_kernel,
-        in_specs=[VMEM] * 3,
-        out_specs=[VMEM] * 2,
-        out_shape=[pltpu.VMEM((G // 2, 2 * NQ), BF16), pltpu.VMEM((G // 2, 2 * HALF), F32)],
+        in_specs=[VMEM] * 3 + [FAR],
+        out_specs=[VMEM] * 3,
+        out_shape=[
+            pltpu.VMEM((G // 2, 2 * NQ), BF16),
+            pltpu.VMEM((G // 2, 2 * HALF), F32),
+            pltpu.VMEM(left.shape, BF16),
+        ],
         scratch_shapes=[
             pltpu.VMEM((cells.shape[0], 128), F32),
             pltpu.VMEM((G, G), BF16),
+            pltpu.SemaphoreType.DMA,
         ],
         compiler_params=LIMIT,
         name="early",
-    )(cells, phi, right)
-
-
-def main(near, left):
+    )(cells, phi, right, left)
+
+
+def main(near):
     rows = near[0].shape[0]
     return pl.pallas_call(
         main_kernel,
-        in_specs=[VMEM] * 7 + [FAR],
+        in_specs=[VMEM] * 8,
         out_specs=VMEM,
         out_shape=jax.ShapeDtypeStruct((8 * PEERS, 128), BF16),
         scratch_shapes=[
@@ -317,12 +322,10 @@
             pltpu.VMEM((G // 2, 2 * HALF), F32),
             pltpu.VMEM((4 * PEERS, 128), F32),
             pltpu.VMEM((8 * PEERS, 128), F32),
-            pltpu.VMEM(left.shape, BF16),
-            pltpu.SemaphoreType.DMA,
         ],
         compiler_params=LIMIT,
         name="propagate",
-    )(*near, left)
+    )(*near)
 
 
 def finish(parts, final, prop):
@@ -416,10 +419,10 @@
     cells = cells.reshape(peers * ROWS, 128)
     other = lax.ppermute(cells, "grp", [(0, 1), (1, 0), (2, 3), (3, 2)])
     cells, right_near, phi = (placed(a, pltpu.VMEM) for a in (cells, right, phi))
-    first, factors = (placed(a, pltpu.VMEM) for a in early(cells, phi, right_near))
+    made = early(cells, phi, right_near, placed(left, pltpu.HBM))
+    first, factors, left = (placed(a, pltpu.VMEM) for a in made)
     other, prop, back = (placed(a, pltpu.VMEM) for a in (other, prop, back))
-    near = (other, first, factors, right_near, phi, prop, back)
-    sent = main(near, placed(left, pltpu.HBM))
+    sent = main((other, first, factors, right_near, phi, prop, back, left))
     runs = [
         [64 * far + 16 * z + 2 * y + x for z in range(4) for y in range(8)]
         for far in range(2)

time: 62.9 us -> 62.7 us (level)
  waiting for transfers between devices: 8.71 us -> 9.89 us
  local copies, waits for them, and re-layouts: 3.59 us -> 2.56 us
    all_to_all x1, waiting for transfers between devices: 8.71 us -> 9.89 us  [local(): lax.all_to_all(mine, ('beam', 'grp'), 0, 0, tiled=True, axis_index_groups...]
    unnamed x22 -> x18, local copies, waits for them, and re-layouts: 2.88 us -> 1.93 us
  transfers between devices with their start and end apart: 2 -> 2, of which waited for: 1 -> 1; matrix products, arithmetic and copies ran while one was open for 4% -> 3% of each run, Pallas kernels for 6% -> 6%
where the time goes in v8:
time: 62.7 us; the launch traced here: 62.4 us
  starting transfers between devices  26.1 us (42%)
  blocking collectives  13.1 us (21%)
  waiting for transfers between devices  9.89 us (16%)
  Pallas kernels  8.98 us (14%)
  local copies, waits for them, and re-layouts  2.56 us (4%)
  other arithmetic  1.51 us (2%)
    all_to_all x1, starting transfers between devices, local(): lax.all_to_all(mine, ('beam', 'grp'), 0, 0, tiled=True, axis_index_groups...  20.5 us
    all_to_all x1, blocking collectives, local(): lax.all_to_all(sent.reshape(PEERS, 8, 128), 'beam', 0, 0, tiled=True, axi...  13.1 us
    all_to_all x1, waiting for transfers between devices, local(): lax.all_to_all(mine, ('beam', 'grp'), 0, 0, tiled=True, axis_index_groups...  9.89 us
    ppermute x1, starting transfers between devices, local(): other = lax.ppermute(cells, 'grp', [(0, 1), (1, 0), (2, 3), (3, 2)])  5.59 us
    pallas_call x1, Pallas kernels, main(): pl.pallas_call(main_kernel, in_specs=[VMEM] * 8, out_specs=VMEM, out_shap...  3.53 us
    pallas_call x1, Pallas kernels, prepare(): pl.pallas_call(prepare_kernel, in_specs=[VMEM] * 5, out_specs=[VMEM] * 3,...  2.39 us
    unnamed x18, local copies, waits for them, and re-layouts  1.93 us
    pallas_call x1, Pallas kernels, early(): pl.pallas_call(early_kernel, in_specs=[VMEM] * 3 + [FAR], out_specs=[VMEM...  1.33 us
  transfers between devices with their start and end apart: 2, of which 1 were waited for; matrix products, arithmetic and copies ran while one was open for 3% of the time, Pallas kernels for 6%

profile of v8, /device:TPU:1, one launch (start us, length us, event | category | flops | bytes accessed | tf_op | source)
XLA Modules:
  0.0 62.4 jit_solution(3552291314197775372)
XLA Ops:
  0.0 0.0 copy-start
  0.0 0.0 copy-start.1
  0.0 0.0 copy-start.5
  0.0 0.0 copy-start.6
  0.0 0.0 copy-start.7
  0.0 0.8 %copy-done.7 = bf16[2,2048]{1,0:T(2,128)(2,1)S(1)} copy-done((bf16[2,2048]{1,0:T(2,128)(2,1)S(1)}, bf16[2,2048]{1,0:T(2,128)(2,1)}, u32[]{:S(2)}) %copy-start.7) | copy-done | bytes 8216
  0.8 0.0 copy-start.8
  0.8 0.8 %message.1 = bf16[1536,128]{1,0:T(8,128)(2,1)} custom-call(bf16[2,2048]{1,0:T(2,128)(2,1)S(1)} %copy-done.7), custom_call_target="tpu_custom_call" | custom-call | tf_op jit(solution)/shard_map/message/pallas_call | solution.py:385
  1.6 20.5 %all-to-all-start = ((bf16[128,6,2,128]{3,2,1,0:T(2,128)(2,1)}), bf16[128,6,2,128]{3,2,1,0:T(2,128)(2,1)S(1)}, u32[]{:S(2)}, u32[]{:S(2)}) async-start(bf16[128,6,2,128]{3,2,1,0:T(2,128)(2,1)} %bitcast), calls=%async_computation | async-start | bytes 786432 | tf_op jit(solution)/shard_map/all_to_all | solution.py:410
  22.2 0.0 copy-done
  22.2 0.1 constant_dynamic-slice_fusion
  22.3 0.5 fusion.14
  22.8 0.0 copy-done.8
  22.8 1.3 %fusion.12 = (f32[1,512]{1,0:T(1,128)S(1)}, f32[1,512]{1,0:T(1,128)S(1)}, f32[512,1]{0,1:T(1,128)S(1)}) fusion(s32[512,2]{0,1:T(2,128)S(1)} %copy-done.8, s32[]{:T(128)} %bitcast.5, s32[]{:T(128)} %bitcast.4), kind=kLoop, calls=%fused_computation.23 | loop fusion | flops 13824 | bytes 10248 | tf_op jit(solution)/shard_map/mul | solution.py:351
  24.1 0.1 fusion.9
  24.2 0.0 copy-done.1
  24.2 0.0 copy-done.5
  24.3 0.0 copy-done.6
  24.3 0.0 copy-start.2
  24.3 1.1 %copy-done.2 = bf16[512,768]{1,0:T(8,128)(2,1)S(1)} copy-done((bf16[512,768]{1,0:T(8,128)(2,1)S(1)}, bf16[512,768]{1,0:T(8,128)(2,1)}, u32[]{:S(2)}) %copy-start.2) | copy-done | bytes 786456
  25.4 2.4 %prepare.1 = (bf16[512,1024]{1,0:T(8,128)(2,1)S(1)}, f32[384,768]{1,0:T(8,128)}, bf16[1024,512]{1,0:T(8,128)(2,1)S(1)}) custom-call(f32[8,512]{1,0:T(8,128)S(1)} %concatenate.6.beams, bf16[512,768]{1,0:T(8,128)(2,1)S(1)} %copy-done.1, bf16[512,768]{1,0:T(8,128)(2,1)S(1)} %copy-done.2, f32[8,384]{1,0:T(8,128)S(1)} %copy-done.6, f32[384,8]{1,0:T(8,128)S(1)} %copy-done.5), custom_call_target="tpu_custom_call" | custom-call | tf_op jit(solution)/shard_map/prepare/pallas_call | solution.py:274
  27.8 0.1 cosine_select_fusion
  28.0 9.9 %all-to-all-done = bf16[128,6,2,128]{3,2,1,0:T(2,128)(2,1)S(1)} async-done(((bf16[128,6,2,128]{3,2,1,0:T(2,128)(2,1)}), bf16[128,6,2,128]{3,2,1,0:T(2,128)(2,1)S(1)}, u32[]{:S(2)}, u32[]{:S(2)}) %all-to-all-start) | async-done | bytes 393248 | tf_op jit(solution)/shard_map/all_to_all | solution.py:410
  37.8 0.0 copy-start.4
  37.8 5.6 %collective-permute-start = (bf16[1536,128]{1,0:T(8,128)(2,1)S(1)}, bf16[1536,128]{1,0:T(8,128)(2,1)S(1)}, u32[]{:S(2)}, u32[]{:S(2)}) collective-permute-start(bf16[1536,128]{1,0:T(8,128)(2,1)S(1)} %bitcast.28), channel_id=1, source_target_pairs={{0,1},{1,0},{2,3},{3,2},{4,5},{5,4},{6,7},{7,6},{8,9},{9,8},{10,11... | collective-permute-start | bytes 1179656 | tf_op jit(solution)/shard_map/ppermute | solution.py:420
  43.4 1.3 %early.1 = (bf16[256,768]{1,0:T(8,128)(2,1)S(1)}, f32[256,512]{1,0:T(8,128)S(1)}, bf16[704,512]{1,0:T(8,128)(2,1)S(1)}) custom-call(bf16[1536,128]{1,0:T(8,128)(2,1)S(1)} %bitcast.29, bf16[512,1024]{1,0:T(8,128)(2,1)S(1)} %get-tuple-element.20.phi, bf16[512,768]{1,0:T(8,128)(2,1)S(1)} %copy-done.1, bf16[704,512]{1,0:T(8,128)(2,1)} %constant.123.clone.left_far), custom_call_target="tpu_custom_call" | custom-call | tf_op jit(solution)/shard_map/early/pallas_call | solution.py:289
  44.8 0.0 collective-permute-done.other
  44.8 0.0 copy-done.3
  44.8 0.0 copy-done.4
  44.8 3.5 %propagate.1 = bf16[256,128]{1,0:T(8,128)(2,1)S(1)} custom-call(bf16[1536,128]{1,0:T(8,128)(2,1)S(1)} %collective-permute-done.other, bf16[256,768]{1,0:T(8,128)(2,1)S(1)} %get-tuple-element.21.early, f32[256,512]{1,0:T(8,128)S(1)} %get-tuple-element.22.own_factors, bf16[512,768]{1,0:T(8,128)(2,1)S(1)} %copy-done.1, ...), custom_call_target="tpu_custom_call" | custom-call | tf_op jit(solution)/shard_map/propagate/pallas_call | solution.py:310
  48.4 13.1 %all_to_all.10 = bf16[32,8,128]{2,1,0:T(8,128)(2,1)S(1)} all-to-all(bf16[32,8,128]{2,1,0:T(8,128)(2,1)S(1)} %bitcast.30), channel_id=1, replica_groups={{0,8,16,24,32,40,48,56,64,72,80,88,96,104,112,120,128,136,144,152,160,1..., dimensions={0} | all-to-all | bytes 131072 | tf_op jit(solution)/shard_map/all_to_all | solution.py:431
  61.5 0.9 %finish.1 = f32[2,16,512]{2,1,0:T(8,128)} custom-call(bf16[256,128]{1,0:T(8,128)(2,1)S(1)} %bitcast.31, bf16[1024,512]{1,0:T(8,128)(2,1)S(1)} %get-tuple-element.25.final, f32[2,512]{1,0:T(2,128)S(1)} %pad_maximum_fusion.prop), custom_call_target="tpu_custom_call" | custom-call | tf_op jit(solution)/shard_map/finish/pallas_call | solution.py:332
  (7 shorter events, 0.1 us)
Async XLA Ops:
  0.0 22.2 %copy-start = (s32[64,2]{0,1:T(2,128)S(1)}, s32[64,2]{0,1:T(2,128)}, u32[]{:S(2)}) copy-start(s32[64,2]{0,1:T(2,128)} %param.9) | copy-start | bytes 1540
  0.0 24.2 %copy-start.1 = (bf16[512,768]{1,0:T(8,128)(2,1)S(1)}, bf16[512,768]{1,0:T(8,128)(2,1)}, u32[]{:S(2)}) copy-start(bf16[512,768]{1,0:T(8,128)(2,1)} %constant.122.clone.right) | copy-start | bytes 2359300
  0.0 24.2 %copy-start.5 = (f32[384,8]{1,0:T(8,128)S(1)}, f32[384,8]{1,0:T(8,128)}, u32[]{:S(2)}) copy-start(f32[384,8]{1,0:T(8,128)} %constant.126.chirp_t) | copy-start | bytes 36868
  0.0 24.2 %copy-start.6 = (f32[8,384]{1,0:T(8,128)S(1)}, f32[8,384]{1,0:T(8,128)}, u32[]{:S(2)}) copy-start(f32[8,384]{1,0:T(8,128)} %constant.125.clone.chirp) | copy-start | bytes 36868
  0.0 0.8 %copy-start.7 = (bf16[2,2048]{1,0:T(2,128)(2,1)S(1)}, bf16[2,2048]{1,0:T(2,128)(2,1)}, u32[]{:S(2)}) copy-start(bf16[2,2048]{1,0:T(2,128)(2,1)} %cells.1) | copy-start | bytes 24580
  0.8 22.0 %copy-start.8 = (s32[512,2]{0,1:T(2,128)S(1)}, s32[512,2]{0,1:T(2,128)}, u32[]{:S(2)}) copy-start(s32[512,2]{0,1:T(2,128)} %param.8) | copy-start | bytes 12292
  1.6 36.2 %all-to-all-start = ((bf16[128,6,2,128]{3,2,1,0:T(2,128)(2,1)}), bf16[128,6,2,128]{3,2,1,0:T(2,128)(2,1)S(1)}, u32[]{:S(2)}, u32[]{:S(2)}) async-start(bf16[128,6,2,128]{3,2,1,0:T(2,128)(2,1)} %bitcast), calls=%async_computation | async-start | bytes 786432 | tf_op jit(solution)/shard_map/all_to_all | solution.py:410
  24.3 1.1 %copy-start.2 = (bf16[512,768]{1,0:T(8,128)(2,1)S(1)}, bf16[512,768]{1,0:T(8,128)(2,1)}, u32[]{:S(2)}) copy-start(bf16[512,768]{1,0:T(8,128)(2,1)} %constant.124.clone.back) | copy-start | bytes 2359300
  37.8 7.0 %copy-start.3 = (bf16[512,768]{1,0:T(8,128)(2,1)S(1)}, bf16[512,768]{1,0:T(8,128)(2,1)}, u32[]{:S(2)}) copy-start(bf16[512,768]{1,0:T(8,128)(2,1)} %constant.124.clone.back) | copy-start | bytes 2359300
  37.8 7.0 %copy-start.4 = (f32[384,768]{1,0:T(8,128)S(1)}, f32[384,768]{1,0:T(8,128)}, u32[]{:S(2)}) copy-start(f32[384,768]{1,0:T(8,128)} %get-tuple-element.23.prop) | copy-start | bytes 3538948
  37.8 6.9 %collective-permute-start = (bf16[1536,128]{1,0:T(8,128)(2,1)S(1)}, bf16[1536,128]{1,0:T(8,128)(2,1)S(1)}, u32[]{:S(2)}, u32[]{:S(2)}) collective-permute-start(bf16[1536,128]{1,0:T(8,128)(2,1)S(1)} %bitcast.28), channel_id=1, source_target_pairs={{0,1},{1,0},{2,3},{3,2},{4,5},{5,4},{6,7},{7,6},{8,9},{9,8},{10,11... | collective-permute-start | bytes 1179656 | tf_op jit(solution)/shard_map/ppermute | solution.py:420

commit v9 on v8

--- a/solution.py
+++ b/solution.py
@@ -109,7 +109,17 @@
     return lax.dot_general(a, b, (((1,), (1,)), ((), ())), preferred_element_type=F32)
 
 
-def prepare_kernel(beams, right, back, chirp, chirp_t, phi, prop, final):
+def prepare_kernel(
+    beams, right_far, back_far, chirp, chirp_t, phi, prop, final, right, back, sems
+):
+    copies = (
+        pltpu.make_async_copy(right_far, right, sems.at[0]),
+        pltpu.make_async_copy(back_far, back, sems.at[1]),
+    )
+    for copy in copies:
+        copy.start()
+    for copy in copies:
+        copy.wait()
     index = lax.broadcasted_iota(jnp.int32, (BAND, G), 0).astype(F32)
     on_x = index == beams[0:1, :]
     on_y = jnp.where(index == beams[1:2, :], 1.0, 0.0).astype(BF16)
@@ -273,16 +283,18 @@
 def prepare(beams, right, back, chirp):
     return pl.pallas_call(
         prepare_kernel,
-        in_specs=[VMEM] * 5,
-        out_specs=[VMEM] * 3,
+        in_specs=[VMEM, FAR, FAR, VMEM, VMEM],
+        out_specs=[VMEM] * 4,
         out_shape=[
             pltpu.VMEM((G, 2 * G), BF16),
             pltpu.HBM((NQ, 2 * NQ), F32),
             pltpu.VMEM((2 * G, 2 * BAND), BF16),
+            pltpu.VMEM(right.shape, BF16),
         ],
+        scratch_shapes=[pltpu.VMEM(back.shape, BF16), pltpu.SemaphoreType.DMA((2,))],
         compiler_params=LIMIT,
         name="prepare",
-    )(beams, right, back, chirp, chirp.T)
+    )(beams, placed(right, pltpu.HBM), placed(back, pltpu.HBM), chirp, chirp.T)
 
 
 def early(cells, phi, right, left):
@@ -415,7 +427,7 @@
     beams = own_coefficients(wave_vectors, site)
     made = prepare(beams, right, back, chirp)
     band = band_rows(2 * position)
-    cells, phi, prop, final, band = lax.optimization_barrier((cells, *made, band))
+    cells, phi, prop, final, right, band = lax.optimization_barrier((cells, *made, band))
     cells = cells.reshape(peers * ROWS, 128)
     other = lax.ppermute(cells, "grp", [(0, 1), (1, 0), (2, 3), (3, 2)])
     cells, right_near, phi = (placed(a, pltpu.VMEM) for a in (cells, right, phi))

time: 62.7 us -> 62.7 us (level)
  Pallas kernels: 8.98 us -> 10.4 us
  local copies, waits for them, and re-layouts: 2.56 us -> 1.44 us
    pallas_call x1, Pallas kernels: 2.39 us -> 3.77 us  [prepare(): pl.pallas_call(prepare_kernel, in_specs=[VMEM, FAR, FAR, VMEM, VMEM], out...]
    unnamed x18 -> x14, local copies, waits for them, and re-layouts: 1.93 us -> 0.75 us
  transfers between devices with their start and end apart: 2 -> 2, of which waited for: 1 -> 1; matrix products, arithmetic and copies ran while one was open for 3% -> 4% of each run, Pallas kernels for 6% -> 8%
where the time goes in v9:
time: 62.7 us; the launch traced here: 62.4 us
  starting transfers between devices  26.1 us (42%)
  blocking collectives  13.1 us (21%)
  Pallas kernels  10.4 us (17%)
  waiting for transfers between devices  9.51 us (15%)
  other arithmetic  1.59 us (3%)
  local copies, waits for them, and re-layouts  1.44 us (2%)
    all_to_all x1, starting transfers between devices, local(): lax.all_to_all(mine, ('beam', 'grp'), 0, 0, tiled=True, axis_index_groups...  20.5 us
    all_to_all x1, blocking collectives, local(): lax.all_to_all(sent.reshape(PEERS, 8, 128), 'beam', 0, 0, tiled=True, axi...  13.1 us
    all_to_all x1, waiting for transfers between devices, local(): lax.all_to_all(mine, ('beam', 'grp'), 0, 0, tiled=True, axis_index_groups...  9.5 us
    ppermute x1, starting transfers between devices, local(): other = lax.ppermute(cells, 'grp', [(0, 1), (1, 0), (2, 3), (3, 2)])  5.59 us
    pallas_call x1, Pallas kernels, prepare(): pl.pallas_call(prepare_kernel, in_specs=[VMEM, FAR, FAR, VMEM, VMEM], out...  3.77 us
    pallas_call x1, Pallas kernels, main(): pl.pallas_call(main_kernel, in_specs=[VMEM] * 8, out_specs=VMEM, out_shap...  3.53 us
    mul x1, other arithmetic, own_coefficients(): coef_i = (weight * jnp.sin(angle)).astype(BF16).astype(F32) * G  1.36 us
    pallas_call x1, Pallas kernels, early(): pl.pallas_call(early_kernel, in_specs=[VMEM] * 3 + [FAR], out_specs=[VMEM...  1.33 us
  transfers between devices with their start and end apart: 2, of which 1 were waited for; matrix products, arithmetic and copies ran while one was open for 4% of the time, Pallas kernels for 8%

profile of v9, /device:TPU:1, one launch (start us, length us, event | category | flops | bytes accessed | tf_op | source)
XLA Modules:
  0.0 62.4 jit_solution(14597072477195607548)
XLA Ops:
  0.0 0.0 copy-start
  0.0 0.0 copy-start.3
  0.0 0.0 copy-start.4
  0.0 0.0 copy-start.5
  0.0 0.7 %copy-done.5 = bf16[2,2048]{1,0:T(2,128)(2,1)S(1)} copy-done((bf16[2,2048]{1,0:T(2,128)(2,1)S(1)}, bf16[2,2048]{1,0:T(2,128)(2,1)}, u32[]{:S(2)}) %copy-start.5) | copy-done | bytes 8216
  0.8 0.0 copy-start.6
  0.8 0.8 %message.1 = bf16[1536,128]{1,0:T(8,128)(2,1)} custom-call(bf16[2,2048]{1,0:T(2,128)(2,1)S(1)} %copy-done.5), custom_call_target="tpu_custom_call" | custom-call | tf_op jit(solution)/shard_map/message/pallas_call | solution.py:397
  1.6 20.5 %all-to-all-start = ((bf16[128,6,2,128]{3,2,1,0:T(2,128)(2,1)}), bf16[128,6,2,128]{3,2,1,0:T(2,128)(2,1)S(1)}, u32[]{:S(2)}, u32[]{:S(2)}) async-start(bf16[128,6,2,128]{3,2,1,0:T(2,128)(2,1)} %bitcast), calls=%async_computation | async-start | bytes 786432 | tf_op jit(solution)/shard_map/all_to_all | solution.py:422
  22.2 0.0 copy-done
  22.2 0.1 constant_dynamic-slice_fusion
  22.3 0.6 fusion.14
  22.8 0.0 copy-done.6
  22.9 1.4 %fusion.12 = (f32[1,512]{1,0:T(1,128)S(1)}, f32[1,512]{1,0:T(1,128)S(1)}, f32[512,1]{0,1:T(1,128)S(1)}) fusion(s32[512,2]{0,1:T(2,128)S(1)} %copy-done.6, s32[]{:T(128)} %bitcast.5, s32[]{:T(128)} %bitcast.4), kind=kLoop, calls=%fused_computation.23 | loop fusion | flops 13824 | bytes 10248 | tf_op jit(solution)/shard_map/mul | solution.py:363
  24.2 0.1 fusion.9
  24.3 0.0 copy-done.3
  24.3 0.0 copy-done.4
  24.4 3.8 %prepare.1 = (bf16[512,1024]{1,0:T(8,128)(2,1)S(1)}, f32[384,768]{1,0:T(8,128)}, bf16[1024,512]{1,0:T(8,128)(2,1)S(1)}, bf16[512,768]{1,0:T(8,128)(2,1)S(1)}) custom-call(f32[8,512]{1,0:T(8,128)S(1)} %concatenate.6.beams, bf16[512,768]{1,0:T(8,128)(2,1)} %constant.122.clone.right_far, bf16[512,768]{1,0:T(8,128)(2,1)} %constant.124.clone.back_far.back, ...), custom_call_target="tpu_custom_call" | custom-call | tf_op jit(solution)/shard_map/prepare/pallas_call | solution.py:284
  28.2 0.1 cosine_select_fusion
  28.3 9.5 %all-to-all-done = bf16[128,6,2,128]{3,2,1,0:T(2,128)(2,1)S(1)} async-done(((bf16[128,6,2,128]{3,2,1,0:T(2,128)(2,1)}), bf16[128,6,2,128]{3,2,1,0:T(2,128)(2,1)S(1)}, u32[]{:S(2)}, u32[]{:S(2)}) %all-to-all-start) | async-done | bytes 393248 | tf_op jit(solution)/shard_map/all_to_all | solution.py:422
  37.8 0.0 copy-start.1
  37.8 0.0 copy-start.2
  37.8 5.6 %collective-permute-start = (bf16[1536,128]{1,0:T(8,128)(2,1)S(1)}, bf16[1536,128]{1,0:T(8,128)(2,1)S(1)}, u32[]{:S(2)}, u32[]{:S(2)}) collective-permute-start(bf16[1536,128]{1,0:T(8,128)(2,1)S(1)} %bitcast.28), channel_id=1, source_target_pairs={{0,1},{1,0},{2,3},{3,2},{4,5},{5,4},{6,7},{7,6},{8,9},{9,8},{10,11... | collective-permute-start | bytes 1179656 | tf_op jit(solution)/shard_map/ppermute | solution.py:432
  43.4 1.3 %early.1 = (bf16[256,768]{1,0:T(8,128)(2,1)S(1)}, f32[256,512]{1,0:T(8,128)S(1)}, bf16[704,512]{1,0:T(8,128)(2,1)S(1)}) custom-call(bf16[1536,128]{1,0:T(8,128)(2,1)S(1)} %bitcast.29, bf16[512,1024]{1,0:T(8,128)(2,1)S(1)} %get-tuple-element.23.phi, bf16[512,768]{1,0:T(8,128)(2,1)S(1)} %get-tuple-element.24.right, bf16[704,512]{1,0:T(8,128)(2,1)} %constant.123.clone.left_far), custom_call_target="tpu_custom_call" | custom-call | tf_op jit(solution)/shard_map/early/pallas_call | solution.py:301
  44.7 0.0 collective-permute-done.other
  44.8 0.0 copy-done.1
  44.8 0.0 copy-done.2
  44.8 3.5 %propagate.1 = bf16[256,128]{1,0:T(8,128)(2,1)S(1)} custom-call(bf16[1536,128]{1,0:T(8,128)(2,1)S(1)} %collective-permute-done.other, bf16[256,768]{1,0:T(8,128)(2,1)S(1)} %get-tuple-element.25.early, f32[256,512]{1,0:T(8,128)S(1)} %get-tuple-element.26.own_factors, bf16[512,768]{1,0:T(8,128)(2,1)S(1)} %get-tuple-element.24.right, ...), custom_call_target="tpu_custom_call" | custom-call | tf_op jit(solution)/shard_map/propagate/pallas_call | solution.py:322
  48.3 13.1 %all_to_all.10 = bf16[32,8,128]{2,1,0:T(8,128)(2,1)S(1)} all-to-all(bf16[32,8,128]{2,1,0:T(8,128)(2,1)S(1)} %bitcast.30), channel_id=1, replica_groups={{0,8,16,24,32,40,48,56,64,72,80,88,96,104,112,120,128,136,144,152,160,1..., dimensions={0} | all-to-all | bytes 131072 | tf_op jit(solution)/shard_map/all_to_all | solution.py:443
  61.5 0.9 %finish.1 = f32[2,16,512]{2,1,0:T(8,128)} custom-call(bf16[256,128]{1,0:T(8,128)(2,1)S(1)} %bitcast.31, bf16[1024,512]{1,0:T(8,128)(2,1)S(1)} %get-tuple-element.29.final, f32[2,512]{1,0:T(2,128)S(1)} %pad_maximum_fusion.prop), custom_call_target="tpu_custom_call" | custom-call | tf_op jit(solution)/shard_map/finish/pallas_call | solution.py:344
  (6 shorter events, 0.1 us)
Async XLA Ops:
  0.0 22.2 %copy-start = (s32[64,2]{0,1:T(2,128)S(1)}, s32[64,2]{0,1:T(2,128)}, u32[]{:S(2)}) copy-start(s32[64,2]{0,1:T(2,128)} %param.9) | copy-start | bytes 1540
  0.0 24.3 %copy-start.3 = (f32[384,8]{1,0:T(8,128)S(1)}, f32[384,8]{1,0:T(8,128)}, u32[]{:S(2)}) copy-start(f32[384,8]{1,0:T(8,128)} %constant.126.chirp_t) | copy-start | bytes 36868
  0.0 24.3 %copy-start.4 = (f32[8,384]{1,0:T(8,128)S(1)}, f32[8,384]{1,0:T(8,128)}, u32[]{:S(2)}) copy-start(f32[8,384]{1,0:T(8,128)} %constant.125.clone.chirp) | copy-start | bytes 36868
  0.0 0.7 %copy-start.5 = (bf16[2,2048]{1,0:T(2,128)(2,1)S(1)}, bf16[2,2048]{1,0:T(2,128)(2,1)}, u32[]{:S(2)}) copy-start(bf16[2,2048]{1,0:T(2,128)(2,1)} %cells.1) | copy-start | bytes 24580
  0.8 22.1 %copy-start.6 = (s32[512,2]{0,1:T(2,128)S(1)}, s32[512,2]{0,1:T(2,128)}, u32[]{:S(2)}) copy-start(s32[512,2]{0,1:T(2,128)} %param.8) | copy-start | bytes 12292
  1.6 36.2 %all-to-all-start = ((bf16[128,6,2,128]{3,2,1,0:T(2,128)(2,1)}), bf16[128,6,2,128]{3,2,1,0:T(2,128)(2,1)S(1)}, u32[]{:S(2)}, u32[]{:S(2)}) async-start(bf16[128,6,2,128]{3,2,1,0:T(2,128)(2,1)} %bitcast), calls=%async_computation | async-start | bytes 786432 | tf_op jit(solution)/shard_map/all_to_all | solution.py:422
  37.8 7.0 %copy-start.1 = (bf16[512,768]{1,0:T(8,128)(2,1)S(1)}, bf16[512,768]{1,0:T(8,128)(2,1)}, u32[]{:S(2)}) copy-start(bf16[512,768]{1,0:T(8,128)(2,1)} %constant.124.clone.back_far.back) | copy-start | bytes 2359300
  37.8 7.0 %copy-start.2 = (f32[384,768]{1,0:T(8,128)S(1)}, f32[384,768]{1,0:T(8,128)}, u32[]{:S(2)}) copy-start(f32[384,768]{1,0:T(8,128)} %get-tuple-element.27.prop) | copy-start | bytes 3538948
  37.8 6.9 %collective-permute-start = (bf16[1536,128]{1,0:T(8,128)(2,1)S(1)}, bf16[1536,128]{1,0:T(8,128)(2,1)S(1)}, u32[]{:S(2)}, u32[]{:S(2)}) collective-permute-start(bf16[1536,128]{1,0:T(8,128)(2,1)S(1)} %bitcast.28), channel_id=1, source_target_pairs={{0,1},{1,0},{2,3},{3,2},{4,5},{5,4},{6,7},{7,6},{8,9},{9,8},{10,11... | collective-permute-start | bytes 1179656 | tf_op jit(solution)/shard_map/ppermute | solution.py:432
